TPU v7x, 128 devices: a whole 4x4x4 slice. The times are simulated.
128 devices in a mesh: tgt: 8 (over y_hi, z), ptr: 16 (over x, y_lo, core).
Axes of the slice: x: 4, y: 4 (y_hi: 2, y_lo: 2; y = y_hi * 2 + y_lo), z: 4, core: 2. Of those that a mesh axis runs over, the one named last changes fastest.
Arguments:
- targets: float32 [64, 32, 1024], P('tgt'), may hold values from -12 to 12
- partners: float32 [32, 32, 2048], P(None, None, 'ptr'), may hold values from -6 to 6
- occupied: int32 [16], P('ptr'), may hold values 0 or 1
- retained: int32 [1], replicated, may hold values from 32 to 64
Outputs:
- compressed: float32 [64, 32, 1024], P('tgt', 'ptr')
All inputs are finite; a program needn't handle non-finite values. No bound on the sum of `occupied` on one device may be relied on, other than what follows from the above.
Results may differ from a plain program's by a relative error of at most 0.00008.
Values sent between devices are 32-bit elements; how exact they have to be, the bound alone decides.
No kernel may reach another device: no remote copies, remote signals or barrier semaphores. Data moves between devices by JAX's collectives and lax.ppermute only.
A program may use at most 64 MiB of HBM per device.

v0:
```python
import math

import jax
import jax.numpy as jnp
from jax import lax
from jax.sharding import Mesh
from jax.sharding import PartitionSpec as P

TGT = ("tgt_0", "tgt_1")


HIGHEST_PRECISION = lax.Precision.HIGHEST


def cut_along(shard, dim, peers):
    before, after = (shard.shape[:dim], shard.shape[dim + 1 :])
    return jnp.moveaxis(shard.reshape(*before, peers, -1, *after), dim, 0)


def sent_and_summed(shard, axis, dim):
    peers = lax.axis_size(axis)
    blocks = lax.all_to_all(cut_along(shard, dim, peers), axis, 0, 0, tiled=True)
    return jnp.sum(blocks, axis=0)


def laid_out(blocks, dim):
    blocks = jnp.moveaxis(blocks, 0, dim)
    shape = blocks.shape
    return blocks.reshape(*shape[:dim], shape[dim] * shape[dim + 1], *shape[dim + 2 :])


def gather_in_order(shard, axes, sequence):
    blocks = shard[None]
    for k in sequence:
        blocks = lax.all_gather(blocks, axes[k], axis=0, tiled=True)
    carried = [lax.axis_size(axes[k]) for k in reversed(sequence)]
    blocks = blocks.reshape(*carried, *shard.shape)
    turned = sorted(range(len(sequence)), key=lambda place: sequence[len(sequence) - 1 - place])
    return blocks.transpose(*turned, *range(len(sequence), blocks.ndim)).reshape(-1, *shard.shape)


def whole_of(shard, axes, sequence, dim):
    return laid_out(gather_in_order(shard, axes, sequence), dim)


def copy_for_each(shard, axis):
    copies = jnp.broadcast_to(shard, (lax.axis_size(axis), *shard.shape))
    return lax.all_to_all(copies, axis, split_axis=0, concat_axis=0, tiled=True)


def of_everyone(shard, axis):
    return copy_for_each(shard, axis).sum(axis=0)


def gather_directly(shard, axis, dim):
    return laid_out(copy_for_each(shard, axis), dim)


def cas_matrix(length):
    indices = jnp.arange(length, dtype=jnp.int32)
    phases = (indices[:, None] * indices[None, :] % length).astype(jnp.float32) * (
        2.0 * math.pi / length
    )
    return jnp.cos(phases) + jnp.sin(phases)


def coulomb_table(length):
    indices = jnp.arange(length, dtype=jnp.int32)
    signed = jnp.where(indices < length // 2, indices, indices - length).astype(jnp.float32)
    wave = signed * (2.0 * math.pi / length)
    wave = wave * wave
    total = wave[:, None, None] + wave[None, :, None] + wave[None, None, :]
    safe = jnp.where(total > 0.0, total, jnp.float32(1.0))
    return jnp.where(total > 0.0, 4.0 * math.pi / safe, jnp.float32(0.0))


def transform(field, matrix, packed):
    length = matrix.shape[0]
    after_first = jnp.dot(matrix, field.reshape(length, -1), precision=HIGHEST_PRECISION)
    after_second = jnp.einsum(
        "ky,xyn->xkn", matrix, after_first.reshape(length, length, -1), precision=HIGHEST_PRECISION
    )
    after_third = jnp.dot(
        after_second.reshape(-1, packed.shape[0]), packed, precision=HIGHEST_PRECISION
    )
    return after_third.reshape(field.shape)


def shards(targets, partners, occupied, retained):
    length = targets.shape[1]
    owned_count = targets.shape[0]
    partner_count = partners.shape[2] // length
    plane_cells = length * length
    all_cells = plane_cells * length
    matrix = cas_matrix(length)
    packing = max(1, 128 // length)
    packed = jnp.kron(jnp.eye(packing, dtype=jnp.float32), matrix)
    kernel_wide = jnp.broadcast_to(
        (coulomb_table(length) / all_cells)[:, :, None, :], (length, length, partner_count, length)
    ).reshape(length, length, partner_count * length)
    occupancy = 0.25 + 0.75 * jnp.repeat(occupied.astype(jnp.float32), 4)
    weighted = (
        partners.reshape(length, length, partner_count, length) * occupancy[None, None, :, None]
    ).reshape(length, length, partner_count * length)

    def action(target_one):
        spread = jnp.broadcast_to(
            target_one.reshape(length, length, 1, length), (length, length, partner_count, length)
        ).reshape(length, length, partner_count * length)
        density = spread * partners
        potential = transform(kernel_wide * transform(density, matrix, packed), matrix, packed)
        summed = (weighted * potential).reshape(length, length, partner_count, length).sum(axis=2)
        return summed.reshape(length, plane_cells)

    slab_count = length // lax.axis_size("ptr")
    slab_start = lax.axis_index("ptr") * slab_count
    every_action = lax.map(action, targets)
    action_slab = sent_and_summed(every_action, "ptr", 1)
    own_slab = lax.dynamic_slice_in_dim(targets, slab_start, slab_count, 1)
    target_slab = whole_of(own_slab, TGT, (0, 1), 0)
    total_targets = target_slab.shape[0]
    columns = (
        jnp.einsum("asm,bsm->ab", target_slab, action_slab, precision=HIGHEST_PRECISION) / all_cells
    )
    first_owned = lax.axis_index(TGT) * owned_count
    summed_columns = of_everyone(columns, "ptr")
    intersection = gather_directly(summed_columns, TGT, 1)
    lower = jnp.linalg.cholesky(intersection)
    inverse = jax.scipy.linalg.solve_triangular(
        lower, jnp.eye(total_targets, dtype=jnp.float32), lower=True
    )
    all_actions = gather_directly(action_slab, TGT, 0)
    own_rows = lax.dynamic_slice_in_dim(inverse, first_owned, owned_count, 0)
    result = jnp.einsum("bc,csm->bsm", own_rows, all_actions, precision=HIGHEST_PRECISION)
    global_rows = first_owned + jnp.arange(owned_count, dtype=jnp.int32)
    keeping = (global_rows < retained[0]).astype(jnp.float32)
    return result * keeping[:, None, None]


def solution(mesh):
    finer = Mesh(mesh.devices.reshape(2, 4, mesh.shape["ptr"]), ("tgt_0", "tgt_1", "ptr"))
    in_specs = (P(TGT, None, None), P(None, None, "ptr"), P("ptr"), P())
    out_specs = P(TGT, "ptr", None)
    return jax.shard_map(
        shards, mesh=finer, in_specs=in_specs, out_specs=out_specs, check_vma=False
    )
```

profile of v0, /device:TPU:1, one launch (start us, length us, event | category | flops | bytes accessed | tf_op | source)
XLA Modules:
  0.0 232.2 jit_solution(1970234617254161562)
XLA Ops:
  3.8 142.1 %while.12 = (s32[]{:T(128)}, f32[8,32,1024]{2,0,1:T(8,128)}, f32[8,32,1024]{2,1,0:T(8,128)}, f32[32,32,128]{2,1,0:T(8,128)}, f32[32,32,128]{2,1,0:T(8,128)}, /*i...) while((s32[]{:T(128)}, f32[8,32,1024]{2,0,1:T(8,128)}, ...), condition=%wide.region_2.3_spmd.clone.clone, body=%wide.region_0.2_spmd.clone.clone.sunk | while | flops 604549120 | bytes 18551004 | solution.py:117
  7.5 1.9 reshape.221
  9.5 2.0 convolution_bitcast_fusion.9
  17.9 3.6 %dynamic_update_slice.7 = f32[8,32,1024]{2,0,1:T(8,128)} dynamic-update-slice(f32[8,32,1024]{2,0,1:T(8,128)} %get-tuple-element.185, f32[1,32,1024]{2,0,1:T(1,128)S(1)} %broadcast_in_dim.79, s32[]{:T(128)S(6)} %copy.75, s32[]{:T(128)} %constant.97.clone.1..sunk, s32[]{:T(128)} %constant.97.clone.1..sunk) | dynamic-update-slice | bytes 262148 | tf_op jit(solution)/shard_map/while/body/jit(dynamic_update_index_in_dim)/dynamic_update_slice | solution.py:117
  25.3 1.9 reshape.221
  27.2 2.0 convolution_bitcast_fusion.9
  35.7 3.6 %dynamic_update_slice.7 = f32[8,32,1024]{2,0,1:T(8,128)} dynamic-update-slice(f32[8,32,1024]{2,0,1:T(8,128)} %get-tuple-element.185, f32[1,32,1024]{2,0,1:T(1,128)S(1)} %broadcast_in_dim.79, s32[]{:T(128)S(6)} %copy.75, s32[]{:T(128)} %constant.97.clone.1..sunk, s32[]{:T(128)} %constant.97.clone.1..sunk) | dynamic-update-slice | bytes 262148 | tf_op jit(solution)/shard_map/while/body/jit(dynamic_update_index_in_dim)/dynamic_update_slice | solution.py:117
  43.1 1.9 reshape.221
  45.0 2.0 convolution_bitcast_fusion.9
  53.4 3.6 %dynamic_update_slice.7 = f32[8,32,1024]{2,0,1:T(8,128)} dynamic-update-slice(f32[8,32,1024]{2,0,1:T(8,128)} %get-tuple-element.185, f32[1,32,1024]{2,0,1:T(1,128)S(1)} %broadcast_in_dim.79, s32[]{:T(128)S(6)} %copy.75, s32[]{:T(128)} %constant.97.clone.1..sunk, s32[]{:T(128)} %constant.97.clone.1..sunk) | dynamic-update-slice | bytes 262148 | tf_op jit(solution)/shard_map/while/body/jit(dynamic_update_index_in_dim)/dynamic_update_slice | solution.py:117
  60.8 1.9 reshape.221
  62.8 2.0 convolution_bitcast_fusion.9
  71.2 3.6 %dynamic_update_slice.7 = f32[8,32,1024]{2,0,1:T(8,128)} dynamic-update-slice(f32[8,32,1024]{2,0,1:T(8,128)} %get-tuple-element.185, f32[1,32,1024]{2,0,1:T(1,128)S(1)} %broadcast_in_dim.79, s32[]{:T(128)S(6)} %copy.75, s32[]{:T(128)} %constant.97.clone.1..sunk, s32[]{:T(128)} %constant.97.clone.1..sunk) | dynamic-update-slice | bytes 262148 | tf_op jit(solution)/shard_map/while/body/jit(dynamic_update_index_in_dim)/dynamic_update_slice | solution.py:117
  80.5 2.0 convolution_bitcast_fusion.9
  89.0 3.6 %dynamic_update_slice.7 = f32[8,32,1024]{2,0,1:T(8,128)} dynamic-update-slice(f32[8,32,1024]{2,0,1:T(8,128)} %get-tuple-element.185, f32[1,32,1024]{2,0,1:T(1,128)S(1)} %broadcast_in_dim.79, s32[]{:T(128)S(6)} %copy.75, s32[]{:T(128)} %constant.97.clone.1..sunk, s32[]{:T(128)} %constant.97.clone.1..sunk) | dynamic-update-slice | bytes 262148 | tf_op jit(solution)/shard_map/while/body/jit(dynamic_update_index_in_dim)/dynamic_update_slice | solution.py:117
  98.3 2.0 convolution_bitcast_fusion.9
  106.7 3.6 %dynamic_update_slice.7 = f32[8,32,1024]{2,0,1:T(8,128)} dynamic-update-slice(f32[8,32,1024]{2,0,1:T(8,128)} %get-tuple-element.185, f32[1,32,1024]{2,0,1:T(1,128)S(1)} %broadcast_in_dim.79, s32[]{:T(128)S(6)} %copy.75, s32[]{:T(128)} %constant.97.clone.1..sunk, s32[]{:T(128)} %constant.97.clone.1..sunk) | dynamic-update-slice | bytes 262148 | tf_op jit(solution)/shard_map/while/body/jit(dynamic_update_index_in_dim)/dynamic_update_slice | solution.py:117
  116.0 2.0 convolution_bitcast_fusion.9
  124.5 3.6 %dynamic_update_slice.7 = f32[8,32,1024]{2,0,1:T(8,128)} dynamic-update-slice(f32[8,32,1024]{2,0,1:T(8,128)} %get-tuple-element.185, f32[1,32,1024]{2,0,1:T(1,128)S(1)} %broadcast_in_dim.79, s32[]{:T(128)S(6)} %copy.75, s32[]{:T(128)} %constant.97.clone.1..sunk, s32[]{:T(128)} %constant.97.clone.1..sunk) | dynamic-update-slice | bytes 262148 | tf_op jit(solution)/shard_map/while/body/jit(dynamic_update_index_in_dim)/dynamic_update_slice | solution.py:117
  133.8 2.0 convolution_bitcast_fusion.9
  142.2 3.6 %dynamic_update_slice.7 = f32[8,32,1024]{2,0,1:T(8,128)} dynamic-update-slice(f32[8,32,1024]{2,0,1:T(8,128)} %get-tuple-element.185, f32[1,32,1024]{2,0,1:T(1,128)S(1)} %broadcast_in_dim.79, s32[]{:T(128)S(6)} %copy.75, s32[]{:T(128)} %constant.97.clone.1..sunk, s32[]{:T(128)} %constant.97.clone.1..sunk) | dynamic-update-slice | bytes 262148 | tf_op jit(solution)/shard_map/while/body/jit(dynamic_update_index_in_dim)/dynamic_update_slice | solution.py:117
  145.8 3.1 %copy.31 = f32[16,8,2,1024]{3,2,1,0:T(2,128)} copy(f32[16,8,2,1024]{3,1,2,0:T(8,128)} %bitcast.118) | data formatting | bytes 2097152 | tf_op jit(solution)/shard_map/transpose | solution.py:17
  148.9 6.8 %all-to-all-start = ((f32[16,8,2,1024]{3,2,1,0:T(2,128)}), f32[16,8,2,1024]{3,2,1,0:T(2,128)S(1)}, u32[]{:S(2)}, u32[]{:S(2)}) async-start(f32[16,8,2,1024]{3,2,1,0:T(2,128)} %copy.31), calls=%async_computation | async-start | bytes 2097152 | tf_op jit(solution)/shard_map/all_to_all | solution.py:22
  156.8 8.7 %all-gather = f32[16,2,1024]{2,0,1:T(8,128)S(1)} all-gather(f32[8,2,1024]{2,0,1:T(8,128)S(1)} %copy.42), channel_id=2, replica_groups=mesh['tgt_0'=2,'tgt_1'=4,'ptr'=16] {'tgt_0'}, dimensions={0}, use_global_device_ids=true | all-gather | bytes 196608 | tf_op jit(solution)/shard_map/all_gather | solution.py:35
  165.5 11.7 %all_gather.7 = f32[8,8,2,1024]{3,1,0,2:T(8,128)S(1)} all-gather(f32[2,8,2,1024]{3,1,0,2:T(8,128)S(1)} %bitcast.119), channel_id=1, replica_groups=mesh['tgt_0'=2,'tgt_1'=4,'ptr'=16] {'tgt_1'}, dimensions={0}, use_global_device_ids=true | all-gather | bytes 655360 | tf_op jit(solution)/shard_map/all_gather | solution.py:35
  178.8 14.4 %all-to-all-start.1 = ((f32[16,1,512]{2,1,0:T(1,128)}), f32[16,1,512]{2,1,0:T(1,128)S(1)}, u32[]{:S(2)}, u32[]{:S(2)}) async-start(f32[16,1,512]{2,1,0:T(1,128)} %reshape.212), calls=%async_computation.1 | async-start | bytes 65536 | tf_op jit(solution)/shard_map/all_to_all | solution.py:48
  193.9 5.2 %all-to-all-done.1 = f32[16,1,512]{2,1,0:T(1,128)S(1)} async-done(((f32[16,1,512]{2,1,0:T(1,128)}), f32[16,1,512]{2,1,0:T(1,128)S(1)}, u32[]{:S(2)}, u32[]{:S(2)}) %all-to-all-start.1) | async-done | bytes 32800 | tf_op jit(solution)/shard_map/all_to_all | solution.py:48
  201.2 5.7 %all-to-all-start.2 = ((f32[8,1,512]{2,1,0:T(1,128)}), f32[8,1,512]{2,1,0:T(1,128)S(1)}, u32[]{:S(2)}, u32[]{:S(2)}) async-start(f32[8,1,512]{2,1,0:T(1,128)} %reshape.214), calls=%async_computation.2 | async-start | bytes 32768 | tf_op jit(solution)/shard_map/all_to_all | solution.py:48
  207.0 6.5 %all-to-all-done.2 = f32[8,1,512]{2,1,0:T(1,128)S(1)} async-done(((f32[8,1,512]{2,1,0:T(1,128)}), f32[8,1,512]{2,1,0:T(1,128)S(1)}, u32[]{:S(2)}, u32[]{:S(2)}) %all-to-all-start.2) | async-done | bytes 16416 | tf_op jit(solution)/shard_map/all_to_all | solution.py:48
  214.4 3.5 %all-to-all-start.3 = ((f32[8,8,2,1024]{3,1,2,0:T(8,128)}), f32[8,8,2,1024]{3,1,2,0:T(8,128)S(1)}, u32[]{:S(2)}, u32[]{:S(2)}) async-start(f32[8,8,2,1024]{3,1,2,0:T(8,128)} %broadcast_in_dim.57), calls=%async_computation.3 | async-start | bytes 1048576 | tf_op jit(solution)/shard_map/all_to_all | solution.py:48
  218.8 5.8 %cholesky.17 = f32[64,64]{1,0:T(8,128)S(1)} custom-call(f32[64,64]{1,0:T(8,128)S(1)} %fusion.40), custom_call_target="Cholesky" | custom-call | tf_op jit(solution)/shard_map/jit(cholesky)/cholesky | solution.py:128
  226.0 4.9 %custom-call.7 = f32[1,64,64]{1,2,0:T(8,128)S(1)} custom-call(f32[1,64,64]{2,1,0:T(8,128)S(1)} %fusion.39), custom_call_target="InvertDiagBlocksLowerTriangular" | custom-call | tf_op jit(solution)/shard_map/jit(_solve_triangular)/triangular_solve | solution.py:129
  (192 shorter events, 100.8 us)
Async XLA Ops:
  12.5 2.3 copy-start
  30.3 2.3 copy-start
  48.0 2.3 copy-start
  65.8 2.3 copy-start
  83.6 2.3 copy-start
  101.3 2.3 copy-start
  119.1 2.3 copy-start
  136.8 2.3 copy-start
  148.9 28.3 %all-to-all-start = ((f32[16,8,2,1024]{3,2,1,0:T(2,128)}), f32[16,8,2,1024]{3,2,1,0:T(2,128)S(1)}, u32[]{:S(2)}, u32[]{:S(2)}) async-start(f32[16,8,2,1024]{3,2,1,0:T(2,128)} %copy.31), calls=%async_computation | async-start | bytes 2097152 | tf_op jit(solution)/shard_map/all_to_all | solution.py:22
  178.8 20.2 %all-to-all-start.1 = ((f32[16,1,512]{2,1,0:T(1,128)}), f32[16,1,512]{2,1,0:T(1,128)S(1)}, u32[]{:S(2)}, u32[]{:S(2)}) async-start(f32[16,1,512]{2,1,0:T(1,128)} %reshape.212), calls=%async_computation.1 | async-start | bytes 65536 | tf_op jit(solution)/shard_map/all_to_all | solution.py:48
  201.2 12.3 %all-to-all-start.2 = ((f32[8,1,512]{2,1,0:T(1,128)}), f32[8,1,512]{2,1,0:T(1,128)S(1)}, u32[]{:S(2)}, u32[]{:S(2)}) async-start(f32[8,1,512]{2,1,0:T(1,128)} %reshape.214), calls=%async_computation.2 | async-start | bytes 32768 | tf_op jit(solution)/shard_map/all_to_all | solution.py:48
  214.4 16.7 %all-to-all-start.3 = ((f32[8,8,2,1024]{3,1,2,0:T(8,128)}), f32[8,8,2,1024]{3,1,2,0:T(8,128)S(1)}, u32[]{:S(2)}, u32[]{:S(2)}) async-start(f32[8,8,2,1024]{3,1,2,0:T(8,128)} %broadcast_in_dim.57), calls=%async_computation.3 | async-start | bytes 1048576 | tf_op jit(solution)/shard_map/all_to_all | solution.py:48
where the time goes:
time: 235 us; the launch traced here: 232 us
  local copies, waits for them, and re-layouts  94.5 us (40%)
  matrix products  44 us (19%)
  starting transfers between devices  30.5 us (13%)
  other arithmetic  28.5 us (12%)
  blocking collectives  20.4 us (9%)
  waiting for transfers between devices  11.7 us (5%)
    dynamic_update_slice x8, local copies, waits for them, and re-layouts, shards(): every_action = lax.map(action, targets)  28.9 us
    all_to_all x3, starting transfers between devices, copy_for_each(): return lax.all_to_all(copies, axis, split_axis=0, concat_axis=0, tiled=True)  23.6 us
    dot_general x16, matrix products, transform(): jnp.dot(matrix, field.reshape(length, -1), precision=HIGHEST_PRECISION)  23.3 us
    all_gather x2, blocking collectives, gather_in_order(): blocks = lax.all_gather(blocks, axes[k], axis=0, tiled=True)  20.4 us
    reshape x8, local copies, waits for them, and re-layouts, action(): spread = jnp.broadcast_to(target_one.reshape(length, length, 1, length),...  15.4 us
    all_to_all x3, waiting for transfers between devices, copy_for_each(): return lax.all_to_all(copies, axis, split_axis=0, concat_axis=0, tiled=True)  11.7 us
    broadcast_in_dim x8, local copies, waits for them, and re-layouts, shards(): jnp.broadcast_to((coulomb_table(length) / all_cells)[:, :, None, :], (len...  11.3 us
    reduce_sum x8, other arithmetic, action(): (weighted * potential).reshape(length, length, partner_count, length)  10.7 us
  transfers between devices with their start and end apart: 4, of which 2 were waited for; matrix products, arithmetic and copies ran while one was open for 6% of the time, Pallas kernels for 0%

commit v1 on v0

--- a/solution.py
+++ b/solution.py
@@ -1,8 +1,12 @@
-import math
+import functools
 
 import jax
 import jax.numpy as jnp
+import ml_dtypes
+import numpy as np
 from jax import lax
+from jax.experimental import pallas as pl
+from jax.experimental.pallas import tpu as pltpu
 from jax.sharding import Mesh
 from jax.sharding import PartitionSpec as P
 
@@ -56,65 +60,208 @@
     return laid_out(copy_for_each(shard, axis), dim)
 
 
-def cas_matrix(length):
-    indices = jnp.arange(length, dtype=jnp.int32)
-    phases = (indices[:, None] * indices[None, :] % length).astype(jnp.float32) * (
-        2.0 * math.pi / length
-    )
-    return jnp.cos(phases) + jnp.sin(phases)
-
-
-def coulomb_table(length):
-    indices = jnp.arange(length, dtype=jnp.int32)
-    signed = jnp.where(indices < length // 2, indices, indices - length).astype(jnp.float32)
-    wave = signed * (2.0 * math.pi / length)
-    wave = wave * wave
-    total = wave[:, None, None] + wave[None, :, None] + wave[None, None, :]
-    safe = jnp.where(total > 0.0, total, jnp.float32(1.0))
-    return jnp.where(total > 0.0, 4.0 * math.pi / safe, jnp.float32(0.0))
-
-
-def transform(field, matrix, packed):
-    length = matrix.shape[0]
-    after_first = jnp.dot(matrix, field.reshape(length, -1), precision=HIGHEST_PRECISION)
-    after_second = jnp.einsum(
-        "ky,xyn->xkn", matrix, after_first.reshape(length, length, -1), precision=HIGHEST_PRECISION
-    )
-    after_third = jnp.dot(
-        after_second.reshape(-1, packed.shape[0]), packed, precision=HIGHEST_PRECISION
-    )
-    return after_third.reshape(field.shape)
+def split_np(a):
+    a = a.astype(np.float64)
+    hi = a.astype(np.float32).astype(ml_dtypes.bfloat16)
+    lo = (a - hi.astype(np.float64)).astype(np.float32).astype(ml_dtypes.bfloat16)
+    return hi, lo
+
+def half_bases(n):
+    h = n // 2
+    y = np.arange(h) + 0.5
+    k = np.arange(h)
+    even = np.cos(2 * np.pi * k[:, None] * y[None] / n) * np.sqrt(2.0 / h)
+    even[0] *= np.sqrt(0.5)
+    k = np.arange(1, h + 1)
+    odd = np.sin(2 * np.pi * k[:, None] * y[None] / n) * np.sqrt(2.0 / h)
+    odd[-1] *= np.sqrt(0.5)
+    return (even, odd), (np.arange(h), np.arange(1, h + 1))
+
+def tables(n, reps):
+    bases, freqs = half_bases(n)
+    lanes = []
+    kern = []
+    ix = np.arange(n)
+    wx = np.where(ix < n // 2, ix, ix - n) * (2 * np.pi / n)
+    for sy in (0, 1):
+        for sz in (0, 1):
+            m = np.einsum("ky,lz->yzkl", bases[sy], bases[sz]).reshape((n // 2) ** 2, (n // 2) ** 2)
+            lanes.append(m)
+            tot = (wx**2)[:, None, None] + ((freqs[sy] * 2 * np.pi / n) ** 2)[None, :, None] + ((freqs[sz] * 2 * np.pi / n) ** 2)[None, None, :]
+            g = np.where(tot > 0, 4 * np.pi / np.where(tot > 0, tot, 1.0), 0.0) / 4
+            kern.append(g.reshape(n, -1))
+    lanes = np.stack(lanes)
+    mh, ml = split_np(lanes)
+    nh, nl = split_np(np.swapaxes(lanes, 1, 2))
+    ph = 2 * np.pi * (ix[:, None] * ix[None] % n) / n
+    cas = (np.cos(ph) + np.sin(ph)) / np.sqrt(n)
+    w = np.kron(np.eye(reps), cas)
+    wh, wl = split_np(w)
+    lw = np.block([[wh, wh], [wl, np.zeros_like(wl)]])
+    return (np.stack([mh, ml]), np.stack([nh, nl]), lw.astype(ml_dtypes.bfloat16), np.stack(kern).astype(np.float32))
+
+def split(v):
+    hi = v.astype(jnp.bfloat16)
+    lo = (v - hi.astype(jnp.float32)).astype(jnp.bfloat16)
+    return hi, lo
+
+def dot(a, b):
+    return jnp.dot(a, b, preferred_element_type=jnp.float32)
+
+def lane_iota(rows):
+    return lax.broadcasted_iota(jnp.int32, (rows, 128), 1)
+
+def take(v, idx):
+    return jnp.take_along_axis(v, idx, axis=1)
+
+def fold_index(lane, sy, sz):
+    yy = (lane // 16) % 4
+    z = lane % 16
+    return (3 - yy if sy else yy) * 32 + (31 - z if sz else z)
+
+def unfold_index(lane, odd_tile, sy):
+    yy = lane // 32
+    z = lane % 32
+    z = jnp.where(z >= 16, 31 - z, z)
+    y8 = (4 if odd_tile else 0) + yy
+    if sy:
+        y8 = 7 - y8
+    return y8 * 16 + z
+
+def fold(tiles, rows):
+    lane = lane_iota(rows)
+    low = lane < 64
+    out = {}
+    for sy in (0, 1):
+        for sz in (0, 1):
+            idx = fold_index(lane, sy, sz)
+            for h in (0, 1):
+                a, b = (2 * h, 2 * h + 1) if sy == 0 else (7 - 2 * h, 6 - 2 * h)
+                out[sy, sz, h] = jnp.where(low, take(tiles[a], idx), take(tiles[b], idx))
+    return out
+
+def unfold(folded, rows):
+    lane = lane_iota(rows)
+    low = lane % 32 < 16
+    out = []
+    for t in range(8):
+        sy = t // 4
+        h = t // 2 if sy == 0 else (7 - t) // 2
+        odd = t % 2
+        if sy == 0:
+            idx = unfold_index(lane, odd, 0)
+        else:
+            yy = lane // 32
+            z = lane % 32
+            z = jnp.where(z >= 16, 31 - z, z)
+            idx = ((7 if t % 2 == 0 else 3) - yy) * 16 + z
+        out.append(jnp.where(low, take(folded[sy, 0, h], idx), take(folded[sy, 1, h], idx)))
+    return out
+
+
+def body(nj, tb, t_ref, p_ref, occ_ref, m_ref, n_ref, w_ref, k_ref, o_ref, pf, pw, tf, gh, gl, ust, ps):
+    n = 32
+    rows = nj * n
+
+    @pl.when(pl.program_id(0) == 0)
+    def _():
+        lane = lane_iota(n)
+        for j in range(nj):
+            tiles = []
+            for t in range(8):
+                acc = None
+                for yy in range(4):
+                    src = p_ref[pl.ds(4 * t + yy, n, stride=n), :]
+                    if yy != j:
+                        src = pltpu.roll(src, ((yy - j) % 4) * n, 1)
+                    acc = src if acc is None else jnp.where(lane // n == yy, src, acc)
+                tiles.append(acc)
+            f = fold(tiles, n)
+            for (sy, sz, h), v in f.items():
+                c = (2 * sy + sz) * 256 + h * 128
+                pf[j * n:(j + 1) * n, c:c + 128] = v
+                pw[j * n:(j + 1) * n, c:c + 128] = v * occ_ref[0, 0]
+
+    for i in range(tb):
+        f = fold([t_ref[i, :, 128 * t:128 * t + 128] for t in range(8)], n)
+        for (sy, sz, h), v in f.items():
+            c = (2 * sy + sz) * 256 + h * 128
+            tf[:, c:c + 128] = v
+        for j in range(nj):
+            r = slice(j * n, (j + 1) * n)
+            q = slice(i * rows + j * n, i * rows + (j + 1) * n)
+            d = [tf[:, 256 * s:256 * s + 256] * pf[r, 256 * s:256 * s + 256] for s in range(4)]
+            a, b, c, e = d[0] + d[1], d[0] - d[1], d[2] + d[3], d[2] - d[3]
+            for s, g in enumerate((a + c, b + e, a - c, b - e)):
+                hi, lo = split(g)
+                gh[s, q, :] = hi
+                gl[s, q, :] = lo
+    for s in range(4):
+        u = dot(gh[s], m_ref[0, s]) + dot(gl[s], m_ref[0, s]) + dot(gh[s], m_ref[1, s])
+        for i in range(tb):
+            hi, lo = split(u[i * rows:(i + 1) * rows])
+            ust[0:rows, :] = hi
+            ust[rows:2 * rows, :] = lo
+            v = dot(w_ref[...], ust[...])
+            v = (v[:rows] + v[rows:]).reshape(nj, n, 256) * k_ref[s][None]
+            hi, lo = split(v.reshape(rows, 256))
+            ust[0:rows, :] = hi
+            ust[rows:2 * rows, :] = lo
+            v = dot(w_ref[...], ust[...])
+            v = v[:rows] + v[rows:]
+            hi, lo = split(v)
+            gh[s, i * rows:(i + 1) * rows, :] = hi
+            gl[s, i * rows:(i + 1) * rows, :] = lo
+        ps[s] = dot(gh[s], n_ref[0, s]) + dot(gl[s], n_ref[0, s]) + dot(gh[s], n_ref[1, s])
+    for i in range(tb):
+        acc = [None] * 4
+        for j in range(nj):
+            r = slice(j * n, (j + 1) * n)
+            q = slice(i * rows + j * n, i * rows + (j + 1) * n)
+            g = [ps[s, q, :] for s in range(4)]
+            a, b, c, e = g[0] + g[1], g[0] - g[1], g[2] + g[3], g[2] - g[3]
+            for s, v in enumerate((a + c, b + e, a - c, b - e)):
+                v = v * pw[r, 256 * s:256 * s + 256]
+                acc[s] = v if acc[s] is None else acc[s] + v
+        folded = {(s // 2, s % 2, h): acc[s][:, 128 * h:128 * h + 128] for s in range(4) for h in (0, 1)}
+        for t, v in enumerate(unfold(folded, n)):
+            o_ref[i, :, 128 * t:128 * t + 128] = v
+
+def exchange(targets, partners, occupied, tb=8):
+    na, n, plane = targets.shape
+    nj = partners.shape[2] // n
+    m, mt, lw, kt = tables(n, nj)
+    occ = (0.25 + 0.75 * occupied.astype(jnp.float32)).reshape(1, 1)
+    rows = nj * n
+    full = lambda a: pl.BlockSpec(a.shape, lambda i: (0,) * a.ndim)
+    p2 = partners.reshape(n * n, nj * n)
+    return pl.pallas_call(
+        functools.partial(body, nj, tb),
+        out_shape=jax.ShapeDtypeStruct(targets.shape, jnp.float32),
+        grid=(na // tb,),
+        in_specs=[pl.BlockSpec((tb, n, plane), lambda i: (i, 0, 0)), full(p2), pl.BlockSpec(memory_space=pltpu.SMEM), full(m), full(mt), full(lw), full(kt)],
+        out_specs=pl.BlockSpec((tb, n, plane), lambda i: (i, 0, 0)),
+        scratch_shapes=[
+            pltpu.VMEM((rows, plane), jnp.float32),
+            pltpu.VMEM((rows, plane), jnp.float32),
+            pltpu.VMEM((n, plane), jnp.float32),
+            pltpu.VMEM((4, tb * rows, plane // 4), jnp.bfloat16),
+            pltpu.VMEM((4, tb * rows, plane // 4), jnp.bfloat16),
+            pltpu.VMEM((2 * rows, plane // 4), jnp.bfloat16),
+            pltpu.VMEM((4, tb * rows, plane // 4), jnp.float32),
+        ],
+        compiler_params=pltpu.CompilerParams(vmem_limit_bytes=48 << 20),
+    )(targets, p2, occ, jnp.asarray(m), jnp.asarray(mt), jnp.asarray(lw), jnp.asarray(kt))
 
 
 def shards(targets, partners, occupied, retained):
     length = targets.shape[1]
     owned_count = targets.shape[0]
-    partner_count = partners.shape[2] // length
-    plane_cells = length * length
-    all_cells = plane_cells * length
-    matrix = cas_matrix(length)
-    packing = max(1, 128 // length)
-    packed = jnp.kron(jnp.eye(packing, dtype=jnp.float32), matrix)
-    kernel_wide = jnp.broadcast_to(
-        (coulomb_table(length) / all_cells)[:, :, None, :], (length, length, partner_count, length)
-    ).reshape(length, length, partner_count * length)
-    occupancy = 0.25 + 0.75 * jnp.repeat(occupied.astype(jnp.float32), 4)
-    weighted = (
-        partners.reshape(length, length, partner_count, length) * occupancy[None, None, :, None]
-    ).reshape(length, length, partner_count * length)
-
-    def action(target_one):
-        spread = jnp.broadcast_to(
-            target_one.reshape(length, length, 1, length), (length, length, partner_count, length)
-        ).reshape(length, length, partner_count * length)
-        density = spread * partners
-        potential = transform(kernel_wide * transform(density, matrix, packed), matrix, packed)
-        summed = (weighted * potential).reshape(length, length, partner_count, length).sum(axis=2)
-        return summed.reshape(length, plane_cells)
+    all_cells = length**3
 
     slab_count = length // lax.axis_size("ptr")
     slab_start = lax.axis_index("ptr") * slab_count
-    every_action = lax.map(action, targets)
+    every_action = exchange(targets, partners, occupied)
     action_slab = sent_and_summed(every_action, "ptr", 1)
     own_slab = lax.dynamic_slice_in_dim(targets, slab_start, slab_count, 1)
     target_slab = whole_of(own_slab, TGT, (0, 1), 0)

time: 235 us -> 104 us (0.44)
  local copies, waits for them, and re-layouts: 94.5 us -> 13.1 us
  matrix products: 44 us -> 1.11 us
  other arithmetic: 28.5 us -> 13.9 us
  Pallas kernels: 0 us -> 11 us
    dot_general x48 -> x0, matrix products: 42.9 us -> none  [the longest x16 23.3 us: transform(): jnp.dot(matrix, field.reshape(length, -1), precision=HIGHEST_PRECISION)]
    dynamic_update_slice x8 -> x0, local copies, waits for them, and re-layouts: 28.9 us -> none  [shards(): every_action = lax.map(action, targets)]
    reshape x24 -> x2, local copies, waits for them, and re-layouts: 29.8 us -> 1.73 us  [cut_along(): return jnp.moveaxis(shard.reshape(*before, peers, -1, *after), dim, 0)]
    broadcast_in_dim x32 -> x0, local copies, waits for them, and re-layouts: 17.6 us -> none  [the longest x8 11.3 us: shards(): jnp.broadcast_to((coulomb_table(length) / all_cells)[:, :, None, :], (len...]
    pallas_call x0 -> x1, Pallas kernels: none -> 11 us  [exchange(): pl.pallas_call(functools.partial(body, nj, tb), out_shape=jax.ShapeDtypeS...]
    reduce_sum x8 -> x0, other arithmetic: 10.7 us -> none  [action(): (weighted * potential).reshape(length, length, partner_count, length)]
    dynamic_slice x8 -> x0, local copies, waits for them, and re-layouts: 7.36 us -> none  [shards(): every_action = lax.map(action, targets)]
    unnamed x7 -> x19, local copies, waits for them, and re-layouts: 1.61 us -> 8.12 us
  transfers between devices with their start and end apart: 4 -> 4, of which waited for: 2 -> 2; matrix products, arithmetic and copies ran while one was open for 6% -> 14% of each run, Pallas kernels for 0% -> 0%
where the time goes in v1:
time: 104 us; the launch traced here: 103 us
  starting transfers between devices  30.5 us (29%)
  blocking collectives  20.4 us (20%)
  other arithmetic  13.9 us (13%)
  local copies, waits for them, and re-layouts  13.1 us (13%)
  waiting for transfers between devices  11.7 us (11%)
  Pallas kernels  11 us (11%)
  between operations  1.47 us (1%)
  matrix products  1.11 us (1%)
    all_to_all x3, starting transfers between devices, copy_for_each(): return lax.all_to_all(copies, axis, split_axis=0, concat_axis=0, tiled=True)  23.6 us
    all_gather x2, blocking collectives, gather_in_order(): blocks = lax.all_gather(blocks, axes[k], axis=0, tiled=True)  20.4 us
    all_to_all x3, waiting for transfers between devices, copy_for_each(): return lax.all_to_all(copies, axis, split_axis=0, concat_axis=0, tiled=True)  11.7 us
    pallas_call x1, Pallas kernels, exchange(): pl.pallas_call(functools.partial(body, nj, tb), out_shape=jax.ShapeDtypeS...  11 us
    unnamed x19, local copies, waits for them, and re-layouts  8.12 us
    all_to_all x1, starting transfers between devices, sent_and_summed(): lax.all_to_all(cut_along(shard, dim, peers), axis, 0, 0, tiled=True)  6.83 us
    another operation x3, other arithmetic, shards(): lower = jnp.linalg.cholesky(intersection)  6.52 us
    another operation x2, other arithmetic, shards(): jax.scipy.linalg.solve_triangular(lower, jnp.eye(total_targets, dtype=jnp...  5.55 us
  transfers between devices with their start and end apart: 4, of which 2 were waited for; matrix products, arithmetic and copies ran while one was open for 14% of the time, Pallas kernels for 0%

profile of v1, /device:TPU:1, one launch (start us, length us, event | category | flops | bytes accessed | tf_op | source)
XLA Modules:
  0.0 103.2 jit_solution(12923101928529779787)
XLA Ops:
  0.7 1.2 %copy-done = f32[8,32,1024]{2,1,0:T(8,128)S(1)} copy-done((f32[8,32,1024]{2,1,0:T(8,128)S(1)}, f32[8,32,1024]{2,1,0:T(8,128)}, u32[]{:S(2)}) %copy-start) | copy-done | bytes 1048600
  1.9 1.2 %copy-done.1 = bf16[2,4,256,256]{3,2,1,0:T(8,128)(2,1)S(1)} copy-done((bf16[2,4,256,256]{3,2,1,0:T(8,128)(2,1)S(1)}, bf16[2,4,256,256]{3,2,1,0:T(8,128)(2,1)}, u32[]{:S(2)}) %copy-start.1) | copy-done | bytes 1048600
  3.1 1.2 %copy-done.2 = bf16[2,4,256,256]{3,2,1,0:T(8,128)(2,1)S(1)} copy-done((bf16[2,4,256,256]{3,2,1,0:T(8,128)(2,1)S(1)}, bf16[2,4,256,256]{3,2,1,0:T(8,128)(2,1)}, u32[]{:S(2)}) %copy-start.2) | copy-done | bytes 1048600
  4.3 1.0 %copy-done.3 = f32[32,32,128]{2,1,0:T(8,128)S(1)} copy-done((f32[32,32,128]{2,1,0:T(8,128)S(1)}, f32[32,32,128]{2,1,0:T(8,128)}, u32[]{:S(2)}) %copy-start.3) | copy-done | bytes 524312
  5.4 0.9 copy-done.4
  6.3 0.9 copy-done.5
  7.2 11.0 %shard_map.82 = f32[8,32,1024]{2,1,0:T(8,128)S(1)} custom-call(f32[8,32,1024]{2,1,0:T(8,128)S(1)} %copy-done, f32[1024,128]{1,0:T(8,128)S(1)} %bitcast.46, f32[1,1]{1,0:T(1,128)} %bitcast.6.occ_ref, bf16[2,4,256,256]{3,2,1,0:T(8,128)(2,1)S(1)} %copy-done.1, bf16[2,4,256,256]{3,2,1,0:T(8,128)(2,1)S(1)} %copy-done.2, bf16[256,256]{1,0:T(8,128)(2,1)S(1)} %copy-done.4, ...), custom_call_target="tpu_custom_call" | custom-call | tf_op jit(solution)/shard_map/pallas_call | solution.py:238
  18.2 0.6 reshape.37
  18.8 1.1 %copy.42 = f32[8,16,2,1024]{3,2,0,1:T(2,128)} copy(f32[8,16,2,1024]{3,2,1,0:T(2,128)S(1)} %reshape.37) | data formatting | bytes 2097152 | tf_op jit(solution)/shard_map/reshape | solution.py:21
  19.9 6.8 %all-to-all-start = ((f32[16,8,2,1024]{3,2,1,0:T(2,128)}), f32[16,8,2,1024]{3,2,1,0:T(2,128)S(1)}, u32[]{:S(2)}, u32[]{:S(2)}) async-start(f32[16,8,2,1024]{3,2,1,0:T(2,128)} %bitcast.44), calls=%async_computation | async-start | bytes 2097152 | tf_op jit(solution)/shard_map/all_to_all | solution.py:26
  26.7 1.0 constant_dynamic-slice_fusion
  27.8 8.7 %all-gather = f32[16,2,1024]{2,0,1:T(8,128)S(1)} all-gather(f32[8,2,1024]{2,0,1:T(8,128)S(1)} %copy.34), channel_id=2, replica_groups=mesh['tgt_0'=2,'tgt_1'=4,'ptr'=16] {'tgt_0'}, dimensions={0}, use_global_device_ids=true | all-gather | bytes 196608 | tf_op jit(solution)/shard_map/all_gather | solution.py:39
  36.5 11.7 %all_gather.7 = f32[8,8,2,1024]{3,1,0,2:T(8,128)S(1)} all-gather(f32[2,8,2,1024]{3,1,0,2:T(8,128)S(1)} %bitcast.49), channel_id=1, replica_groups=mesh['tgt_0'=2,'tgt_1'=4,'ptr'=16] {'tgt_1'}, dimensions={0}, use_global_device_ids=true | all-gather | bytes 655360 | tf_op jit(solution)/shard_map/all_gather | solution.py:39
  48.2 0.3 reduce_sum.18
  48.6 0.5 fusion
  49.1 0.7 reshape.43
  49.8 14.4 %all-to-all-start.1 = ((f32[16,1,512]{2,1,0:T(1,128)}), f32[16,1,512]{2,1,0:T(1,128)S(1)}, u32[]{:S(2)}, u32[]{:S(2)}) async-start(f32[16,1,512]{2,1,0:T(1,128)} %reshape.43), calls=%async_computation.1 | async-start | bytes 65536 | tf_op jit(solution)/shard_map/all_to_all | solution.py:52
  64.9 5.2 %all-to-all-done.1 = f32[16,1,512]{2,1,0:T(1,128)S(1)} async-done(((f32[16,1,512]{2,1,0:T(1,128)}), f32[16,1,512]{2,1,0:T(1,128)S(1)}, u32[]{:S(2)}, u32[]{:S(2)}) %all-to-all-start.1) | async-done | bytes 32800 | tf_op jit(solution)/shard_map/all_to_all | solution.py:52
  70.1 0.6 broadcast.62
  70.7 0.8 reduce.6
  71.5 0.7 reshape.45
  72.2 5.7 %all-to-all-start.2 = ((f32[8,1,512]{2,1,0:T(1,128)}), f32[8,1,512]{2,1,0:T(1,128)S(1)}, u32[]{:S(2)}, u32[]{:S(2)}) async-start(f32[8,1,512]{2,1,0:T(1,128)} %reshape.45), calls=%async_computation.2 | async-start | bytes 32768 | tf_op jit(solution)/shard_map/all_to_all | solution.py:52
  78.0 6.5 %all-to-all-done.2 = f32[8,1,512]{2,1,0:T(1,128)S(1)} async-done(((f32[8,1,512]{2,1,0:T(1,128)}), f32[8,1,512]{2,1,0:T(1,128)S(1)}, u32[]{:S(2)}, u32[]{:S(2)}) %all-to-all-start.2) | async-done | bytes 16416 | tf_op jit(solution)/shard_map/all_to_all | solution.py:52
  84.5 0.8 broadcast_in_dim.18
  85.4 3.5 %all-to-all-start.3 = ((f32[8,8,2,1024]{3,1,2,0:T(8,128)}), f32[8,8,2,1024]{3,1,2,0:T(8,128)S(1)}, u32[]{:S(2)}, u32[]{:S(2)}) async-start(f32[8,8,2,1024]{3,1,2,0:T(8,128)} %broadcast_in_dim.18), calls=%async_computation.3 | async-start | bytes 1048576 | tf_op jit(solution)/shard_map/all_to_all | solution.py:52
  88.9 0.7 reduce.7
  89.8 5.8 %cholesky.17 = f32[64,64]{1,0:T(8,128)S(1)} custom-call(f32[64,64]{1,0:T(8,128)S(1)} %fusion.4), custom_call_target="Cholesky" | custom-call | tf_op jit(solution)/shard_map/jit(cholesky)/cholesky | solution.py:275
  95.7 0.6 compare_reduce_fusion
  96.3 0.7 fusion.3
  97.0 4.9 %custom-call.7 = f32[1,64,64]{1,2,0:T(8,128)S(1)} custom-call(f32[1,64,64]{2,1,0:T(8,128)S(1)} %fusion.3), custom_call_target="InvertDiagBlocksLowerTriangular" | custom-call | tf_op jit(solution)/shard_map/jit(_solve_triangular)/triangular_solve | solution.py:276
  102.1 0.4 convolution_multiply_fusion
  102.5 0.7 copy.31
  (22 shorter events, 0.7 us)
Async XLA Ops:
  0.7 1.2 %copy-start = (f32[8,32,1024]{2,1,0:T(8,128)S(1)}, f32[8,32,1024]{2,1,0:T(8,128)}, u32[]{:S(2)}) copy-start(f32[8,32,1024]{2,1,0:T(8,128)} %t_ref.1) | copy-start | bytes 3145732
  1.9 1.2 %copy-start.1 = (bf16[2,4,256,256]{3,2,1,0:T(8,128)(2,1)S(1)}, bf16[2,4,256,256]{3,2,1,0:T(8,128)(2,1)}, u32[]{:S(2)}) copy-start(bf16[2,4,256,256]{3,2,1,0:T(8,128)(2,1)} %constant.86.clone.m_ref) | copy-start | bytes 3145732
  3.1 1.2 %copy-start.2 = (bf16[2,4,256,256]{3,2,1,0:T(8,128)(2,1)S(1)}, bf16[2,4,256,256]{3,2,1,0:T(8,128)(2,1)}, u32[]{:S(2)}) copy-start(bf16[2,4,256,256]{3,2,1,0:T(8,128)(2,1)} %constant.87.clone.n_ref) | copy-start | bytes 3145732
  4.3 1.0 %copy-start.3 = (f32[32,32,128]{2,1,0:T(8,128)S(1)}, f32[32,32,128]{2,1,0:T(8,128)}, u32[]{:S(2)}) copy-start(f32[32,32,128]{2,1,0:T(8,128)} %param.9) | copy-start | bytes 1572868
  5.4 0.9 copy-start.4
  6.3 0.9 copy-start.5
  19.9 28.3 %all-to-all-start = ((f32[16,8,2,1024]{3,2,1,0:T(2,128)}), f32[16,8,2,1024]{3,2,1,0:T(2,128)S(1)}, u32[]{:S(2)}, u32[]{:S(2)}) async-start(f32[16,8,2,1024]{3,2,1,0:T(2,128)} %bitcast.44), calls=%async_computation | async-start | bytes 2097152 | tf_op jit(solution)/shard_map/all_to_all | solution.py:26
  49.8 20.2 %all-to-all-start.1 = ((f32[16,1,512]{2,1,0:T(1,128)}), f32[16,1,512]{2,1,0:T(1,128)S(1)}, u32[]{:S(2)}, u32[]{:S(2)}) async-start(f32[16,1,512]{2,1,0:T(1,128)} %reshape.43), calls=%async_computation.1 | async-start | bytes 65536 | tf_op jit(solution)/shard_map/all_to_all | solution.py:52
  72.2 12.3 %all-to-all-start.2 = ((f32[8,1,512]{2,1,0:T(1,128)}), f32[8,1,512]{2,1,0:T(1,128)S(1)}, u32[]{:S(2)}, u32[]{:S(2)}) async-start(f32[8,1,512]{2,1,0:T(1,128)} %reshape.45), calls=%async_computation.2 | async-start | bytes 32768 | tf_op jit(solution)/shard_map/all_to_all | solution.py:52
  85.4 16.7 %all-to-all-start.3 = ((f32[8,8,2,1024]{3,1,2,0:T(8,128)}), f32[8,8,2,1024]{3,1,2,0:T(8,128)S(1)}, u32[]{:S(2)}, u32[]{:S(2)}) async-start(f32[8,8,2,1024]{3,1,2,0:T(8,128)} %broadcast_in_dim.18), calls=%async_computation.3 | async-start | bytes 1048576 | tf_op jit(solution)/shard_map/all_to_all | solution.py:52

commit v2 on v0

v2 whole, which is shorter than its diff:
```python
import functools

import jax
import jax.numpy as jnp
import ml_dtypes
import numpy as np
from jax import lax
from jax.experimental import pallas as pl
from jax.experimental.pallas import tpu as pltpu
from jax.sharding import Mesh
from jax.sharding import PartitionSpec as P

TGT = ("tgt_0", "tgt_1")
PTR = ("ptr_0", "ptr_1", "core")
SLABS = ("ptr_0", "ptr_1")
LANES = 128


def split_np(a):
    a = a.astype(np.float64)
    hi = a.astype(np.float32).astype(ml_dtypes.bfloat16)
    lo = (a - hi.astype(np.float64)).astype(np.float32).astype(ml_dtypes.bfloat16)
    return hi, lo


def half_bases(n):
    h = n // 2
    y = np.arange(h) + 0.5
    even_k, odd_k = np.arange(h), np.arange(1, h + 1)
    even = np.cos(2 * np.pi * even_k[:, None] * y[None] / n) * np.sqrt(2.0 / h)
    even[0] *= np.sqrt(0.5)
    odd = np.sin(2 * np.pi * odd_k[:, None] * y[None] / n) * np.sqrt(2.0 / h)
    odd[-1] *= np.sqrt(0.5)
    return (even, odd), (even_k, odd_k)


def tables(n, reps):
    bases, freqs = half_bases(n)
    planes, kernels = [], []
    ix = np.arange(n)
    wave = lambda k: (k * (2 * np.pi / n)) ** 2
    wx = wave(np.where(ix < n // 2, ix, ix - n))
    for sy in (0, 1):
        for sz in (0, 1):
            m = np.einsum("ky,lz->yzkl", bases[sy], bases[sz])
            planes.append(m.reshape(n * n // 4, n * n // 4))
            total = wx[:, None, None] + wave(freqs[sy])[:, None] + wave(freqs[sz])[None]
            g = np.where(total > 0, 4 * np.pi / np.where(total > 0, total, 1.0), 0.0)
            kernels.append(g.reshape(n, -1) / 4)
    planes = np.stack(planes)
    phase = 2 * np.pi * (ix[:, None] * ix[None] % n) / n
    wh, wl = split_np(np.kron(np.eye(reps), (np.cos(phase) + np.sin(phase)) / np.sqrt(n)))
    left = np.block([[wh, wh], [wl, np.zeros_like(wl)]]).astype(ml_dtypes.bfloat16)
    forward = np.stack(split_np(planes))
    back = np.stack(split_np(np.swapaxes(planes, 1, 2)))
    return forward, back, left, np.stack(kernels).astype(np.float32)


def split(v):
    hi = v.astype(jnp.bfloat16)
    return hi, (v - hi.astype(jnp.float32)).astype(jnp.bfloat16)


def dot(a, b):
    return jnp.dot(a, b, preferred_element_type=jnp.float32)


def take(v, idx):
    return jnp.take_along_axis(v, idx, axis=1)


def fold(tiles, rows):
    lane = lax.broadcasted_iota(jnp.int32, (rows, LANES), 1)
    y, z = (lane // 16) % 4, lane % 16
    out = {}
    for sy in (0, 1):
        for sz in (0, 1):
            idx = (3 - y if sy else y) * 32 + (31 - z if sz else z)
            for h in (0, 1):
                a, b = (7 - 2 * h, 6 - 2 * h) if sy else (2 * h, 2 * h + 1)
                out[2 * sy + sz, h] = jnp.where(lane < 64, take(tiles[a], idx), take(tiles[b], idx))
    return out


def unfold(folded, rows):
    lane = lax.broadcasted_iota(jnp.int32, (rows, LANES), 1)
    y, z = lane // 32, lane % 32
    low = z < 16
    z = jnp.where(low, z, 31 - z)
    out = []
    for t in range(8):
        sy = t // 4
        h = (7 - t) // 2 if sy else t // 2
        first = 7 - 4 * (t % 2) if sy else 4 * (t % 2)
        idx = (first - y if sy else first + y) * 16 + z
        out.append(jnp.where(low, take(folded[2 * sy, h], idx), take(folded[2 * sy + 1, h], idx)))
    return out


def butterfly(d):
    a, b, c, e = d[0] + d[1], d[0] - d[1], d[2] + d[3], d[2] - d[3]
    return a + c, b + e, a - c, b - e


def solve_body(last, tb, nj, n, *refs):
    if last:
        t_ref, prior, p_ref, occ_ref, m_hbm, b_hbm, w_hbm, k_hbm, o_ref = refs[:9]
    else:
        t_hbm, p_ref, occ_ref, m_hbm, b_hbm, w_hbm, k_hbm, o_ref, tf_out = refs[:9]
    pbuf, pf, pw, mw, bw, ww, kw, tbuf, gh, gl, ust, ps, sems = refs[9:]
    rows, quarter = nj * n, n * n // 4
    copies = [
        pltpu.make_async_copy(src, dst, sems.at[i])
        for i, (src, dst) in enumerate(
            ((p_ref, pbuf), (m_hbm, mw), (w_hbm, ww), (k_hbm, kw), (b_hbm, bw))
        )
    ]
    if last:
        copies.append(pltpu.make_async_copy(t_ref, tbuf, sems.at[5]))
    else:
        mine = pl.ds(lax.axis_index("core") * tb, tb)
        copies.append(pltpu.make_async_copy(t_hbm.at[mine], tbuf, sems.at[5]))
    for i in (0, 5, 1, 2, 3, 4):
        copies[i].start()
    copies[0].wait()
    lane = lax.broadcasted_iota(jnp.int32, (n, LANES), 1)
    for j in range(nj):
        tiles = []
        for t in range(8):
            acc = None
            for y in range(4):
                src = pbuf[pl.ds(4 * t + y, n, stride=n), :]
                if y != j:
                    src = pltpu.roll(src, ((y - j) % 4) * n, 1)
                acc = src if acc is None else jnp.where(lane // n == y, src, acc)
            tiles.append(acc)
        for (s, h), v in fold(tiles, n).items():
            at = slice(s * quarter + h * LANES, s * quarter + (h + 1) * LANES)
            pf[j * n : (j + 1) * n, at] = v
            pw[j * n : (j + 1) * n, at] = v * occ_ref[0, 0]
    copies[5].wait()
    for i in range(tb):
        if not last:
            tiles = [tbuf[i, :, LANES * t : LANES * (t + 1)] for t in range(8)]
            for (s, h), v in fold(tiles, n).items():
                tf_out[i, :, s * quarter + h * LANES : s * quarter + (h + 1) * LANES] = v
        tf = tbuf if last else tf_out
        for j in range(nj):
            r = slice(j * n, (j + 1) * n)
            q = slice(i * rows + j * n, i * rows + (j + 1) * n)
            d = [
                tf[i, :, quarter * s : quarter * (s + 1)] * pf[r, quarter * s : quarter * (s + 1)]
                for s in range(4)
            ]
            for s, g in enumerate(butterfly(d)):
                gh[s, q, :], gl[s, q, :] = split(g)
    for i in (1, 2, 3, 4):
        copies[i].wait()
    for s in range(4):
        u = dot(gh[s], mw[0, s]) + dot(gl[s], mw[0, s]) + dot(gh[s], mw[1, s])
        for i in range(tb):
            at = slice(i * rows, (i + 1) * rows)
            ust[i, :rows, :], ust[i, rows:, :] = split(u[at])
            v = dot(ww[...], ust[i])
            v = (v[:rows] + v[rows:]).reshape(nj, n, quarter) * kw[s][None]
            ust[i, :rows, :], ust[i, rows:, :] = split(v.reshape(rows, quarter))
            v = dot(ww[...], ust[i])
            gh[s, at, :], gl[s, at, :] = split(v[:rows] + v[rows:])
        ps[s] = dot(gh[s], bw[0, s]) + dot(gl[s], bw[0, s]) + dot(gh[s], bw[1, s])
    for i in range(tb):
        acc = [prior[i, :, quarter * s : quarter * (s + 1)] if last else None for s in range(4)]
        for j in range(nj):
            r = slice(j * n, (j + 1) * n)
            q = slice(i * rows + j * n, i * rows + (j + 1) * n)
            for s, v in enumerate(butterfly([ps[s, q, :] for s in range(4)])):
                v = v * pw[r, quarter * s : quarter * (s + 1)]
                acc[s] = v if acc[s] is None else acc[s] + v
        if last:
            folded = {(s, h): acc[s][:, LANES * h : LANES * (h + 1)] for s in range(4) for h in (0, 1)}
            peers = o_ref.shape[0]
            each = n // peers
            for t, v in enumerate(unfold(folded, n)):
                for d in range(peers):
                    o_ref[d, i * each : (i + 1) * each, LANES * t : LANES * (t + 1)] = v[
                        d * each : (d + 1) * each
                    ]
        else:
            for s in range(4):
                o_ref[i, :, quarter * s : quarter * (s + 1)] = acc[s]


def solve(targets, partners, occupied, consts, prior=None, peers=8):
    last = prior is not None
    n = 32
    nj = partners.shape[1] // n
    tb = prior.shape[0] if last else targets.shape[0] // 2
    rows, quarter = nj * n, n * n // 4
    forward, back, left, kernel = consts
    occ = (0.25 + 0.75 * occupied.astype(jnp.float32)).reshape(1, 1)
    hbm = pl.BlockSpec(memory_space=pl.ANY)
    vmem = pl.BlockSpec(memory_space=pltpu.VMEM)
    smem = pl.BlockSpec(memory_space=pltpu.SMEM)
    part = jax.ShapeDtypeStruct((tb, n, n * n), jnp.float32)
    if last:
        operands = (targets, prior)
        out_shape = jax.ShapeDtypeStruct((peers, tb * n // peers, n * n), jnp.float32)
        in_specs, out_specs = [hbm, vmem, hbm, smem, hbm, hbm, hbm, hbm], vmem
    else:
        operands = (targets,)
        out_shape = (part, part)
        in_specs, out_specs = [hbm, hbm, smem, hbm, hbm, hbm, hbm], (vmem, vmem)
    return pl.pallas_call(
        functools.partial(solve_body, last, tb, nj, n),
        out_shape=out_shape,
        in_specs=in_specs,
        out_specs=out_specs,
        scratch_shapes=[
            pltpu.VMEM(partners.shape, jnp.float32),
            pltpu.VMEM((rows, n * n), jnp.float32),
            pltpu.VMEM((rows, n * n), jnp.float32),
            pltpu.VMEM(forward.shape, jnp.bfloat16),
            pltpu.VMEM(back.shape, jnp.bfloat16),
            pltpu.VMEM(left.shape, jnp.bfloat16),
            pltpu.VMEM(kernel.shape, jnp.float32),
            pltpu.VMEM(part.shape, jnp.float32),
            pltpu.VMEM((4, tb * rows, quarter), jnp.bfloat16),
            pltpu.VMEM((4, tb * rows, quarter), jnp.bfloat16),
            pltpu.VMEM((tb, 2 * rows, quarter), jnp.bfloat16),
            pltpu.VMEM((4, tb * rows, quarter), jnp.float32),
            pltpu.SemaphoreType.DMA((6,)),
        ],
        compiler_params=pltpu.CompilerParams(vmem_limit_bytes=48 << 20),
        cost_estimate=pl.CostEstimate(
            flops=2 * 5 * tb * 4 * rows * quarter * quarter, bytes_accessed=8 << 20, transcendentals=0
        ),
    )(*operands, partners, occ, forward, back, left, kernel)


def spread_body(copies, in_ref, o_ref):
    peers, rows, _ = in_ref.shape
    total = in_ref[0]
    for k in range(1, peers):
        total = total + in_ref[k]
    each = 4
    for core in (0, 1):
        picked = jnp.concatenate(
            [
                total[i * each + 2 * core + q : i * each + 2 * core + q + 1]
                for q in (0, 1)
                for i in range(rows // each)
            ],
            axis=0,
        )
        for k in range(copies):
            o_ref[2 * k + core] = picked


def spread(received, copies):
    _, rows, plane = received.shape
    return pl.pallas_call(
        functools.partial(spread_body, copies),
        out_shape=jax.ShapeDtypeStruct((2 * copies, rows // 2, plane), jnp.float32),
        compiler_params=pltpu.CompilerParams(vmem_limit_bytes=16 << 20),
    )(received)


def plane_of(ref, q):
    return jnp.concatenate([ref[8 * g + 4 * q : 8 * g + 4 * q + 4, :] for g in range(ref.shape[0] // 8)], axis=0)


def overlap_body(scale, t_ref, a_ref, o_ref):
    half = t_ref.shape[0] // 2
    total = None
    for q in (0, 1):
        s = lax.dot_general(
            plane_of(t_ref, q),
            plane_of(a_ref, q),
            (((1,), (1,)), ((), ())),
            precision=lax.Precision.HIGHEST,
            preferred_element_type=jnp.float32,
        )
        total = s if total is None else total + s
    total = total * scale
    packed = jnp.concatenate([total[: half // 2], total[half // 2 :]], axis=1)
    for k in range(o_ref.shape[0]):
        o_ref[k] = packed


def overlap(target_slab, action_slab, copies, scale):
    half = target_slab.shape[0] // 2
    return pl.pallas_call(
        functools.partial(overlap_body, scale),
        out_shape=jax.ShapeDtypeStruct((copies, half // 2, 2 * half), jnp.float32),
        compiler_params=pltpu.CompilerParams(vmem_limit_bytes=16 << 20),
    )(target_slab, action_slab)


def compress_body(owned, s_ref, a_ref, keep_ref, o_ref, inv_ref):
    total = s_ref[0]
    for k in range(1, s_ref.shape[0]):
        total = total + s_ref[k]
    half = total.shape[0]
    count = 2 * half
    square = jnp.concatenate([total[:, :count], total[:, count:]], axis=0)
    square = 0.5 * (square + square.T)
    row = lax.broadcasted_iota(jnp.int32, (count, count), 0)
    col = lax.broadcasted_iota(jnp.int32, (count, count), 1)
    wide = jnp.concatenate([square, jnp.where(row == col, 1.0, 0.0)], axis=1)
    tiles = [wide[8 * t : 8 * t + 8] for t in range(count // 8)]
    sub = lax.broadcasted_iota(jnp.int32, (8, LANES), 0)
    down = lambda v, k: jnp.broadcast_to(v[k : k + 1], (8, LANES))
    for p in range(count // 8):
        later = range(p, count // 8)
        cols = {
            (t, k): jnp.broadcast_to(tiles[t][:, 8 * p + k : 8 * p + k + 1], (8, LANES))
            for t in later
            for k in range(8)
        }
        root = jnp.ones((8, LANES), jnp.float32)
        for k in range(8):
            pivot = down(cols[p, k], k)
            over = 1.0 / pivot
            root = jnp.where(sub == k, lax.rsqrt(pivot), root)
            line = down(tiles[p], k)
            cross = [down(cols[p, m], k) for m in range(k + 1, 8)]
            for t in later:
                f = cols[t, k] * over
                if t == p:
                    f = jnp.where(sub > k, f, 0.0)
                tiles[t] = tiles[t] - f * line
                for m in range(k + 1, 8):
                    cols[t, m] = cols[t, m] - f * cross[m - k - 1]
        inv_ref[8 * p : 8 * p + 8, :] = tiles[p] * root
    first = lax.axis_index(TGT) * owned
    mine = inv_ref[pl.ds(pl.multiple_of(first, 8), owned), :][:, count:]
    kept = first + lax.broadcasted_iota(jnp.int32, (owned, count), 0) < keep_ref[0]
    mine = jnp.where(kept, mine, 0.0)
    for q in (0, 1):
        o_ref[:, q, :] = jnp.dot(
            mine,
            plane_of(a_ref, q),
            precision=lax.Precision.HIGHEST,
            preferred_element_type=jnp.float32,
        )


def compress(summands, action_slab, retained, owned):
    count = action_slab.shape[0] // 2
    vmem = pl.BlockSpec(memory_space=pltpu.VMEM)
    return pl.pallas_call(
        functools.partial(compress_body, owned),
        out_shape=jax.ShapeDtypeStruct((owned, 2, action_slab.shape[1]), jnp.float32),
        in_specs=[vmem, vmem, pl.BlockSpec(memory_space=pltpu.SMEM)],
        out_specs=vmem,
        scratch_shapes=[pltpu.VMEM((count, LANES), jnp.float32)],
        compiler_params=pltpu.CompilerParams(vmem_limit_bytes=16 << 20),
    )(summands, action_slab, retained)


def gathered(shard, axes):
    for name in reversed(axes):
        shard = lax.all_gather(shard, name, axis=0, tiled=True)
    return shard


def shards(targets, partners, occupied, retained):
    owned, n, plane = targets.shape
    consts = [jnp.asarray(c) for c in tables(n, partners.shape[2] // n)]
    partners = partners.reshape(n * n, -1)
    swap = [(0, 1), (1, 0)]
    other_partners = lax.ppermute(partners, "core", swap)
    other_occupied = lax.ppermute(occupied.astype(jnp.float32), "core", swap)
    thick = n // lax.axis_size(PTR)
    first_plane = lax.axis_index(PTR) * thick
    own_slab = lax.dynamic_slice_in_dim(targets, first_plane, thick, 1)
    own_slab = own_slab.reshape(2, -1, thick, plane).transpose(0, 2, 1, 3).reshape(-1, plane)
    target_slab = gathered(own_slab, TGT)
    partial_actions, folded = solve(targets, partners, occupied, consts)
    cut = solve(folded, other_partners, other_occupied, consts, partial_actions, lax.axis_size(SLABS))
    received = lax.all_to_all(cut, SLABS, 0, 0, tiled=True)
    copies = spread(received, lax.axis_size(TGT))
    action_slab = lax.all_to_all(copies, TGT + ("core",), 0, 0, tiled=True).reshape(-1, plane)
    summands = overlap(target_slab, action_slab, lax.axis_size(PTR), 1.0 / n**3)
    summands = lax.all_to_all(summands, PTR, 0, 0, tiled=True)
    return compress(summands, action_slab, retained, owned)


def solution(mesh):
    names = TGT + PTR
    finer = Mesh(mesh.devices.reshape(2, 4, 4, 2, 2), names)
    in_specs = (P(TGT, None, None), P(None, None, PTR), P(PTR), P())
    out_specs = P(TGT, PTR, None)
    return jax.shard_map(
        shards, mesh=finer, in_specs=in_specs, out_specs=out_specs, check_vma=False
    )
```

time: 235 us -> 90.2 us (0.38)
  local copies, waits for them, and re-layouts: 94.5 us -> 7.56 us
  matrix products: 44 us -> 0 us
  other arithmetic: 28.5 us -> 0 us
  Pallas kernels: 0 us -> 20 us
  blocking collectives: 20.4 us -> 34.6 us
  starting transfers between devices: 30.5 us -> 18.6 us
  waiting for transfers between devices: 11.7 us -> 6.81 us
    dot_general x50 -> x0, matrix products: 43.8 us -> none  [the longest x16 23.3 us: transform(): jnp.dot(matrix, field.reshape(length, -1), precision=HIGHEST_PRECISION)]
    reshape x26 -> x1, local copies, waits for them, and re-layouts: 29.9 us -> 0.02 us  [shards(): own_slab.reshape(2, -1, thick, plane).transpose(0, 2, 1, 3)]
    dynamic_update_slice x8 -> x0, local copies, waits for them, and re-layouts: 28.9 us -> none  [shards(): every_action = lax.map(action, targets)]
    pallas_call x0 -> x5, Pallas kernels: none -> 20 us  [the longest x2 14.7 us: solve(): pl.pallas_call(functools.partial(solve_body, last, tb, nj, n), out_shape=...]
    broadcast_in_dim x33 -> x0, local copies, waits for them, and re-layouts: 18.5 us -> none  [the longest x8 11.3 us: shards(): jnp.broadcast_to((coulomb_table(length) / all_cells)[:, :, None, :], (len...]
    all_to_all x4 -> x2, starting transfers between devices: 30.5 us -> 16.3 us  [the longest x1 9.81 us: shards(): lax.all_to_all(copies, TGT + ('core',), 0, 0, tiled=True).reshape(-1, plane)]
    all_to_all x0 -> x1, blocking collectives: none -> 13.5 us  [shards(): received = lax.all_to_all(cut, SLABS, 0, 0, tiled=True)]
    another operation x5 -> x0, other arithmetic: 12.1 us -> none  [the longest x3 6.52 us: shards(): lower = jnp.linalg.cholesky(intersection)]
  transfers between devices with their start and end apart: 4 -> 4, of which waited for: 2 -> 1; matrix products, arithmetic and copies ran while one was open for 6% -> 1% of each run, Pallas kernels for 0% -> 8%
where the time goes in v2:
time: 90.2 us; the launch traced here: 89.6 us
  blocking collectives  34.6 us (38%)
  Pallas kernels  20 us (22%)
  starting transfers between devices  18.6 us (21%)
  local copies, waits for them, and re-layouts  7.56 us (8%)
  waiting for transfers between devices  6.81 us (8%)
  between operations  2.01 us (2%)
    all_gather x2, blocking collectives, gathered(): shard = lax.all_gather(shard, name, axis=0, tiled=True)  21.2 us
    pallas_call x2, Pallas kernels, solve(): pl.pallas_call(functools.partial(solve_body, last, tb, nj, n), out_shape=...  14.7 us
    all_to_all x1, blocking collectives, shards(): received = lax.all_to_all(cut, SLABS, 0, 0, tiled=True)  13.5 us
    all_to_all x1, starting transfers between devices, shards(): lax.all_to_all(copies, TGT + ('core',), 0, 0, tiled=True).reshape(-1, plane)  9.81 us
    all_to_all x1, waiting for transfers between devices, shards(): summands = lax.all_to_all(summands, PTR, 0, 0, tiled=True)  6.81 us
    unnamed x18, local copies, waits for them, and re-layouts  6.53 us
    all_to_all x1, starting transfers between devices, shards(): summands = lax.all_to_all(summands, PTR, 0, 0, tiled=True)  6.48 us
    pallas_call x1, Pallas kernels, compress(): pl.pallas_call(functools.partial(compress_body, owned), out_shape=jax.Sha...  2.96 us
  transfers between devices with their start and end apart: 4, of which 1 were waited for; matrix products, arithmetic and copies ran while one was open for 1% of the time, Pallas kernels for 8%

profile of v2, /device:TPU:1, one launch (start us, length us, event | category | flops | bytes accessed | tf_op | source)
XLA Modules:
  0.0 89.6 jit_solution(10119176928087523260)
XLA Ops:
  0.0 1.4 %collective-permute-start = (f32[1024,128]{1,0:T(8,128)}, f32[1024,128]{1,0:T(8,128)S(1)}, u32[]{:S(2)}, u32[]{:S(2)}) collective-permute-start(f32[1024,128]{1,0:T(8,128)} %bitcast.9), channel_id=1, source_target_pairs={{0,1},{1,0},{2,3},{3,2},{4,5},{5,4},{6,7},{7,6},{8,9},{9,8},{10,11... | collective-permute-start | bytes 1572872 | tf_op jit(solution)/shard_map/ppermute | solution.py:371
  2.1 0.9 %collective-permute-start.1 = (f32[1]{0:T(128)}, f32[1]{0:T(128)}, u32[]{:S(2)}, u32[]{:S(2)}) collective-permute-start(f32[1]{0:T(128)} %convert_element_type.4), channel_id=1, source_target_pairs={{0,1},{1,0},{2,3},{3,2},{4,5},{5,4},{6,7},{7,6},{8,9},{9,8},{10,11... | collective-permute-start | bytes 20 | tf_op jit(solution)/shard_map/ppermute | solution.py:372
  3.0 0.0 copy-start
  3.0 1.2 %copy-done = f32[8,32,1024]{2,1,0:T(8,128)S(1)} copy-done((f32[8,32,1024]{2,1,0:T(8,128)S(1)}, f32[8,32,1024]{2,1,0:T(8,128)}, u32[]{:S(2)}) %copy-start) | copy-done | bytes 1048600
  4.2 0.0 copy-start.1
  4.2 1.0 %copy-done.1 = f32[32,32,128]{2,1,0:T(8,128)S(1)} copy-done((f32[32,32,128]{2,1,0:T(8,128)S(1)}, f32[32,32,128]{2,1,0:T(8,128)}, u32[]{:S(2)}) %copy-start.1) | copy-done | bytes 524312
  5.2 0.0 copy-start.2
  5.2 1.2 %copy-done.2 = bf16[2,4,256,256]{3,2,1,0:T(8,128)(2,1)S(1)} copy-done((bf16[2,4,256,256]{3,2,1,0:T(8,128)(2,1)S(1)}, bf16[2,4,256,256]{3,2,1,0:T(8,128)(2,1)}, u32[]{:S(2)}) %copy-start.2) | copy-done | bytes 1048600
  6.5 0.0 copy-start.4
  6.5 1.2 %copy-done.4 = bf16[2,4,256,256]{3,2,1,0:T(8,128)(2,1)S(1)} copy-done((bf16[2,4,256,256]{3,2,1,0:T(8,128)(2,1)S(1)}, bf16[2,4,256,256]{3,2,1,0:T(8,128)(2,1)}, u32[]{:S(2)}) %copy-start.4) | copy-done | bytes 1048600
  7.7 0.0 copy-start.6
  7.7 0.9 %copy-done.6 = bf16[256,256]{1,0:T(8,128)(2,1)S(1)} copy-done((bf16[256,256]{1,0:T(8,128)(2,1)S(1)}, bf16[256,256]{1,0:T(8,128)(2,1)}, u32[]{:S(2)}) %copy-start.6) | copy-done | bytes 131096
  8.6 0.0 copy-start.7
  8.6 0.9 %copy-done.7 = f32[4,32,256]{2,1,0:T(8,128)S(1)} copy-done((f32[4,32,256]{2,1,0:T(8,128)S(1)}, f32[4,32,256]{2,1,0:T(8,128)}, u32[]{:S(2)}) %copy-start.7) | copy-done | bytes 131096
  9.5 0.0 copy-start.3
  9.5 7.2 %shard_map.82 = (f32[4,32,1024]{2,1,0:T(8,128)S(1)}, f32[4,32,1024]{2,1,0:T(8,128)S(1)}) custom-call(f32[8,32,1024]{2,1,0:T(8,128)S(1)} %copy-done, f32[1024,128]{1,0:T(8,128)S(1)} %bitcast.10, f32[1,1]{1,0:T(1,128)} %bitcast.3.refs_2_, bf16[2,4,256,256]{3,2,1,0:T(8,128)(2,1)S(1)} %copy-done.2, bf16[2,4,256,256]{3,2,1,0:T(8,128)(2,1)S(1)} %copy-done.4, ...), custom_call_target="tpu_custom_call" | custom-call | flops 1342177280 | bytes 8388608 | tf_op jit(solution)/shard_map/pallas_call | solution.py:212
  17.3 0.0 collective-permute-done.refs_2_
  17.4 0.0 copy-done.3
  17.4 0.0 copy-done.5
  17.4 0.0 copy-done.8
  17.4 7.6 %shard_map.83 = f32[8,16,1024]{2,1,0:T(8,128)S(1)} custom-call(f32[4,32,1024]{2,1,0:T(8,128)S(1)} %get-tuple-element.7.refs_0_, f32[4,32,1024]{2,1,0:T(8,128)S(1)} %get-tuple-element.8.refs_1_, f32[1024,128]{1,0:T(8,128)S(1)} %collective-permute-done.refs_2_, f32[1,1]{1,0:T(1,128)} %bitcast.4.refs_3_, bf16[2,4,256,256]{3,2,1,0:T(8,128)(2,1)S(1)} %copy-done.3, ...), custom_call_target="tpu_custom_call" | custom-call | flops 1342177280 | bytes 8388608 | tf_op jit(solution)/shard_map/pallas_call | solution.py:212
  24.9 13.5 %all_to_all.15.in_ref = f32[8,16,1024]{2,1,0:T(8,128)S(1)} all-to-all(f32[8,16,1024]{2,1,0:T(8,128)S(1)} %shard_map.83), channel_id=1, replica_groups=mesh['tgt_0'=2,'tgt_1'=4,'ptr_0'=4,'ptr_1'=2,'core'=2] {'ptr_0','ptr_1'}, dimensions={0} | all-to-all | bytes 1048576 | tf_op jit(solution)/shard_map/all_to_all | solution.py:380
  38.4 0.8 shard_map.84
  39.3 9.8 %all-to-all-start.1 = ((f32[16,8,1024]{2,1,0:T(8,128)}), f32[16,8,1024]{2,1,0:T(8,128)S(1)}, u32[]{:S(2)}, u32[]{:S(2)}) async-start(f32[16,8,1024]{2,1,0:T(8,128)} %shard_map.84), calls=%async_computation.1 | async-start | bytes 1048576 | tf_op jit(solution)/shard_map/all_to_all | solution.py:382
  49.1 1.0 %constant_dynamic-slice_fusion = f32[8,2,1024]{2,1,0:T(2,128)S(1)} fusion(f32[8,32,1024]{2,1,0:T(8,128)} %refs_0_.1, s32[]{:T(128)S(6)} %select_n.3), kind=kLoop, calls=%fused_computation | loop fusion | bytes 131076 | tf_op jit(solution)/shard_map/dynamic_slice | solution.py:375
  50.1 11.9 %all_gather.6 = f32[64,1024]{1,0:T(8,128)S(1)} all-gather(f32[16,1024]{1,0:T(8,128)S(1)} %reshape.19), channel_id=1, replica_groups=mesh['tgt_0'=2,'tgt_1'=4,'ptr_0'=4,'ptr_1'=2,'core'=2] {'tgt_1'}, dimensions={0}, use_global_device_ids=true | all-gather | bytes 327680 | tf_op jit(solution)/shard_map/all_gather | solution.py:362
  62.0 9.2 %all_gather.7.t_ref = f32[128,1024]{1,0:T(8,128)S(1)} all-gather(f32[64,1024]{1,0:T(8,128)S(1)} %all_gather.6), channel_id=1, replica_groups=mesh['tgt_0'=2,'tgt_1'=4,'ptr_0'=4,'ptr_1'=2,'core'=2] {'tgt_0'}, dimensions={0}, use_global_device_ids=true | all-gather | bytes 786432 | tf_op jit(solution)/shard_map/all_gather | solution.py:362
  71.3 0.0 all-to-all-done.1
  71.3 1.4 %shard_map.85 = f32[16,32,128]{2,1,0:T(8,128)} custom-call(f32[128,1024]{1,0:T(8,128)S(1)} %all_gather.7.t_ref, f32[128,1024]{1,0:T(8,128)S(1)} %bitcast.7), custom_call_target="tpu_custom_call" | custom-call | tf_op jit(solution)/shard_map/pallas_call | solution.py:291
  72.7 6.5 %all-to-all-start.2 = ((f32[16,32,128]{2,1,0:T(8,128)}), f32[16,32,128]{2,1,0:T(8,128)S(1)}, u32[]{:S(2)}, u32[]{:S(2)}) async-start(f32[16,32,128]{2,1,0:T(8,128)} %shard_map.85), calls=%async_computation.2 | async-start | bytes 524288 | tf_op jit(solution)/shard_map/all_to_all | solution.py:384
  79.8 6.8 %all-to-all-done.2.s_ref = f32[16,32,128]{2,1,0:T(8,128)S(1)} async-done(((f32[16,32,128]{2,1,0:T(8,128)}), f32[16,32,128]{2,1,0:T(8,128)S(1)}, u32[]{:S(2)}, u32[]{:S(2)}) %all-to-all-start.2) | async-done | bytes 262176 | tf_op jit(solution)/shard_map/all_to_all | solution.py:384
  86.6 3.0 %shard_map.86 = f32[8,2,1024]{2,1,0:T(2,128)} custom-call(f32[16,32,128]{2,1,0:T(8,128)S(1)} %all-to-all-done.2.s_ref, f32[128,1024]{1,0:T(8,128)S(1)} %bitcast.8, s32[1]{0:T(128)S(6)} %copy.11.keep_ref), custom_call_target="tpu_custom_call" | custom-call | tf_op jit(solution)/shard_map/pallas_call | solution.py:350
  (5 shorter events, 0.1 us)
Async XLA Ops:
  0.0 17.3 %collective-permute-start = (f32[1024,128]{1,0:T(8,128)}, f32[1024,128]{1,0:T(8,128)S(1)}, u32[]{:S(2)}, u32[]{:S(2)}) collective-permute-start(f32[1024,128]{1,0:T(8,128)} %bitcast.9), channel_id=1, source_target_pairs={{0,1},{1,0},{2,3},{3,2},{4,5},{5,4},{6,7},{7,6},{8,9},{9,8},{10,11... | collective-permute-start | bytes 1572872 | tf_op jit(solution)/shard_map/ppermute | solution.py:371
  2.1 14.6 %collective-permute-start.1 = (f32[1]{0:T(128)}, f32[1]{0:T(128)}, u32[]{:S(2)}, u32[]{:S(2)}) collective-permute-start(f32[1]{0:T(128)} %convert_element_type.4), channel_id=1, source_target_pairs={{0,1},{1,0},{2,3},{3,2},{4,5},{5,4},{6,7},{7,6},{8,9},{9,8},{10,11... | collective-permute-start | bytes 20 | tf_op jit(solution)/shard_map/ppermute | solution.py:372
  3.0 1.2 %copy-start = (f32[8,32,1024]{2,1,0:T(8,128)S(1)}, f32[8,32,1024]{2,1,0:T(8,128)}, u32[]{:S(2)}) copy-start(f32[8,32,1024]{2,1,0:T(8,128)} %refs_0_.1) | copy-start | bytes 3145732
  4.2 1.0 %copy-start.1 = (f32[32,32,128]{2,1,0:T(8,128)S(1)}, f32[32,32,128]{2,1,0:T(8,128)}, u32[]{:S(2)}) copy-start(f32[32,32,128]{2,1,0:T(8,128)} %param.9) | copy-start | bytes 1572868
  5.2 1.2 %copy-start.2 = (bf16[2,4,256,256]{3,2,1,0:T(8,128)(2,1)S(1)}, bf16[2,4,256,256]{3,2,1,0:T(8,128)(2,1)}, u32[]{:S(2)}) copy-start(bf16[2,4,256,256]{3,2,1,0:T(8,128)(2,1)} %constant.31.clone.refs_3_.refs_4_) | copy-start | bytes 3145732
  6.5 1.2 %copy-start.4 = (bf16[2,4,256,256]{3,2,1,0:T(8,128)(2,1)S(1)}, bf16[2,4,256,256]{3,2,1,0:T(8,128)(2,1)}, u32[]{:S(2)}) copy-start(bf16[2,4,256,256]{3,2,1,0:T(8,128)(2,1)} %constant.32.clone.refs_4_.refs_5_) | copy-start | bytes 3145732
  7.7 0.9 %copy-start.6 = (bf16[256,256]{1,0:T(8,128)(2,1)S(1)}, bf16[256,256]{1,0:T(8,128)(2,1)}, u32[]{:S(2)}) copy-start(bf16[256,256]{1,0:T(8,128)(2,1)} %constant.33.clone.refs_5_.refs_6_) | copy-start | bytes 393220
  8.6 0.9 %copy-start.7 = (f32[4,32,256]{2,1,0:T(8,128)S(1)}, f32[4,32,256]{2,1,0:T(8,128)}, u32[]{:S(2)}) copy-start(f32[4,32,256]{2,1,0:T(8,128)} %constant.34.clone.refs_6_.refs_7_) | copy-start | bytes 393220
  9.5 7.8 %copy-start.3 = (bf16[2,4,256,256]{3,2,1,0:T(8,128)(2,1)S(1)}, bf16[2,4,256,256]{3,2,1,0:T(8,128)(2,1)}, u32[]{:S(2)}) copy-start(bf16[2,4,256,256]{3,2,1,0:T(8,128)(2,1)} %constant.31.clone.refs_3_.refs_4_) | copy-start | bytes 3145732
  9.5 7.9 %copy-start.5 = (bf16[2,4,256,256]{3,2,1,0:T(8,128)(2,1)S(1)}, bf16[2,4,256,256]{3,2,1,0:T(8,128)(2,1)}, u32[]{:S(2)}) copy-start(bf16[2,4,256,256]{3,2,1,0:T(8,128)(2,1)} %constant.32.clone.refs_4_.refs_5_) | copy-start | bytes 3145732
  9.5 7.9 %copy-start.8 = (f32[4,32,256]{2,1,0:T(8,128)S(1)}, f32[4,32,256]{2,1,0:T(8,128)}, u32[]{:S(2)}) copy-start(f32[4,32,256]{2,1,0:T(8,128)} %constant.34.clone.refs_6_.refs_7_) | copy-start | bytes 393220
  39.3 32.0 %all-to-all-start.1 = ((f32[16,8,1024]{2,1,0:T(8,128)}), f32[16,8,1024]{2,1,0:T(8,128)S(1)}, u32[]{:S(2)}, u32[]{:S(2)}) async-start(f32[16,8,1024]{2,1,0:T(8,128)} %shard_map.84), calls=%async_computation.1 | async-start | bytes 1048576 | tf_op jit(solution)/shard_map/all_to_all | solution.py:382
  72.7 13.9 %all-to-all-start.2 = ((f32[16,32,128]{2,1,0:T(8,128)}), f32[16,32,128]{2,1,0:T(8,128)S(1)}, u32[]{:S(2)}, u32[]{:S(2)}) async-start(f32[16,32,128]{2,1,0:T(8,128)} %shard_map.85), calls=%async_computation.2 | async-start | bytes 524288 | tf_op jit(solution)/shard_map/all_to_all | solution.py:384

commit v3 on v2

v3 whole, which is shorter than its diff:
```python
import functools

import jax
import jax.numpy as jnp
import ml_dtypes
import numpy as np
from jax import lax
from jax.experimental import pallas as pl
from jax.experimental.pallas import tpu as pltpu
from jax.sharding import Mesh
from jax.sharding import PartitionSpec as P

TGT = ("tgt_0", "tgt_1")
PTR = ("ptr_0", "ptr_1", "core")
SLABS = ("ptr_0", "ptr_1")
LANES = 128
SOLVE_PARAMS = pltpu.CompilerParams(vmem_limit_bytes=24 << 20)
SMALL_PARAMS = pltpu.CompilerParams(vmem_limit_bytes=16 << 20)


def split_np(a):
    a = a.astype(np.float64)
    hi = a.astype(np.float32).astype(ml_dtypes.bfloat16)
    lo = (a - hi.astype(np.float64)).astype(np.float32).astype(ml_dtypes.bfloat16)
    return hi, lo


def half_bases(n):
    h = n // 2
    y = np.arange(h) + 0.5
    even_k, odd_k = np.arange(h), np.arange(1, h + 1)
    even = np.cos(2 * np.pi * even_k[:, None] * y[None] / n) * np.sqrt(2.0 / h)
    even[0] *= np.sqrt(0.5)
    odd = np.sin(2 * np.pi * odd_k[:, None] * y[None] / n) * np.sqrt(2.0 / h)
    odd[-1] *= np.sqrt(0.5)
    return (even, odd), (even_k, odd_k)


def tables(n, reps):
    bases, freqs = half_bases(n)
    planes, kernels = [], []
    ix = np.arange(n)
    wave = lambda k: (k * (2 * np.pi / n)) ** 2
    wx = wave(np.where(ix < n // 2, ix, ix - n))
    for sy in (0, 1):
        for sz in (0, 1):
            m = np.einsum("ky,lz->yzkl", bases[sy], bases[sz])
            planes.append(m.reshape(n * n // 4, n * n // 4))
            total = wx[:, None, None] + wave(freqs[sy])[:, None] + wave(freqs[sz])[None]
            g = np.where(total > 0, 4 * np.pi / np.where(total > 0, total, 1.0), 0.0)
            kernels.append(g.reshape(n, -1) / 4)
    planes = np.stack(planes)
    phase = 2 * np.pi * (ix[:, None] * ix[None] % n) / n
    wh, wl = split_np(np.kron(np.eye(reps), (np.cos(phase) + np.sin(phase)) / np.sqrt(n)))
    left = np.block([[wh, wh], [wl, np.zeros_like(wl)]]).astype(ml_dtypes.bfloat16)
    matrices = [*split_np(planes), *split_np(np.swapaxes(planes, 1, 2)), left[None]]
    return np.concatenate(matrices), np.stack(kernels).astype(np.float32)


def split(v):
    hi = v.astype(jnp.bfloat16)
    return hi, (v - hi.astype(jnp.float32)).astype(jnp.bfloat16)


def dot(a, b):
    return jnp.dot(a, b, preferred_element_type=jnp.float32)


def take(v, idx):
    return jnp.take_along_axis(v, idx, axis=1)


def fold(tiles, rows):
    lane = lax.broadcasted_iota(jnp.int32, (rows, LANES), 1)
    y, z = (lane // 16) % 4, lane % 16
    out = {}
    for sy in (0, 1):
        for sz in (0, 1):
            idx = (3 - y if sy else y) * 32 + (31 - z if sz else z)
            for h in (0, 1):
                a, b = (7 - 2 * h, 6 - 2 * h) if sy else (2 * h, 2 * h + 1)
                out[2 * sy + sz, h] = jnp.where(lane < 64, take(tiles[a], idx), take(tiles[b], idx))
    return out


def unfold(folded, rows):
    lane = lax.broadcasted_iota(jnp.int32, (rows, LANES), 1)
    y, z = lane // 32, lane % 32
    low = z < 16
    z = jnp.where(low, z, 31 - z)
    out = []
    for t in range(8):
        sy = t // 4
        h = (7 - t) // 2 if sy else t // 2
        first = 7 - 4 * (t % 2) if sy else 4 * (t % 2)
        idx = (first - y if sy else first + y) * 16 + z
        out.append(jnp.where(low, take(folded[2 * sy, h], idx), take(folded[2 * sy + 1, h], idx)))
    return out


def butterfly(d):
    a, b, c, e = d[0] + d[1], d[0] - d[1], d[2] + d[3], d[2] - d[3]
    return a + c, b + e, a - c, b - e


def fold_body(nj, n, p_ref, occ_hbm, keep_hbm, o_ref, keep_ref, scalars, sems):
    copies = [
        pltpu.make_async_copy(src, scalars.at[i], sems.at[i]) for i, src in enumerate((occ_hbm, keep_hbm))
    ]
    for copy in copies:
        copy.start()
    for copy in copies:
        copy.wait()
    keep_ref[...] = jnp.full(keep_ref.shape, scalars[1, 0], jnp.int32)
    occ = jnp.full((n, LANES), scalars[0, 0], jnp.int32).astype(jnp.float32)
    root = jnp.sqrt(0.25 + 0.75 * occ)
    quarter = n * n // 4
    lane = lax.broadcasted_iota(jnp.int32, (n, LANES), 1)
    for j in range(nj):
        tiles = []
        for t in range(8):
            acc = None
            for y in range(4):
                src = p_ref[pl.ds(4 * t + y, n, stride=n), :]
                if y != j:
                    src = pltpu.roll(src, ((y - j) % 4) * n, 1)
                acc = src if acc is None else jnp.where(lane // n == y, src, acc)
            tiles.append(acc * root)
        for (s, h), v in fold(tiles, n).items():
            o_ref[j * n : (j + 1) * n, s * quarter + h * LANES : s * quarter + (h + 1) * LANES] = v


def folded_partners(partners, occupied, retained):
    n = partners.shape[0]
    nj = partners.shape[2] // n
    vmem = pl.BlockSpec(memory_space=pltpu.VMEM)
    hbm = pl.BlockSpec(memory_space=pltpu.HBM)
    return pl.pallas_call(
        functools.partial(fold_body, nj, n),
        out_shape=(
            jax.ShapeDtypeStruct((nj * n, n * n), jnp.float32),
            jax.ShapeDtypeStruct((8, LANES), jnp.int32),
        ),
        in_specs=[vmem, hbm, hbm],
        out_specs=(vmem, vmem),
        scratch_shapes=[pltpu.SMEM((2, 1), jnp.int32), pltpu.SemaphoreType.DMA((2,))],
        compiler_params=SMALL_PARAMS,
        cost_estimate=pl.CostEstimate(flops=2 << 30, bytes_accessed=8 << 20, transcendentals=0),
    )(partners.reshape(n * n, -1), occupied, retained)


def solve_body(last, tb, nj, n, *refs):
    if last:
        tf, prior, pf, w_ref, k_ref, o_ref = refs[:6]
    else:
        t_ref, pf, w_ref, k_ref, o_ref, tf = refs[:6]
    gh, gl, ust, ps = refs[6:]
    rows, quarter = nj * n, n * n // 4
    if not last:
        first = lax.axis_index("core") * tb
        for i in range(tb):
            tiles = [t_ref[first + i, :, LANES * t : LANES * (t + 1)] for t in range(8)]
            for (s, h), v in fold(tiles, n).items():
                tf[i, :, s * quarter + h * LANES : s * quarter + (h + 1) * LANES] = v
    for i in range(tb):
        for j in range(nj):
            r = slice(j * n, (j + 1) * n)
            q = slice(i * rows + j * n, i * rows + (j + 1) * n)
            d = [
                tf[i, :, quarter * s : quarter * (s + 1)] * pf[r, quarter * s : quarter * (s + 1)]
                for s in range(4)
            ]
            for s, g in enumerate(butterfly(d)):
                gh[s, q, :], gl[s, q, :] = split(g)
    left = w_ref[16]
    for s in range(4):
        mh, ml, bh, bl = (w_ref[4 * k + s] for k in range(4))
        u = dot(gh[s], mh) + dot(gl[s], mh) + dot(gh[s], ml)
        for i in range(tb):
            at = slice(i * rows, (i + 1) * rows)
            ust[i, :rows, :], ust[i, rows:, :] = split(u[at])
            v = dot(left, ust[i])
            v = (v[:rows] + v[rows:]).reshape(nj, n, quarter) * k_ref[s][None]
            ust[i, :rows, :], ust[i, rows:, :] = split(v.reshape(rows, quarter))
            v = dot(left, ust[i])
            gh[s, at, :], gl[s, at, :] = split(v[:rows] + v[rows:])
        ps[s] = dot(gh[s], bh) + dot(gl[s], bh) + dot(gh[s], bl)
    for i in range(tb):
        acc = [prior[i, :, quarter * s : quarter * (s + 1)] if last else None for s in range(4)]
        for j in range(nj):
            r = slice(j * n, (j + 1) * n)
            q = slice(i * rows + j * n, i * rows + (j + 1) * n)
            for s, v in enumerate(butterfly([ps[s, q, :] for s in range(4)])):
                v = v * pf[r, quarter * s : quarter * (s + 1)]
                acc[s] = v if acc[s] is None else acc[s] + v
        if last:
            folded = {(s, h): acc[s][:, LANES * h : LANES * (h + 1)] for s in range(4) for h in (0, 1)}
            peers = o_ref.shape[0]
            each = n // peers
            for t, v in enumerate(unfold(folded, n)):
                for d in range(peers):
                    o_ref[d, i * each : (i + 1) * each, LANES * t : LANES * (t + 1)] = v[
                        d * each : (d + 1) * each
                    ]
        else:
            for s in range(4):
                o_ref[i, :, quarter * s : quarter * (s + 1)] = acc[s]


def solve(targets, partners, consts, prior=None, peers=8):
    last = prior is not None
    n = targets.shape[1]
    nj = partners.shape[0] // n
    tb = prior.shape[0] if last else targets.shape[0] // 2
    rows, quarter = nj * n, n * n // 4
    vmem = pl.BlockSpec(memory_space=pltpu.VMEM)
    part = jax.ShapeDtypeStruct((tb, n, n * n), jnp.float32)
    if last:
        operands = (targets, prior, partners, *consts)
        out_shape = jax.ShapeDtypeStruct((peers, tb * n // peers, n * n), jnp.float32)
    else:
        operands = (targets, partners, *consts)
        out_shape = (part, part)
    return pl.pallas_call(
        functools.partial(solve_body, last, tb, nj, n),
        out_shape=out_shape,
        in_specs=[vmem] * len(operands),
        out_specs=vmem if last else (vmem, vmem),
        scratch_shapes=[
            pltpu.VMEM((4, tb * rows, quarter), jnp.bfloat16),
            pltpu.VMEM((4, tb * rows, quarter), jnp.bfloat16),
            pltpu.VMEM((tb, 2 * rows, quarter), jnp.bfloat16),
            pltpu.VMEM((4, tb * rows, quarter), jnp.float32),
        ],
        compiler_params=SOLVE_PARAMS,
        cost_estimate=pl.CostEstimate(
            flops=2 * 5 * tb * 4 * rows * quarter * quarter, bytes_accessed=8 << 20, transcendentals=0
        ),
    )(*operands)


def spread_body(copies, slab_axes, in_ref, t_ref, o_ref):
    peers, rows, plane = in_ref.shape
    each = t_ref.shape[1] // peers
    own = rows // each
    first = lax.axis_index(slab_axes) * each
    t_first = lax.axis_index("core") * own
    total = in_ref[0]
    for k in range(1, peers):
        total = total + in_ref[k]
    half = each // 2
    for core in (0, 1):
        planes = [(q, i) for q in range(half) for i in range(own)]
        picked = [total[i * each + half * core + q : i * each + half * core + q + 1] for q, i in planes]
        picked += [t_ref[t_first + i, pl.ds(first + half * core + q, 1), :] for q, i in planes]
        picked = jnp.concatenate(picked, axis=0)
        for k in range(copies):
            o_ref[2 * k + core] = picked


def spread(received, targets, copies):
    _, rows, plane = received.shape
    vmem = pl.BlockSpec(memory_space=pltpu.VMEM)
    return pl.pallas_call(
        functools.partial(spread_body, copies, SLABS),
        out_shape=jax.ShapeDtypeStruct((2 * copies, rows, plane), jnp.float32),
        in_specs=[vmem, vmem],
        out_specs=vmem,
        compiler_params=SMALL_PARAMS,
    )(received, targets)


def plane_of(ref, q, part):
    first = 8 * part + 4 * q
    return jnp.concatenate([ref[k, first : first + 4, :] for k in range(ref.shape[0])], axis=0)


def overlap_body(scale, a_ref, o_ref):
    total = None
    for q in (0, 1):
        s = lax.dot_general(
            plane_of(a_ref, q, 1),
            plane_of(a_ref, q, 0),
            (((1,), (1,)), ((), ())),
            precision=lax.Precision.HIGHEST,
            preferred_element_type=jnp.float32,
        )
        total = s if total is None else total + s
    total = total * scale
    half = total.shape[0] // 2
    packed = jnp.concatenate([total[:half], total[half:]], axis=1)
    for k in range(o_ref.shape[0]):
        o_ref[k] = packed


def overlap(slab, copies, scale):
    count = slab.shape[0] * 4
    return pl.pallas_call(
        functools.partial(overlap_body, scale),
        out_shape=jax.ShapeDtypeStruct((copies, count // 2, 2 * count), jnp.float32),
        compiler_params=SMALL_PARAMS,
    )(slab)


def compress_body(owned, s_ref, a_ref, keep_ref, o_ref, inv_ref):
    total = s_ref[0]
    for k in range(1, s_ref.shape[0]):
        total = total + s_ref[k]
    half = total.shape[0]
    count = 2 * half
    square = jnp.concatenate([total[:, :count], total[:, count:]], axis=0)
    square = 0.5 * (square + square.T)
    row = lax.broadcasted_iota(jnp.int32, (count, count), 0)
    col = lax.broadcasted_iota(jnp.int32, (count, count), 1)
    wide = jnp.concatenate([square, jnp.where(row == col, 1.0, 0.0)], axis=1)
    tiles = [wide[8 * t : 8 * t + 8] for t in range(count // 8)]
    sub = lax.broadcasted_iota(jnp.int32, (8, LANES), 0)
    down = lambda v, k: jnp.broadcast_to(v[k : k + 1], (8, LANES))
    for p in range(count // 8):
        later = range(p, count // 8)
        cols = {
            (t, k): jnp.broadcast_to(tiles[t][:, 8 * p + k : 8 * p + k + 1], (8, LANES))
            for t in later
            for k in range(8)
        }
        root = jnp.ones((8, LANES), jnp.float32)
        for k in range(8):
            pivot = down(cols[p, k], k)
            over = 1.0 / pivot
            root = jnp.where(sub == k, lax.rsqrt(pivot), root)
            line = down(tiles[p], k)
            cross = [down(cols[p, m], k) for m in range(k + 1, 8)]
            for t in later:
                f = cols[t, k] * over
                if t == p:
                    f = jnp.where(sub > k, f, 0.0)
                tiles[t] = tiles[t] - f * line
                for m in range(k + 1, 8):
                    cols[t, m] = cols[t, m] - f * cross[m - k - 1]
        inv_ref[8 * p : 8 * p + 8, :] = tiles[p] * root
    first = lax.axis_index(TGT) * owned
    mine = inv_ref[pl.ds(pl.multiple_of(first, 8), owned), :][:, count:]
    kept = first + lax.broadcasted_iota(jnp.int32, (owned, count), 0) < keep_ref[:owned, :count]
    mine = jnp.where(kept, mine, 0.0)
    for q in (0, 1):
        o_ref[:, q, :] = jnp.dot(
            mine,
            plane_of(a_ref, q, 0),
            precision=lax.Precision.HIGHEST,
            preferred_element_type=jnp.float32,
        )


def compress(summands, slab, keep, owned):
    count = slab.shape[0] * 4
    vmem = pl.BlockSpec(memory_space=pltpu.VMEM)
    return pl.pallas_call(
        functools.partial(compress_body, owned),
        out_shape=jax.ShapeDtypeStruct((owned, 2, slab.shape[2]), jnp.float32),
        in_specs=[vmem] * 3,
        out_specs=vmem,
        scratch_shapes=[pltpu.VMEM((count, LANES), jnp.float32)],
        compiler_params=SMALL_PARAMS,
    )(summands, slab, keep)


def shards(targets, partners, occupied, retained):
    owned, n, plane = targets.shape
    consts = [jnp.asarray(c) for c in tables(n, partners.shape[2] // n)]
    own_partners, keep = folded_partners(partners, occupied, retained)
    other_partners = lax.ppermute(own_partners, "core", [(0, 1), (1, 0)])
    partial_actions, folded = solve(targets, own_partners, consts)
    cut = solve(folded, other_partners, consts, partial_actions, lax.axis_size(SLABS))
    received = lax.all_to_all(cut, SLABS, 0, 0, tiled=True)
    copies = spread(received, targets, lax.axis_size(TGT))
    slab = lax.all_to_all(copies, TGT + ("core",), 0, 0, tiled=True)
    summands = overlap(slab, lax.axis_size(PTR), 1.0 / n**3)
    summands = lax.all_to_all(summands, PTR, 0, 0, tiled=True)
    return compress(summands, slab, keep, owned)


def solution(mesh):
    names = TGT + PTR
    finer = Mesh(mesh.devices.reshape(2, 4, 4, 2, 2), names)
    in_specs = (P(TGT, None, None), P(None, None, PTR), P(PTR), P())
    out_specs = P(TGT, PTR, None)
    return jax.shard_map(
        shards, mesh=finer, in_specs=in_specs, out_specs=out_specs, check_vma=False
    )
```

time: 90.2 us -> 71.5 us (0.79)
  starting transfers between devices: 18.6 us -> 1.5 us
  blocking collectives: 34.6 us -> 51.1 us
  waiting for transfers between devices: 6.81 us -> 0.01 us
  local copies, waits for them, and re-layouts: 7.56 us -> 1.05 us
  Pallas kernels: 20 us -> 16.2 us
    all_to_all x0 -> x2, blocking collectives: none -> 36.6 us  [the longest x1 25.5 us: shards(): slab = lax.all_to_all(copies, TGT + ('core',), 0, 0, tiled=True)]
    all_gather x2 -> x0, blocking collectives: 21.2 us -> none  [gathered(): shard = lax.all_gather(shard, name, axis=0, tiled=True)]
    all_to_all x2 -> x0, starting transfers between devices: 16.3 us -> none  [the longest x1 9.81 us: shards(): lax.all_to_all(copies, TGT + ('core',), 0, 0, tiled=True).reshape(-1, plane)]
    all_to_all x2 -> x0, waiting for transfers between devices: 6.81 us -> none  [the longest x1 6.81 us: shards(): summands = lax.all_to_all(summands, PTR, 0, 0, tiled=True)]
    unnamed x18 -> x8, local copies, waits for them, and re-layouts: 6.53 us -> 1.05 us
    pallas_call x2, Pallas kernels: 14.7 us -> 10.5 us  [solve(): pl.pallas_call(functools.partial(solve_body, last, tb, nj, n), out_shape=...]
    pallas_call x1 -> x2, Pallas kernels: 0.85 us -> 2.06 us  [the longest x1 1.96 us: folded_partners(): pl.pallas_call(functools.partial(fold_body, nj, n), out_shape=(jax.ShapeD...]
    all_to_all x1, blocking collectives: 13.5 us -> 14.5 us  [shards(): received = lax.all_to_all(cut, SLABS, 0, 0, tiled=True)]
  transfers between devices with their start and end apart: 4 -> 1, of which waited for: 1 -> 0; matrix products, arithmetic and copies ran while one was open for 1% -> 0% of each run, Pallas kernels for 8% -> 7%
where the time goes in v3:
time: 71.5 us; the launch traced here: 71.2 us
  blocking collectives  51.1 us (71%)
  Pallas kernels  16.2 us (23%)
  starting transfers between devices  1.5 us (2%)
  between operations  1.35 us (2%)
  local copies, waits for them, and re-layouts  1.05 us (1%)
    all_to_all x1, blocking collectives, shards(): slab = lax.all_to_all(copies, TGT + ('core',), 0, 0, tiled=True)  25.5 us
    all_to_all x1, blocking collectives, shards(): received = lax.all_to_all(cut, SLABS, 0, 0, tiled=True)  14.5 us
    all_to_all x1, blocking collectives, shards(): summands = lax.all_to_all(summands, PTR, 0, 0, tiled=True)  11.1 us
    pallas_call x2, Pallas kernels, solve(): pl.pallas_call(functools.partial(solve_body, last, tb, nj, n), out_shape=...  10.5 us
    pallas_call x1, Pallas kernels, compress(): pl.pallas_call(functools.partial(compress_body, owned), out_shape=jax.Sha...  2.96 us
    pallas_call x1, Pallas kernels, folded_partners(): pl.pallas_call(functools.partial(fold_body, nj, n), out_shape=(jax.ShapeD...  1.96 us
    ppermute x1, starting transfers between devices, shards(): other_partners = lax.ppermute(own_partners, 'core', [(0, 1), (1, 0)])  1.5 us
  transfers between devices with their start and end apart: 1, of which 0 were waited for; matrix products, arithmetic and copies ran while one was open for 0% of the time, Pallas kernels for 7%

profile of v3, /device:TPU:1, one launch (start us, length us, event | category | flops | bytes accessed | tf_op | source)
XLA Modules:
  0.0 71.2 jit_solution(18346391596959102972)
XLA Ops:
  1.3 0.0 copy-start.1
  1.3 1.0 %copy-done.1 = f32[32,32,128]{2,1,0:T(8,128)S(1)} copy-done((f32[32,32,128]{2,1,0:T(8,128)S(1)}, f32[32,32,128]{2,1,0:T(8,128)}, u32[]{:S(2)}) %copy-start.1) | copy-done | bytes 524312
  2.3 0.0 copy-start
  2.3 0.0 copy-start.2
  2.3 0.0 copy-start.3
  2.3 2.0 %shard_map.64 = (f32[128,1024]{1,0:T(8,128)S(1)}, s32[8,128]{1,0:T(8,128)S(1)}) custom-call(f32[1024,128]{1,0:T(8,128)S(1)} %bitcast.1, s32[1]{0:T(128)S(6)} %copy.7.occ_hbm, s32[1]{0:T(128)S(6)} %copy.8.keep_hbm), custom_call_target="tpu_custom_call" | custom-call | flops 2147483648 | bytes 8388608 | tf_op jit(solution)/shard_map/pallas_call | solution.py:138
  4.3 1.5 %collective-permute-start = (f32[128,1024]{1,0:T(8,128)S(1)}, f32[128,1024]{1,0:T(8,128)S(1)}, u32[]{:S(2)}, u32[]{:S(2)}) collective-permute-start(f32[128,1024]{1,0:T(8,128)S(1)} %get-tuple-element.9.refs_1_), channel_id=1, source_target_pairs={{0,1},{1,0},{2,3},{3,2},{4,5},{5,4},{6,7},{7,6},{8,9},{9,8},{10,11... | collective-permute-start | bytes 1572872 | tf_op jit(solution)/shard_map/ppermute | solution.py:371
  5.8 0.0 copy-done
  5.8 0.0 copy-done.2
  5.8 0.0 copy-done.3
  5.8 5.1 %shard_map.65 = (f32[4,32,1024]{2,1,0:T(8,128)S(1)}, f32[4,32,1024]{2,1,0:T(8,128)S(1)}) custom-call(f32[8,32,1024]{2,1,0:T(8,128)S(1)} %copy-done, f32[128,1024]{1,0:T(8,128)S(1)} %get-tuple-element.9.refs_1_, bf16[17,256,256]{2,1,0:T(8,128)(2,1)S(1)} %copy-done.2, f32[4,32,256]{2,1,0:T(8,128)S(1)} %copy-done.3), custom_call_target="tpu_custom_call" | custom-call | flops 1342177280 | bytes 8388608 | tf_op jit(solution)/shard_map/pallas_call | solution.py:224
  10.9 0.0 collective-permute-done.refs_2_
  10.9 5.4 %shard_map.66 = f32[8,16,1024]{2,1,0:T(8,128)S(1)} custom-call(f32[4,32,1024]{2,1,0:T(8,128)S(1)} %get-tuple-element.10.refs_0_, f32[4,32,1024]{2,1,0:T(8,128)S(1)} %get-tuple-element.11.refs_1_, f32[128,1024]{1,0:T(8,128)S(1)} %collective-permute-done.refs_2_, bf16[17,256,256]{2,1,0:T(8,128)(2,1)S(1)} %copy-done.2, f32[4,32,256]{2,1,0:T(8,128)S(1)} %copy-done.3), custom_call_target="tpu_custom_call" | custom-call | flops 1342177280 | bytes 8388608 | tf_op jit(solution)/shard_map/pallas_call | solution.py:224
  16.3 14.5 %all_to_all.15.in_ref = f32[8,16,1024]{2,1,0:T(8,128)S(1)} all-to-all(f32[8,16,1024]{2,1,0:T(8,128)S(1)} %shard_map.66), channel_id=1, replica_groups=mesh['tgt_0'=2,'tgt_1'=4,'ptr_0'=4,'ptr_1'=2,'core'=2] {'ptr_0','ptr_1'}, dimensions={0} | all-to-all | bytes 1048576 | tf_op jit(solution)/shard_map/all_to_all | solution.py:374
  30.8 0.1 shard_map.67
  30.9 25.5 %all_to_all.16.a_ref = f32[16,16,1024]{2,1,0:T(8,128)S(1)} all-to-all(f32[16,16,1024]{2,1,0:T(8,128)S(1)} %shard_map.67), channel_id=1, replica_groups=mesh['tgt_0'=2,'tgt_1'=4,'ptr_0'=4,'ptr_1'=2,'core'=2] {'tgt_0','tgt_1',..., dimensions={0} | all-to-all | bytes 2097152 | tf_op jit(solution)/shard_map/all_to_all | solution.py:376
  56.4 0.7 %shard_map.68 = f32[16,32,128]{2,1,0:T(8,128)S(1)} custom-call(f32[16,16,1024]{2,1,0:T(8,128)S(1)} %all_to_all.16.a_ref), custom_call_target="tpu_custom_call" | custom-call | tf_op jit(solution)/shard_map/pallas_call | solution.py:298
  57.1 11.1 %all_to_all.17.s_ref = f32[16,32,128]{2,1,0:T(8,128)S(1)} all-to-all(f32[16,32,128]{2,1,0:T(8,128)S(1)} %shard_map.68), channel_id=1, replica_groups=mesh['tgt_0'=2,'tgt_1'=4,'ptr_0'=4,'ptr_1'=2,'core'=2] {'ptr_0','ptr_1',..., dimensions={0} | all-to-all | bytes 524288 | tf_op jit(solution)/shard_map/all_to_all | solution.py:378
  68.2 3.0 %shard_map.69 = f32[8,2,1024]{2,1,0:T(2,128)} custom-call(f32[16,32,128]{2,1,0:T(8,128)S(1)} %all_to_all.17.s_ref, f32[16,16,1024]{2,1,0:T(8,128)S(1)} %all_to_all.16.a_ref, s32[8,128]{1,0:T(8,128)S(1)} %get-tuple-element.12.keep_ref), custom_call_target="tpu_custom_call" | custom-call | tf_op jit(solution)/shard_map/pallas_call | solution.py:357
Async XLA Ops:
  1.3 1.0 %copy-start.1 = (f32[32,32,128]{2,1,0:T(8,128)S(1)}, f32[32,32,128]{2,1,0:T(8,128)}, u32[]{:S(2)}) copy-start(f32[32,32,128]{2,1,0:T(8,128)} %param.7) | copy-start | bytes 1572868
  2.3 3.5 %copy-start = (f32[8,32,1024]{2,1,0:T(8,128)S(1)}, f32[8,32,1024]{2,1,0:T(8,128)}, u32[]{:S(2)}) copy-start(f32[8,32,1024]{2,1,0:T(8,128)} %t_ref.1) | copy-start | bytes 3145732
  2.3 3.5 %copy-start.2 = (bf16[17,256,256]{2,1,0:T(8,128)(2,1)S(1)}, bf16[17,256,256]{2,1,0:T(8,128)(2,1)}, u32[]{:S(2)}) copy-start(bf16[17,256,256]{2,1,0:T(8,128)(2,1)} %constant.4.clone.refs_2_.refs_3_) | copy-start | bytes 6684676
  2.3 3.5 %copy-start.3 = (f32[4,32,256]{2,1,0:T(8,128)S(1)}, f32[4,32,256]{2,1,0:T(8,128)}, u32[]{:S(2)}) copy-start(f32[4,32,256]{2,1,0:T(8,128)} %constant.5.clone.refs_3_.refs_4_) | copy-start | bytes 393220
  4.3 6.6 %collective-permute-start = (f32[128,1024]{1,0:T(8,128)S(1)}, f32[128,1024]{1,0:T(8,128)S(1)}, u32[]{:S(2)}, u32[]{:S(2)}) collective-permute-start(f32[128,1024]{1,0:T(8,128)S(1)} %get-tuple-element.9.refs_1_), channel_id=1, source_target_pairs={{0,1},{1,0},{2,3},{3,2},{4,5},{5,4},{6,7},{7,6},{8,9},{9,8},{10,11... | collective-permute-start | bytes 1572872 | tf_op jit(solution)/shard_map/ppermute | solution.py:371

commit v4 on v3

--- a/solution.py
+++ b/solution.py
@@ -53,7 +53,7 @@
     phase = 2 * np.pi * (ix[:, None] * ix[None] % n) / n
     wh, wl = split_np(np.kron(np.eye(reps), (np.cos(phase) + np.sin(phase)) / np.sqrt(n)))
     left = np.block([[wh, wh], [wl, np.zeros_like(wl)]]).astype(ml_dtypes.bfloat16)
-    matrices = [*split_np(planes), *split_np(np.swapaxes(planes, 1, 2)), left[None]]
+    matrices = [*split_np(planes), left[None]]
     return np.concatenate(matrices), np.stack(kernels).astype(np.float32)
 
 
@@ -64,6 +64,10 @@
 
 def dot(a, b):
     return jnp.dot(a, b, preferred_element_type=jnp.float32)
+
+
+def dot_t(a, b):
+    return lax.dot_general(a, b, (((1,), (1,)), ((), ())), preferred_element_type=jnp.float32)
 
 
 def take(v, idx):
@@ -172,9 +176,9 @@
             ]
             for s, g in enumerate(butterfly(d)):
                 gh[s, q, :], gl[s, q, :] = split(g)
-    left = w_ref[16]
+    left = w_ref[8]
     for s in range(4):
-        mh, ml, bh, bl = (w_ref[4 * k + s] for k in range(4))
+        mh, ml = w_ref[s], w_ref[4 + s]
         u = dot(gh[s], mh) + dot(gl[s], mh) + dot(gh[s], ml)
         for i in range(tb):
             at = slice(i * rows, (i + 1) * rows)
@@ -184,7 +188,7 @@
             ust[i, :rows, :], ust[i, rows:, :] = split(v.reshape(rows, quarter))
             v = dot(left, ust[i])
             gh[s, at, :], gl[s, at, :] = split(v[:rows] + v[rows:])
-        ps[s] = dot(gh[s], bh) + dot(gl[s], bh) + dot(gh[s], bl)
+        ps[s] = dot_t(gh[s], mh) + dot_t(gl[s], mh) + dot_t(gh[s], ml)
     for i in range(tb):
         acc = [prior[i, :, quarter * s : quarter * (s + 1)] if last else None for s in range(4)]
         for j in range(nj):
@@ -239,48 +243,77 @@
     )(*operands)
 
 
-def spread_body(copies, slab_axes, in_ref, t_ref, o_ref):
-    peers, rows, plane = in_ref.shape
-    each = t_ref.shape[1] // peers
-    own = rows // each
+def planes_body(slab_axes, t_ref, _, o_ref):
+    each = o_ref.shape[0] // t_ref.shape[0]
     first = lax.axis_index(slab_axes) * each
-    t_first = lax.axis_index("core") * own
+    for k in range(each):
+        rows = [t_ref[i, pl.ds(first + k, 1), :] for i in range(t_ref.shape[0])]
+        o_ref[k * t_ref.shape[0] : (k + 1) * t_ref.shape[0], :] = jnp.concatenate(rows, axis=0)
+
+
+def chip_planes(targets, after, peers):
+    owned, n, plane = targets.shape
+    return pl.pallas_call(
+        functools.partial(planes_body, SLABS),
+        out_shape=jax.ShapeDtypeStruct((owned * n // peers, plane), jnp.float32),
+        compiler_params=SMALL_PARAMS,
+    )(targets, after)
+
+
+def total_body(in_ref, mine_ref, other_ref):
+    peers, rows, _ = in_ref.shape
     total = in_ref[0]
     for k in range(1, peers):
         total = total + in_ref[k]
-    half = each // 2
+    own = mine_ref.shape[0] // 2
+    each = rows // own
+    halves = []
     for core in (0, 1):
-        planes = [(q, i) for q in range(half) for i in range(own)]
-        picked = [total[i * each + half * core + q : i * each + half * core + q + 1] for q, i in planes]
-        picked += [t_ref[t_first + i, pl.ds(first + half * core + q, 1), :] for q, i in planes]
-        picked = jnp.concatenate(picked, axis=0)
-        for k in range(copies):
-            o_ref[2 * k + core] = picked
-
-
-def spread(received, targets, copies):
+        planes = [(q, i) for q in range(each // 2) for i in range(own)]
+        picked = [total[i * each + each // 2 * core + q : i * each + each // 2 * core + q + 1] for q, i in planes]
+        halves.append(jnp.concatenate(picked, axis=0))
+    second = lax.axis_index("core") == 1
+    mine_ref[...] = jnp.where(second, halves[1], halves[0])
+    other_ref[...] = jnp.where(second, halves[0], halves[1])
+
+
+def total(received):
     _, rows, plane = received.shape
-    vmem = pl.BlockSpec(memory_space=pltpu.VMEM)
-    return pl.pallas_call(
-        functools.partial(spread_body, copies, SLABS),
-        out_shape=jax.ShapeDtypeStruct((2 * copies, rows, plane), jnp.float32),
-        in_specs=[vmem, vmem],
-        out_specs=vmem,
-        compiler_params=SMALL_PARAMS,
-    )(received, targets)
-
-
-def plane_of(ref, q, part):
-    first = 8 * part + 4 * q
-    return jnp.concatenate([ref[k, first : first + 4, :] for k in range(ref.shape[0])], axis=0)
-
-
-def overlap_body(scale, a_ref, o_ref):
+    half = jax.ShapeDtypeStruct((rows // 2, plane), jnp.float32)
+    return pl.pallas_call(total_body, out_shape=(half, half), compiler_params=SMALL_PARAMS)(received)
+
+
+def pair_body(mine_ref, other_ref, o_ref):
+    half = mine_ref.shape[0] // 2
+    second = lax.axis_index("core") == 1
+    mine, other = mine_ref[...], other_ref[...]
+    low, high = jnp.where(second, other, mine), jnp.where(second, mine, other)
+    both = [v[half * q : half * (q + 1)] for q in (0, 1) for v in (low, high)]
+    both = jnp.concatenate(both, axis=0)
+    for k in range(o_ref.shape[0]):
+        o_ref[k] = both
+
+
+def pair(mine, other, copies):
+    rows, plane = mine.shape
+    return pl.pallas_call(
+        pair_body,
+        out_shape=jax.ShapeDtypeStruct((copies, 2 * rows, plane), jnp.float32),
+        compiler_params=SMALL_PARAMS,
+    )(mine, other)
+
+
+def plane_of(ref, q, owned=8):
+    return ref[:, pl.ds(q * owned, owned), :].reshape(ref.shape[0] * owned, ref.shape[2])
+
+
+def overlap_body(scale, t_ref, a_ref, o_ref):
     total = None
+    first = 2 * lax.axis_index("core")
     for q in (0, 1):
         s = lax.dot_general(
-            plane_of(a_ref, q, 1),
-            plane_of(a_ref, q, 0),
+            plane_of(t_ref, first + q),
+            plane_of(a_ref, q),
             (((1,), (1,)), ((), ())),
             precision=lax.Precision.HIGHEST,
             preferred_element_type=jnp.float32,
@@ -288,18 +321,30 @@
         total = s if total is None else total + s
     total = total * scale
     half = total.shape[0] // 2
-    packed = jnp.concatenate([total[:half], total[half:]], axis=1)
+    o_ref[...] = jnp.concatenate([total[:half], total[half:]], axis=1)
+
+
+def overlap(chip_targets, slab, scale):
+    count = slab.shape[0] * 8
+    return pl.pallas_call(
+        functools.partial(overlap_body, scale),
+        out_shape=jax.ShapeDtypeStruct((count // 2, 2 * count), jnp.float32),
+        compiler_params=SMALL_PARAMS,
+    )(chip_targets, slab)
+
+
+def repeat_body(a_ref, b_ref, o_ref):
+    both = a_ref[...] + b_ref[...]
     for k in range(o_ref.shape[0]):
-        o_ref[k] = packed
-
-
-def overlap(slab, copies, scale):
-    count = slab.shape[0] * 4
-    return pl.pallas_call(
-        functools.partial(overlap_body, scale),
-        out_shape=jax.ShapeDtypeStruct((copies, count // 2, 2 * count), jnp.float32),
-        compiler_params=SMALL_PARAMS,
-    )(slab)
+        o_ref[k] = both
+
+
+def repeated_sum(a, b, copies):
+    return pl.pallas_call(
+        repeat_body,
+        out_shape=jax.ShapeDtypeStruct((copies, *a.shape), jnp.float32),
+        compiler_params=SMALL_PARAMS,
+    )(a, b)
 
 
 def compress_body(owned, s_ref, a_ref, keep_ref, o_ref, inv_ref):
@@ -345,14 +390,14 @@
     for q in (0, 1):
         o_ref[:, q, :] = jnp.dot(
             mine,
-            plane_of(a_ref, q, 0),
+            plane_of(a_ref, q),
             precision=lax.Precision.HIGHEST,
             preferred_element_type=jnp.float32,
         )
 
 
 def compress(summands, slab, keep, owned):
-    count = slab.shape[0] * 4
+    count = slab.shape[0] * owned
     vmem = pl.BlockSpec(memory_space=pltpu.VMEM)
     return pl.pallas_call(
         functools.partial(compress_body, owned),
@@ -367,15 +412,18 @@
 def shards(targets, partners, occupied, retained):
     owned, n, plane = targets.shape
     consts = [jnp.asarray(c) for c in tables(n, partners.shape[2] // n)]
+    peers, groups = lax.axis_size(SLABS), lax.axis_size(TGT)
+    swap = [(0, 1), (1, 0)]
     own_partners, keep = folded_partners(partners, occupied, retained)
-    other_partners = lax.ppermute(own_partners, "core", [(0, 1), (1, 0)])
+    other_partners = lax.ppermute(own_partners, "core", swap)
+    chip_targets = lax.all_gather(chip_planes(targets, keep, peers), TGT, axis=0)
     partial_actions, folded = solve(targets, own_partners, consts)
-    cut = solve(folded, other_partners, consts, partial_actions, lax.axis_size(SLABS))
-    received = lax.all_to_all(cut, SLABS, 0, 0, tiled=True)
-    copies = spread(received, targets, lax.axis_size(TGT))
-    slab = lax.all_to_all(copies, TGT + ("core",), 0, 0, tiled=True)
-    summands = overlap(slab, lax.axis_size(PTR), 1.0 / n**3)
-    summands = lax.all_to_all(summands, PTR, 0, 0, tiled=True)
+    cut = solve(folded, other_partners, consts, partial_actions, peers)
+    mine, other = total(lax.all_to_all(cut, SLABS, 0, 0, tiled=True))
+    slab = lax.all_to_all(pair(mine, lax.ppermute(other, "core", swap), groups), TGT, 0, 0, tiled=True)
+    part = overlap(chip_targets, slab, 1.0 / n**3)
+    summands = repeated_sum(part, lax.ppermute(part, "core", swap), peers)
+    summands = lax.all_to_all(summands, SLABS, 0, 0, tiled=True)
     return compress(summands, slab, keep, owned)
 
 

time: 71.5 us -> 88.8 us (1.24)
  between operations: 1.35 us -> 14.8 us
  blocking collectives: 51.1 us -> 46.1 us
  waiting for transfers between devices: 0.01 us -> 3.81 us
  starting transfers between devices: 1.5 us -> 4.46 us
  local copies, waits for them, and re-layouts: 1.05 us -> 2.28 us
    all_to_all x3, blocking collectives: 51.1 us -> 46.1 us  [the longest x1 21.3 us: shards(): lax.all_to_all(pair(mine, lax.ppermute(other, 'core', swap), groups), TGT...]
    ppermute x1 -> x3, starting transfers between devices: 1.5 us -> 4.45 us  [the longest x1 2.22 us: shards(): lax.ppermute(other, 'core', swap)]
    all_gather x0 -> x1, waiting for transfers between devices: none -> 2.09 us  [shards(): lax.all_gather(chip_planes(targets, keep, peers), TGT, axis=0)]
    ppermute x1 -> x3, waiting for transfers between devices: 0.01 us -> 1.7 us  [the longest x1 0.86 us: shards(): lax.ppermute(other, 'core', swap)]
    unnamed x8 -> x10, local copies, waits for them, and re-layouts: 1.05 us -> 2.28 us
  transfers between devices with their start and end apart: 1 -> 4, of which waited for: 0 -> 3; matrix products, arithmetic and copies ran while one was open for 0% -> 0% of each run, Pallas kernels for 7% -> 12%
where the time goes in v4:
time: 88.8 us; the launch traced here: 88.3 us
  blocking collectives  46.1 us (52%)
  Pallas kernels  16.8 us (19%)
  between operations  14.8 us (17%)
  starting transfers between devices  4.46 us (5%)
  waiting for transfers between devices  3.81 us (4%)
  local copies, waits for them, and re-layouts  2.28 us (3%)
    all_to_all x1, blocking collectives, shards(): lax.all_to_all(pair(mine, lax.ppermute(other, 'core', swap), groups), TGT...  21.3 us
    all_to_all x1, blocking collectives, shards(): mine, other = total(lax.all_to_all(cut, SLABS, 0, 0, tiled=True))  13.5 us
    all_to_all x1, blocking collectives, shards(): summands = lax.all_to_all(summands, SLABS, 0, 0, tiled=True)  11.4 us
    pallas_call x2, Pallas kernels, solve(): pl.pallas_call(functools.partial(solve_body, last, tb, nj, n), out_shape=...  10.4 us
    pallas_call x1, Pallas kernels, compress(): pl.pallas_call(functools.partial(compress_body, owned), out_shape=jax.Sha...  2.95 us
    unnamed x10, local copies, waits for them, and re-layouts  2.28 us
    ppermute x1, starting transfers between devices, shards(): lax.ppermute(other, 'core', swap)  2.22 us
    all_gather x1, waiting for transfers between devices, shards(): lax.all_gather(chip_planes(targets, keep, peers), TGT, axis=0)  2.09 us
  transfers between devices with their start and end apart: 4, of which 3 were waited for; matrix products, arithmetic and copies ran while one was open for 0% of the time, Pallas kernels for 12%

profile of v4, /device:TPU:1, one launch (start us, length us, event | category | flops | bytes accessed | tf_op | source)
XLA Modules:
  0.0 88.3 jit_solution(5415152613251184350)
XLA Ops:
  6.5 0.0 all-gather.3.cloned.1.call-start
  7.8 0.0 copy-start.2
  7.8 1.0 %copy-done.2 = f32[32,32,128]{2,1,0:T(8,128)S(1)} copy-done((f32[32,32,128]{2,1,0:T(8,128)S(1)}, f32[32,32,128]{2,1,0:T(8,128)}, u32[]{:S(2)}) %copy-start.2) | copy-done | bytes 524312
  8.9 0.0 copy-start
  8.9 2.0 %shard_map.64 = (f32[128,1024]{1,0:T(8,128)S(1)}, s32[8,128]{1,0:T(8,128)S(1)}) custom-call(f32[1024,128]{1,0:T(8,128)S(1)} %bitcast.3, s32[1]{0:T(128)S(6)} %copy.7.occ_hbm, s32[1]{0:T(128)S(6)} %copy.8.keep_hbm), custom_call_target="tpu_custom_call" | custom-call | flops 2147483648 | bytes 8388608 | tf_op jit(solution)/shard_map/pallas_call | solution.py:142
  10.8 0.0 copy-start.3
  10.9 0.0 copy-start.4
  10.9 0.0 copy-done
  10.9 0.7 shard_map.65
  11.6 0.0 all-gather.3.cloned.1.call-update
  11.7 1.5 %collective-permute-start = (f32[128,1024]{1,0:T(8,128)S(1)}, f32[128,1024]{1,0:T(8,128)S(1)}, u32[]{:S(2)}, u32[]{:S(2)}) collective-permute-start(f32[128,1024]{1,0:T(8,128)S(1)} %get-tuple-element.12.refs_1_), channel_id=1, source_target_pairs={{0,1},{1,0},{2,3},{3,2},{4,5},{5,4},{6,7},{7,6},{8,9},{9,8},{10,11... | collective-permute-start | bytes 1572872 | tf_op jit(solution)/shard_map/ppermute | solution.py:418
  13.2 0.0 copy-done.3
  13.2 0.0 copy-done.4
  13.2 5.2 %shard_map.66 = (f32[4,32,1024]{2,1,0:T(8,128)S(1)}, f32[4,32,1024]{2,1,0:T(8,128)S(1)}) custom-call(f32[8,32,1024]{2,1,0:T(8,128)S(1)} %copy-done, f32[128,1024]{1,0:T(8,128)S(1)} %get-tuple-element.12.refs_1_, bf16[9,256,256]{2,1,0:T(8,128)(2,1)S(1)} %copy-done.3, f32[4,32,256]{2,1,0:T(8,128)S(1)} %copy-done.4), custom_call_target="tpu_custom_call" | custom-call | flops 1342177280 | bytes 8388608 | tf_op jit(solution)/shard_map/pallas_call | solution.py:228
  18.3 0.0 collective-permute-done.refs_2_
  18.3 5.3 %shard_map.67 = f32[8,16,1024]{2,1,0:T(8,128)S(1)} custom-call(f32[4,32,1024]{2,1,0:T(8,128)S(1)} %get-tuple-element.13.refs_0_, f32[4,32,1024]{2,1,0:T(8,128)S(1)} %get-tuple-element.14.refs_1_, f32[128,1024]{1,0:T(8,128)S(1)} %collective-permute-done.refs_2_, bf16[9,256,256]{2,1,0:T(8,128)(2,1)S(1)} %copy-done.3, f32[4,32,256]{2,1,0:T(8,128)S(1)} %copy-done.4), custom_call_target="tpu_custom_call" | custom-call | flops 1342177280 | bytes 8388608 | tf_op jit(solution)/shard_map/pallas_call | solution.py:228
  23.6 13.5 %all_to_all.15.in_ref = f32[8,16,1024]{2,1,0:T(8,128)S(1)} all-to-all(f32[8,16,1024]{2,1,0:T(8,128)S(1)} %shard_map.67), channel_id=1, replica_groups=mesh['tgt_0'=2,'tgt_1'=4,'ptr_0'=4,'ptr_1'=2,'core'=2] {'ptr_0','ptr_1'}, dimensions={0} | all-to-all | bytes 1048576 | tf_op jit(solution)/shard_map/all_to_all | solution.py:422
  37.2 2.2 %collective-permute-start.1 = (f32[8,1024]{1,0:T(8,128)S(1)}, f32[8,1024]{1,0:T(8,128)S(1)}, u32[]{:S(2)}, u32[]{:S(2)}) collective-permute-start(f32[8,1024]{1,0:T(8,128)S(1)} %get-tuple-element.16), channel_id=1, source_target_pairs={{0,1},{1,0},{2,3},{3,2},{4,5},{5,4},{6,7},{7,6},{8,9},{9,8},{10,11... | collective-permute-start | bytes 98312 | tf_op jit(solution)/shard_map/ppermute | solution.py:423
  39.4 0.9 collective-permute-done.1.other_ref
  40.3 21.3 %all_to_all.16.a_ref = f32[8,16,1024]{2,1,0:T(8,128)S(1)} all-to-all(f32[8,16,1024]{2,1,0:T(8,128)S(1)} %shard_map.69), channel_id=1, replica_groups=mesh['tgt_0'=2,'tgt_1'=4,'ptr_0'=4,'ptr_1'=2,'core'=2] {'tgt_0','tgt_1'}, dimensions={0} | all-to-all | bytes 1048576 | tf_op jit(solution)/shard_map/all_to_all | solution.py:423
  61.5 2.1 %all-gather.3.cloned.1.call-done = f32[256,1024]{1,0:T(8,128)} async-done(((f32[32,1024]{1,0:T(8,128)}), f32[256,1024]{1,0:T(8,128)}) %all-gather.3.cloned.1.call-update) | async-done | bytes 1048592 | tf_op jit(solution)/shard_map/all_gather | solution.py:419
  63.6 0.0 copy-start.1
  63.6 1.2 %copy-done.1 = f32[256,1024]{1,0:T(8,128)S(1)} copy-done((f32[256,1024]{1,0:T(8,128)S(1)}, f32[256,1024]{1,0:T(8,128)}, u32[]{:S(2)}) %copy-start.1) | copy-done | bytes 1048600
  64.9 0.6 shard_map.70.a_ref
  65.5 0.7 collective-permute-start.2
  66.2 0.8 collective-permute-done.2.b_ref
  67.1 11.4 %all_to_all.17.s_ref = f32[8,32,128]{2,1,0:T(8,128)S(1)} all-to-all(f32[8,32,128]{2,1,0:T(8,128)S(1)} %shard_map.71), channel_id=1, replica_groups=mesh['tgt_0'=2,'tgt_1'=4,'ptr_0'=4,'ptr_1'=2,'core'=2] {'ptr_0','ptr_1'}, dimensions={0} | all-to-all | bytes 262144 | tf_op jit(solution)/shard_map/all_to_all | solution.py:426
  78.5 2.9 %shard_map.72 = f32[8,2,1024]{2,1,0:T(2,128)} custom-call(f32[8,32,128]{2,1,0:T(8,128)S(1)} %all_to_all.17.s_ref, f32[8,16,1024]{2,1,0:T(8,128)S(1)} %all_to_all.16.a_ref, s32[8,128]{1,0:T(8,128)S(1)} %get-tuple-element.11._.keep_ref), custom_call_target="tpu_custom_call" | custom-call | tf_op jit(solution)/shard_map/pallas_call | solution.py:402
  (3 shorter events, 0.1 us)
Async XLA Ops:
  6.5 57.1 %all-gather.3.cloned.1.call-start = ((), (), s32[]{:S(2)}) async-start(), calls=%async_computation.3 | async-start | bytes 1179648 | tf_op jit(solution)/shard_map/all_gather | solution.py:419
  7.8 1.0 %copy-start.2 = (f32[32,32,128]{2,1,0:T(8,128)S(1)}, f32[32,32,128]{2,1,0:T(8,128)}, u32[]{:S(2)}) copy-start(f32[32,32,128]{2,1,0:T(8,128)} %param.7) | copy-start | bytes 1572868
  8.9 2.0 %copy-start = (f32[8,32,1024]{2,1,0:T(8,128)S(1)}, f32[8,32,1024]{2,1,0:T(8,128)}, u32[]{:S(2)}) copy-start(f32[8,32,1024]{2,1,0:T(8,128)} %refs_0_.1) | copy-start | bytes 3145732
  10.8 2.3 %copy-start.3 = (bf16[9,256,256]{2,1,0:T(8,128)(2,1)S(1)}, bf16[9,256,256]{2,1,0:T(8,128)(2,1)}, u32[]{:S(2)}) copy-start(bf16[9,256,256]{2,1,0:T(8,128)(2,1)} %constant.4.clone.refs_2_.refs_3_) | copy-start | bytes 3538948
  10.9 2.3 %copy-start.4 = (f32[4,32,256]{2,1,0:T(8,128)S(1)}, f32[4,32,256]{2,1,0:T(8,128)}, u32[]{:S(2)}) copy-start(f32[4,32,256]{2,1,0:T(8,128)} %constant.5.clone.refs_3_.refs_4_) | copy-start | bytes 393220
  11.7 6.7 %collective-permute-start = (f32[128,1024]{1,0:T(8,128)S(1)}, f32[128,1024]{1,0:T(8,128)S(1)}, u32[]{:S(2)}, u32[]{:S(2)}) collective-permute-start(f32[128,1024]{1,0:T(8,128)S(1)} %get-tuple-element.12.refs_1_), channel_id=1, source_target_pairs={{0,1},{1,0},{2,3},{3,2},{4,5},{5,4},{6,7},{7,6},{8,9},{9,8},{10,11... | collective-permute-start | bytes 1572872 | tf_op jit(solution)/shard_map/ppermute | solution.py:418
  37.2 3.1 %collective-permute-start.1 = (f32[8,1024]{1,0:T(8,128)S(1)}, f32[8,1024]{1,0:T(8,128)S(1)}, u32[]{:S(2)}, u32[]{:S(2)}) collective-permute-start(f32[8,1024]{1,0:T(8,128)S(1)} %get-tuple-element.16), channel_id=1, source_target_pairs={{0,1},{1,0},{2,3},{3,2},{4,5},{5,4},{6,7},{7,6},{8,9},{9,8},{10,11... | collective-permute-start | bytes 98312 | tf_op jit(solution)/shard_map/ppermute | solution.py:423
  63.6 1.2 %copy-start.1 = (f32[256,1024]{1,0:T(8,128)S(1)}, f32[256,1024]{1,0:T(8,128)}, u32[]{:S(2)}) copy-start(f32[256,1024]{1,0:T(8,128)} %all-gather.3.cloned.1.call-done) | copy-start | bytes 3145732
  65.5 1.6 %collective-permute-start.2 = (f32[32,128]{1,0:T(8,128)S(1)}, f32[32,128]{1,0:T(8,128)S(1)}, u32[]{:S(2)}, u32[]{:S(2)}) collective-permute-start(f32[32,128]{1,0:T(8,128)S(1)} %shard_map.70.a_ref), channel_id=1, source_target_pairs={{0,1},{1,0},{2,3},{3,2},{4,5},{5,4},{6,7},{7,6},{8,9},{9,8},{10,11... | collective-permute-start | bytes 49160 | tf_op jit(solution)/shard_map/ppermute | solution.py:425
Sparse Core Ops, SparseCore 0:
  11.8 51.8 all-gather.2

commit v5 on v3

--- a/solution.py
+++ b/solution.py
@@ -12,7 +12,6 @@
 
 TGT = ("tgt_0", "tgt_1")
 PTR = ("ptr_0", "ptr_1", "core")
-SLABS = ("ptr_0", "ptr_1")
 LANES = 128
 SOLVE_PARAMS = pltpu.CompilerParams(vmem_limit_bytes=24 << 20)
 SMALL_PARAMS = pltpu.CompilerParams(vmem_limit_bytes=16 << 20)
@@ -53,7 +52,7 @@
     phase = 2 * np.pi * (ix[:, None] * ix[None] % n) / n
     wh, wl = split_np(np.kron(np.eye(reps), (np.cos(phase) + np.sin(phase)) / np.sqrt(n)))
     left = np.block([[wh, wh], [wl, np.zeros_like(wl)]]).astype(ml_dtypes.bfloat16)
-    matrices = [*split_np(planes), *split_np(np.swapaxes(planes, 1, 2)), left[None]]
+    matrices = [*split_np(planes), left[None]]
     return np.concatenate(matrices), np.stack(kernels).astype(np.float32)
 
 
@@ -64,6 +63,10 @@
 
 def dot(a, b):
     return jnp.dot(a, b, preferred_element_type=jnp.float32)
+
+
+def dot_t(a, b):
+    return lax.dot_general(a, b, (((1,), (1,)), ((), ())), preferred_element_type=jnp.float32)
 
 
 def take(v, idx):
@@ -154,7 +157,7 @@
         tf, prior, pf, w_ref, k_ref, o_ref = refs[:6]
     else:
         t_ref, pf, w_ref, k_ref, o_ref, tf = refs[:6]
-    gh, gl, ust, ps = refs[6:]
+    gh, gl, ust, ps = refs[-4:]
     rows, quarter = nj * n, n * n // 4
     if not last:
         first = lax.axis_index("core") * tb
@@ -172,9 +175,9 @@
             ]
             for s, g in enumerate(butterfly(d)):
                 gh[s, q, :], gl[s, q, :] = split(g)
-    left = w_ref[16]
+    left = w_ref[8]
     for s in range(4):
-        mh, ml, bh, bl = (w_ref[4 * k + s] for k in range(4))
+        mh, ml = w_ref[s], w_ref[4 + s]
         u = dot(gh[s], mh) + dot(gl[s], mh) + dot(gh[s], ml)
         for i in range(tb):
             at = slice(i * rows, (i + 1) * rows)
@@ -184,7 +187,7 @@
             ust[i, :rows, :], ust[i, rows:, :] = split(v.reshape(rows, quarter))
             v = dot(left, ust[i])
             gh[s, at, :], gl[s, at, :] = split(v[:rows] + v[rows:])
-        ps[s] = dot(gh[s], bh) + dot(gl[s], bh) + dot(gh[s], bl)
+        ps[s] = dot_t(gh[s], mh) + dot_t(gl[s], mh) + dot_t(gh[s], ml)
     for i in range(tb):
         acc = [prior[i, :, quarter * s : quarter * (s + 1)] if last else None for s in range(4)]
         for j in range(nj):
@@ -207,7 +210,7 @@
                 o_ref[i, :, quarter * s : quarter * (s + 1)] = acc[s]
 
 
-def solve(targets, partners, consts, prior=None, peers=8):
+def solve(targets, partners, consts, prior=None, peers=16):
     last = prior is not None
     n = targets.shape[1]
     nj = partners.shape[0] // n
@@ -239,76 +242,75 @@
     )(*operands)
 
 
-def spread_body(copies, slab_axes, in_ref, t_ref, o_ref):
-    peers, rows, plane = in_ref.shape
-    each = t_ref.shape[1] // peers
-    own = rows // each
-    first = lax.axis_index(slab_axes) * each
-    t_first = lax.axis_index("core") * own
-    total = in_ref[0]
-    for k in range(1, peers):
-        total = total + in_ref[k]
-    half = each // 2
+def spread_body(in_ref, o_ref):
+    peers, rows, _ = in_ref.shape
+    halves = []
     for core in (0, 1):
-        planes = [(q, i) for q in range(half) for i in range(own)]
-        picked = [total[i * each + half * core + q : i * each + half * core + q + 1] for q, i in planes]
-        picked += [t_ref[t_first + i, pl.ds(first + half * core + q, 1), :] for q, i in planes]
-        picked = jnp.concatenate(picked, axis=0)
-        for k in range(copies):
-            o_ref[2 * k + core] = picked
-
-
-def spread(received, targets, copies):
+        total = in_ref[core]
+        for k in range(core + 2, peers, 2):
+            total = total + in_ref[k]
+        halves.append(total)
+    order = [v[2 * i + q : 2 * i + q + 1] for q in (0, 1) for v in halves for i in range(rows // 2)]
+    slab = jnp.concatenate(order, axis=0)
+    for k in range(o_ref.shape[0]):
+        o_ref[k] = slab
+
+
+def spread(received, copies):
     _, rows, plane = received.shape
-    vmem = pl.BlockSpec(memory_space=pltpu.VMEM)
-    return pl.pallas_call(
-        functools.partial(spread_body, copies, SLABS),
-        out_shape=jax.ShapeDtypeStruct((2 * copies, rows, plane), jnp.float32),
-        in_specs=[vmem, vmem],
-        out_specs=vmem,
+    return pl.pallas_call(
+        spread_body,
+        out_shape=jax.ShapeDtypeStruct((copies, 2 * rows, plane), jnp.float32),
         compiler_params=SMALL_PARAMS,
-    )(received, targets)
-
-
-def plane_of(ref, q, part):
-    first = 8 * part + 4 * q
-    return jnp.concatenate([ref[k, first : first + 4, :] for k in range(ref.shape[0])], axis=0)
-
-
-def overlap_body(scale, a_ref, o_ref):
+    )(received)
+
+
+def plane_of(ref, q):
+    half = ref.shape[1] // 2
+    return ref[:, q * half : (q + 1) * half, :].reshape(ref.shape[0] * half, ref.shape[2])
+
+
+def overlap_body(scale, t_ref, a_ref, o_ref):
+    owned = t_ref.shape[0]
+    first = 2 * lax.axis_index(PTR)
     total = None
     for q in (0, 1):
+        t = [t_ref[i, pl.ds(first + q, 1), :] for i in range(owned)]
         s = lax.dot_general(
-            plane_of(a_ref, q, 1),
-            plane_of(a_ref, q, 0),
+            jnp.concatenate(t, axis=0),
+            plane_of(a_ref, q),
             (((1,), (1,)), ((), ())),
             precision=lax.Precision.HIGHEST,
             preferred_element_type=jnp.float32,
         )
         total = s if total is None else total + s
     total = total * scale
-    half = total.shape[0] // 2
-    packed = jnp.concatenate([total[:half], total[half:]], axis=1)
+    packed = jnp.concatenate([total[: owned // 2], total[owned // 2 :]], axis=1)
     for k in range(o_ref.shape[0]):
         o_ref[k] = packed
 
 
-def overlap(slab, copies, scale):
-    count = slab.shape[0] * 4
+def overlap(targets, slab, copies, scale):
+    owned = targets.shape[0]
+    count = slab.shape[0] * owned
     return pl.pallas_call(
         functools.partial(overlap_body, scale),
-        out_shape=jax.ShapeDtypeStruct((copies, count // 2, 2 * count), jnp.float32),
+        out_shape=jax.ShapeDtypeStruct((copies, owned // 2, 2 * count), jnp.float32),
         compiler_params=SMALL_PARAMS,
-    )(slab)
+    )(targets, slab)
 
 
 def compress_body(owned, s_ref, a_ref, keep_ref, o_ref, inv_ref):
-    total = s_ref[0]
-    for k in range(1, s_ref.shape[0]):
-        total = total + s_ref[k]
-    half = total.shape[0]
-    count = 2 * half
-    square = jnp.concatenate([total[:, :count], total[:, count:]], axis=0)
+    groups = lax.axis_size(TGT)
+    slabs = s_ref.shape[0] // groups
+    count = groups * owned
+    rows = []
+    for t in range(groups):
+        total = s_ref[t * slabs]
+        for k in range(1, slabs):
+            total = total + s_ref[t * slabs + k]
+        rows += [total[:, :count], total[:, count:]]
+    square = jnp.concatenate(rows, axis=0)
     square = 0.5 * (square + square.T)
     row = lax.broadcasted_iota(jnp.int32, (count, count), 0)
     col = lax.broadcasted_iota(jnp.int32, (count, count), 1)
@@ -345,14 +347,14 @@
     for q in (0, 1):
         o_ref[:, q, :] = jnp.dot(
             mine,
-            plane_of(a_ref, q, 0),
+            plane_of(a_ref, q),
             precision=lax.Precision.HIGHEST,
             preferred_element_type=jnp.float32,
         )
 
 
 def compress(summands, slab, keep, owned):
-    count = slab.shape[0] * 4
+    count = slab.shape[0] * owned
     vmem = pl.BlockSpec(memory_space=pltpu.VMEM)
     return pl.pallas_call(
         functools.partial(compress_body, owned),
@@ -367,15 +369,16 @@
 def shards(targets, partners, occupied, retained):
     owned, n, plane = targets.shape
     consts = [jnp.asarray(c) for c in tables(n, partners.shape[2] // n)]
+    peers, groups = lax.axis_size(PTR), lax.axis_size(TGT)
+    swap = [(0, 1), (1, 0)]
     own_partners, keep = folded_partners(partners, occupied, retained)
-    other_partners = lax.ppermute(own_partners, "core", [(0, 1), (1, 0)])
+    other_partners = lax.ppermute(own_partners, "core", swap)
     partial_actions, folded = solve(targets, own_partners, consts)
-    cut = solve(folded, other_partners, consts, partial_actions, lax.axis_size(SLABS))
-    received = lax.all_to_all(cut, SLABS, 0, 0, tiled=True)
-    copies = spread(received, targets, lax.axis_size(TGT))
-    slab = lax.all_to_all(copies, TGT + ("core",), 0, 0, tiled=True)
-    summands = overlap(slab, lax.axis_size(PTR), 1.0 / n**3)
-    summands = lax.all_to_all(summands, PTR, 0, 0, tiled=True)
+    cut = solve(folded, other_partners, consts, partial_actions, peers)
+    copies = spread(lax.all_to_all(cut, PTR, 0, 0, tiled=True), groups)
+    slab = lax.all_to_all(copies, TGT, 0, 0, tiled=True)
+    summands = overlap(targets, slab, lax.axis_size(TGT + PTR), 1.0 / n**3)
+    summands = lax.all_to_all(summands, TGT + PTR, 0, 0, tiled=True)
     return compress(summands, slab, keep, owned)
 
 

time: 71.5 us -> 69.3 us (0.969)
  blocking collectives: 51.1 us -> 49 us
    all_to_all x3, blocking collectives: 51.1 us -> 49 us  [the longest x1 17.9 us: shards(): summands = lax.all_to_all(summands, TGT + PTR, 0, 0, tiled=True)]
where the time goes in v5:
time: 69.3 us; the launch traced here: 69 us
  blocking collectives  49 us (71%)
  Pallas kernels  16.1 us (23%)
  starting transfers between devices  1.5 us (2%)
  between operations  1.35 us (2%)
  local copies, waits for them, and re-layouts  1.05 us (2%)
    all_to_all x1, blocking collectives, shards(): summands = lax.all_to_all(summands, TGT + PTR, 0, 0, tiled=True)  17.9 us
    all_to_all x1, blocking collectives, shards(): slab = lax.all_to_all(copies, TGT, 0, 0, tiled=True)  16.2 us
    all_to_all x1, blocking collectives, shards(): copies = spread(lax.all_to_all(cut, PTR, 0, 0, tiled=True), groups)  14.9 us
    pallas_call x2, Pallas kernels, solve(): pl.pallas_call(functools.partial(solve_body, last, tb, nj, n), out_shape=...  10.5 us
    pallas_call x1, Pallas kernels, compress(): pl.pallas_call(functools.partial(compress_body, owned), out_shape=jax.Sha...  2.97 us
    pallas_call x1, Pallas kernels, folded_partners(): pl.pallas_call(functools.partial(fold_body, nj, n), out_shape=(jax.ShapeD...  1.96 us
    ppermute x1, starting transfers between devices, shards(): other_partners = lax.ppermute(own_partners, 'core', swap)  1.5 us
  transfers between devices with their start and end apart: 1, of which 0 were waited for; matrix products, arithmetic and copies ran while one was open for 0% of the time, Pallas kernels for 7%

profile of v5, /device:TPU:1, one launch (start us, length us, event | category | flops | bytes accessed | tf_op | source)
XLA Modules:
  0.0 69.0 jit_solution(8498372582835659628)
XLA Ops:
  1.3 0.0 copy-start.1
  1.3 1.0 %copy-done.1 = f32[32,32,128]{2,1,0:T(8,128)S(1)} copy-done((f32[32,32,128]{2,1,0:T(8,128)S(1)}, f32[32,32,128]{2,1,0:T(8,128)}, u32[]{:S(2)}) %copy-start.1) | copy-done | bytes 524312
  2.3 0.0 copy-start
  2.3 0.0 copy-start.2
  2.3 0.0 copy-start.3
  2.3 2.0 %shard_map.64 = (f32[128,1024]{1,0:T(8,128)S(1)}, s32[8,128]{1,0:T(8,128)S(1)}) custom-call(f32[1024,128]{1,0:T(8,128)S(1)} %bitcast.1, s32[1]{0:T(128)S(6)} %copy.7.occ_hbm, s32[1]{0:T(128)S(6)} %copy.8.keep_hbm), custom_call_target="tpu_custom_call" | custom-call | flops 2147483648 | bytes 8388608 | tf_op jit(solution)/shard_map/pallas_call | solution.py:141
  4.3 1.5 %collective-permute-start = (f32[128,1024]{1,0:T(8,128)S(1)}, f32[128,1024]{1,0:T(8,128)S(1)}, u32[]{:S(2)}, u32[]{:S(2)}) collective-permute-start(f32[128,1024]{1,0:T(8,128)S(1)} %get-tuple-element.9.refs_1_), channel_id=1, source_target_pairs={{0,1},{1,0},{2,3},{3,2},{4,5},{5,4},{6,7},{7,6},{8,9},{9,8},{10,11... | collective-permute-start | bytes 1572872 | tf_op jit(solution)/shard_map/ppermute | solution.py:375
  5.8 0.0 copy-done
  5.8 0.0 copy-done.2
  5.8 0.0 copy-done.3
  5.8 5.1 %shard_map.65 = (f32[4,32,1024]{2,1,0:T(8,128)S(1)}, f32[4,32,1024]{2,1,0:T(8,128)S(1)}) custom-call(f32[8,32,1024]{2,1,0:T(8,128)S(1)} %copy-done, f32[128,1024]{1,0:T(8,128)S(1)} %get-tuple-element.9.refs_1_, bf16[9,256,256]{2,1,0:T(8,128)(2,1)S(1)} %copy-done.2, f32[4,32,256]{2,1,0:T(8,128)S(1)} %copy-done.3), custom_call_target="tpu_custom_call" | custom-call | flops 1342177280 | bytes 8388608 | tf_op jit(solution)/shard_map/pallas_call | solution.py:227
  10.9 0.0 collective-permute-done.refs_2_
  10.9 5.4 %shard_map.66 = f32[16,8,1024]{2,1,0:T(8,128)S(1)} custom-call(f32[4,32,1024]{2,1,0:T(8,128)S(1)} %get-tuple-element.10.refs_0_, f32[4,32,1024]{2,1,0:T(8,128)S(1)} %get-tuple-element.11.refs_1_, f32[128,1024]{1,0:T(8,128)S(1)} %collective-permute-done.refs_2_, bf16[9,256,256]{2,1,0:T(8,128)(2,1)S(1)} %copy-done.2, f32[4,32,256]{2,1,0:T(8,128)S(1)} %copy-done.3), custom_call_target="tpu_custom_call" | custom-call | flops 1342177280 | bytes 8388608 | tf_op jit(solution)/shard_map/pallas_call | solution.py:227
  16.3 14.9 %all_to_all.15.in_ref = f32[16,8,1024]{2,1,0:T(8,128)S(1)} all-to-all(f32[16,8,1024]{2,1,0:T(8,128)S(1)} %shard_map.66), channel_id=1, replica_groups=mesh['tgt_0'=2,'tgt_1'=4,'ptr_0'=4,'ptr_1'=2,'core'=2] {'ptr_0','ptr_1',..., dimensions={0} | all-to-all | bytes 1048576 | tf_op jit(solution)/shard_map/all_to_all | solution.py:378
  31.3 0.1 shard_map.67
  31.3 16.2 %all_to_all.16.a_ref = f32[8,16,1024]{2,1,0:T(8,128)S(1)} all-to-all(f32[8,16,1024]{2,1,0:T(8,128)S(1)} %shard_map.67), channel_id=1, replica_groups=mesh['tgt_0'=2,'tgt_1'=4,'ptr_0'=4,'ptr_1'=2,'core'=2] {'tgt_0','tgt_1'}, dimensions={0} | all-to-all | bytes 1048576 | tf_op jit(solution)/shard_map/all_to_all | solution.py:379
  47.5 0.7 shard_map.68
  48.2 17.9 %all_to_all.17.s_ref = f32[128,4,128]{2,1,0:T(4,128)S(1)} all-to-all(f32[128,4,128]{2,1,0:T(4,128)S(1)} %shard_map.68), channel_id=1, replica_groups=mesh['tgt_0'=2,'tgt_1'=4,'ptr_0'=4,'ptr_1'=2,'core'=2] {'tgt_0','tgt_1',..., dimensions={0} | all-to-all | bytes 524288 | tf_op jit(solution)/shard_map/all_to_all | solution.py:381
  66.1 3.0 %shard_map.69 = f32[8,2,1024]{2,1,0:T(2,128)} custom-call(f32[128,4,128]{2,1,0:T(4,128)S(1)} %all_to_all.17.s_ref, f32[8,16,1024]{2,1,0:T(8,128)S(1)} %all_to_all.16.a_ref, s32[8,128]{1,0:T(8,128)S(1)} %get-tuple-element.12.keep_ref), custom_call_target="tpu_custom_call" | custom-call | tf_op jit(solution)/shard_map/pallas_call | solution.py:359
Async XLA Ops:
  1.3 1.0 %copy-start.1 = (f32[32,32,128]{2,1,0:T(8,128)S(1)}, f32[32,32,128]{2,1,0:T(8,128)}, u32[]{:S(2)}) copy-start(f32[32,32,128]{2,1,0:T(8,128)} %param.7) | copy-start | bytes 1572868
  2.3 3.5 %copy-start = (f32[8,32,1024]{2,1,0:T(8,128)S(1)}, f32[8,32,1024]{2,1,0:T(8,128)}, u32[]{:S(2)}) copy-start(f32[8,32,1024]{2,1,0:T(8,128)} %t_ref.1) | copy-start | bytes 3145732
  2.3 3.5 %copy-start.2 = (bf16[9,256,256]{2,1,0:T(8,128)(2,1)S(1)}, bf16[9,256,256]{2,1,0:T(8,128)(2,1)}, u32[]{:S(2)}) copy-start(bf16[9,256,256]{2,1,0:T(8,128)(2,1)} %constant.4.clone.refs_2_.refs_3_) | copy-start | bytes 3538948
  2.3 3.5 %copy-start.3 = (f32[4,32,256]{2,1,0:T(8,128)S(1)}, f32[4,32,256]{2,1,0:T(8,128)}, u32[]{:S(2)}) copy-start(f32[4,32,256]{2,1,0:T(8,128)} %constant.5.clone.refs_3_.refs_4_) | copy-start | bytes 393220
  4.3 6.6 %collective-permute-start = (f32[128,1024]{1,0:T(8,128)S(1)}, f32[128,1024]{1,0:T(8,128)S(1)}, u32[]{:S(2)}, u32[]{:S(2)}) collective-permute-start(f32[128,1024]{1,0:T(8,128)S(1)} %get-tuple-element.9.refs_1_), channel_id=1, source_target_pairs={{0,1},{1,0},{2,3},{3,2},{4,5},{5,4},{6,7},{7,6},{8,9},{9,8},{10,11... | collective-permute-start | bytes 1572872 | tf_op jit(solution)/shard_map/ppermute | solution.py:375

commit v6 on v5

--- a/solution.py
+++ b/solution.py
@@ -35,25 +35,23 @@
     return (even, odd), (even_k, odd_k)
 
 
-def tables(n, reps):
+def tables(n):
     bases, freqs = half_bases(n)
+    half = n // 2
     planes, kernels = [], []
-    ix = np.arange(n)
     wave = lambda k: (k * (2 * np.pi / n)) ** 2
-    wx = wave(np.where(ix < n // 2, ix, ix - n))
+    ix = np.arange(half)
+    weight = np.where(ix == 0, 1.0, 2.0) / half / 8
     for sy in (0, 1):
         for sz in (0, 1):
             m = np.einsum("ky,lz->yzkl", bases[sy], bases[sz])
-            planes.append(m.reshape(n * n // 4, n * n // 4))
-            total = wx[:, None, None] + wave(freqs[sy])[:, None] + wave(freqs[sz])[None]
-            g = np.where(total > 0, 4 * np.pi / np.where(total > 0, total, 1.0), 0.0)
-            kernels.append(g.reshape(n, -1) / 4)
-    planes = np.stack(planes)
-    phase = 2 * np.pi * (ix[:, None] * ix[None] % n) / n
-    wh, wl = split_np(np.kron(np.eye(reps), (np.cos(phase) + np.sin(phase)) / np.sqrt(n)))
-    left = np.block([[wh, wh], [wl, np.zeros_like(wl)]]).astype(ml_dtypes.bfloat16)
-    matrices = [*split_np(planes), left[None]]
-    return np.concatenate(matrices), np.stack(kernels).astype(np.float32)
+            planes.append(m.reshape(half * half, half * half))
+            for wx in (wave(ix), wave(half - ix)):
+                total = wx[:, None, None] + wave(freqs[sy])[:, None] + wave(freqs[sz])[None]
+                g = np.where(total > 0, 4 * np.pi / np.where(total > 0, total, 1.0), 0.0)
+                kernels.append((g * weight[:, None, None]).reshape(half, -1, LANES))
+    kernels = np.stack(kernels).reshape(4, n, -1, LANES).transpose(0, 2, 1, 3)
+    return np.concatenate(split_np(np.stack(planes))), kernels.reshape(-1, n, LANES).astype(np.float32)
 
 
 def split(v):
@@ -101,143 +99,216 @@
     return out
 
 
+def cosines(v):
+    n = len(v)
+    if n == 1:
+        return v
+    half = n // 2
+    even = cosines([v[i] + v[n - 1 - i] for i in range(half)])
+    if n == 2:
+        return [even[0], (v[0] - v[1]) * np.float32(np.sqrt(0.5))]
+    scale = [np.float32(2 * np.cos(np.pi * (2 * i + 1) / (2 * n))) for i in range(half)]
+    odd = cosines([(v[i] - v[n - 1 - i]) * scale[i] for i in range(half)])
+    out = [even[0], odd[0] * np.float32(0.5)]
+    for k in range(1, half):
+        out += [even[k], odd[k] - out[-1]]
+    return out
+
+
+def cosines_t(x):
+    n = len(x)
+    if n == 1:
+        return x
+    half = n // 2
+    even = cosines_t(x[0::2])
+    if n == 2:
+        b = [x[1] * np.float32(np.sqrt(0.5))]
+    else:
+        z = [x[n - 1]]
+        for k in range(half - 2, -1, -1):
+            z.insert(0, x[2 * k + 1] - z[0])
+        z[0] = z[0] * np.float32(0.5)
+        scale = [np.float32(2 * np.cos(np.pi * (2 * i + 1) / (2 * n))) for i in range(half)]
+        b = [c * w for c, w in zip(cosines_t(z), scale)]
+    return [even[i] + b[i] for i in range(half)] + [even[i] - b[i] for i in range(half - 1, -1, -1)]
+
+
+def along_x(v, table):
+    half = len(v) // 2
+    even = [v[i] + v[-1 - i] for i in range(half)]
+    odd = [v[-1 - i] - v[i] if i % 2 else v[i] - v[-1 - i] for i in range(half)]
+    even = cosines_t([c * table(k) for k, c in enumerate(cosines(even))])
+    odd = cosines_t([c * table(half + k) for k, c in enumerate(cosines(odd))])
+    low = [e - o if i % 2 else e + o for i, (e, o) in enumerate(zip(even, odd))]
+    high = [e + o if i % 2 else e - o for i, (e, o) in enumerate(zip(even, odd))]
+    return low + high[::-1]
+
+
 def butterfly(d):
     a, b, c, e = d[0] + d[1], d[0] - d[1], d[2] + d[3], d[2] - d[3]
     return a + c, b + e, a - c, b - e
 
 
-def fold_body(nj, n, p_ref, occ_hbm, keep_hbm, o_ref, keep_ref, scalars, sems):
-    copies = [
-        pltpu.make_async_copy(src, scalars.at[i], sems.at[i]) for i, src in enumerate((occ_hbm, keep_hbm))
-    ]
-    for copy in copies:
-        copy.start()
-    for copy in copies:
-        copy.wait()
-    keep_ref[...] = jnp.full(keep_ref.shape, scalars[1, 0], jnp.int32)
-    occ = jnp.full((n, LANES), scalars[0, 0], jnp.int32).astype(jnp.float32)
+def fold_body(nj, n, p_ref, occ_ref, rank_ref, o_ref, keep_ref):
+    keep_ref[...] = jnp.full(keep_ref.shape, rank_ref[0], jnp.int32)
+    occ = jnp.full((n, LANES), occ_ref[0], jnp.int32).astype(jnp.float32)
     root = jnp.sqrt(0.25 + 0.75 * occ)
-    quarter = n * n // 4
     lane = lax.broadcasted_iota(jnp.int32, (n, LANES), 1)
+    part = lane // n
+    tiles = [[] for _ in range(nj)]
+    for t in range(n // nj):
+        src = [p_ref[pl.ds(nj * t + y, n, stride=n), :] * root for y in range(nj)]
+        for j in range(nj):
+            acc = src[j]
+            for y in range(nj):
+                if y != j:
+                    acc = jnp.where(part == y, pltpu.roll(src[y], ((y - j) % nj) * n, 1), acc)
+            tiles[j].append(acc)
     for j in range(nj):
-        tiles = []
-        for t in range(8):
-            acc = None
-            for y in range(4):
-                src = p_ref[pl.ds(4 * t + y, n, stride=n), :]
-                if y != j:
-                    src = pltpu.roll(src, ((y - j) % 4) * n, 1)
-                acc = src if acc is None else jnp.where(lane // n == y, src, acc)
-            tiles.append(acc * root)
-        for (s, h), v in fold(tiles, n).items():
-            o_ref[j * n : (j + 1) * n, s * quarter + h * LANES : s * quarter + (h + 1) * LANES] = v
+        for (s, h), v in fold(tiles[j], n).items():
+            o_ref[2 * s + h, j * n : (j + 1) * n, :] = v
 
 
 def folded_partners(partners, occupied, retained):
     n = partners.shape[0]
     nj = partners.shape[2] // n
     vmem = pl.BlockSpec(memory_space=pltpu.VMEM)
-    hbm = pl.BlockSpec(memory_space=pltpu.HBM)
+    smem = pl.BlockSpec(memory_space=pltpu.SMEM)
     return pl.pallas_call(
         functools.partial(fold_body, nj, n),
         out_shape=(
-            jax.ShapeDtypeStruct((nj * n, n * n), jnp.float32),
+            jax.ShapeDtypeStruct((n * n // LANES, nj * n, LANES), jnp.float32),
             jax.ShapeDtypeStruct((8, LANES), jnp.int32),
         ),
-        in_specs=[vmem, hbm, hbm],
+        in_specs=[vmem, smem, smem],
         out_specs=(vmem, vmem),
-        scratch_shapes=[pltpu.SMEM((2, 1), jnp.int32), pltpu.SemaphoreType.DMA((2,))],
         compiler_params=SMALL_PARAMS,
         cost_estimate=pl.CostEstimate(flops=2 << 30, bytes_accessed=8 << 20, transcendentals=0),
     )(partners.reshape(n * n, -1), occupied, retained)
 
 
-def solve_body(last, tb, nj, n, *refs):
+def solve_body(last, tb, n, *refs):
     if last:
-        tf, prior, pf, w_ref, k_ref, o_ref = refs[:6]
+        t8, prior, p_ref, w_ref, k_ref, o_ref, p8, gh, gl, ps = refs
     else:
-        t_ref, pf, w_ref, k_ref, o_ref, tf = refs[:6]
-    gh, gl, ust, ps = refs[-4:]
-    rows, quarter = nj * n, n * n // 4
+        t_ref, p_ref, w_ref, k_ref, o_ref, t8, p8, gh, gl, ps, rows_ref = refs
+    quarter = n * n // 4
+    tiles = n * n // LANES
+    pairs = p8.shape[0]
+    sub = lax.broadcasted_iota(jnp.int32, (8, LANES), 0)
+    upper, second, late = sub < tb, sub % 2 == 1, sub % tb >= 2
+    at = lambda k: slice(LANES * k, LANES * (k + 1))
+    cls = lambda s: slice(quarter * s, quarter * (s + 1))
     if not last:
         first = lax.axis_index("core") * tb
         for i in range(tb):
-            tiles = [t_ref[first + i, :, LANES * t : LANES * (t + 1)] for t in range(8)]
-            for (s, h), v in fold(tiles, n).items():
-                tf[i, :, s * quarter + h * LANES : s * quarter + (h + 1) * LANES] = v
-    for i in range(tb):
-        for j in range(nj):
-            r = slice(j * n, (j + 1) * n)
-            q = slice(i * rows + j * n, i * rows + (j + 1) * n)
-            d = [
-                tf[i, :, quarter * s : quarter * (s + 1)] * pf[r, quarter * s : quarter * (s + 1)]
-                for s in range(4)
-            ]
-            for s, g in enumerate(butterfly(d)):
-                gh[s, q, :], gl[s, q, :] = split(g)
-    left = w_ref[8]
-    for s in range(4):
-        mh, ml = w_ref[s], w_ref[4 + s]
-        u = dot(gh[s], mh) + dot(gl[s], mh) + dot(gh[s], ml)
-        for i in range(tb):
-            at = slice(i * rows, (i + 1) * rows)
-            ust[i, :rows, :], ust[i, rows:, :] = split(u[at])
-            v = dot(left, ust[i])
-            v = (v[:rows] + v[rows:]).reshape(nj, n, quarter) * k_ref[s][None]
-            ust[i, :rows, :], ust[i, rows:, :] = split(v.reshape(rows, quarter))
-            v = dot(left, ust[i])
-            gh[s, at, :], gl[s, at, :] = split(v[:rows] + v[rows:])
-        ps[s] = dot_t(gh[s], mh) + dot_t(gl[s], mh) + dot_t(gh[s], ml)
-    for i in range(tb):
-        acc = [prior[i, :, quarter * s : quarter * (s + 1)] if last else None for s in range(4)]
-        for j in range(nj):
-            r = slice(j * n, (j + 1) * n)
-            q = slice(i * rows + j * n, i * rows + (j + 1) * n)
+            folded = fold([t_ref[first + i, :, at(k)] for k in range(tiles)], n)
+            for (s, h), v in folded.items():
+                rows_ref[2 * s + h, i * n : (i + 1) * n, :] = v
+        for k in range(tiles):
+            for x in range(n):
+                rows = [rows_ref[k, pl.ds(i * n + x, 8, stride=0), :] for i in range(tb)]
+                low, high = jnp.where(second, rows[1], rows[0]), jnp.where(second, rows[3], rows[2])
+                t8[x, :, at(k)] = jnp.where(late, high, low)
+    for g in range(pairs):
+        for k in range(tiles):
+            for x in range(n):
+                a, b = (
+                    p_ref[k, pl.ds(j * n + x, 8, stride=0), :] for j in (2 * g, 2 * g + 1)
+                )
+                p8[g, x, :, at(k)] = jnp.where(upper, a, b)
+    for g in range(pairs):
+        for x in range(0, n, 2):
+            both = []
+            for y in (x, x + 1):
+                both.append(butterfly([t8[y, :, cls(s)] * p8[g, y, :, cls(s)] for s in range(4)]))
+            q = slice((g * n + x) * 8, (g * n + x + 2) * 8)
+            for s in range(4):
+                gh[s, q, :], gl[s, q, :] = split(jnp.concatenate([both[0][s], both[1][s]], axis=0))
+
+    def forward(s):
+        ps[s] = dot(gh[s], w_ref[s]) + dot(gl[s], w_ref[s]) + dot(gh[s], w_ref[4 + s])
+
+    def middle(s):
+        for g in range(pairs):
+            for h in range(quarter // LANES):
+                v = [ps[s, (g * n + x) * 8 : (g * n + x + 1) * 8, at(h)] for x in range(n)]
+                k = s * (quarter // LANES) + h
+                v = along_x(v, lambda r, k=k: k_ref[k, pl.ds(r, 8, stride=0), :])
+                for x in range(0, n, 2):
+                    q = slice((g * n + x) * 8, (g * n + x + 2) * 8)
+                    gh[s, q, at(h)], gl[s, q, at(h)] = split(jnp.concatenate(v[x : x + 2], axis=0))
+
+    def back(s):
+        ps[s] = dot_t(gh[s], w_ref[s]) + dot_t(gl[s], w_ref[s]) + dot_t(gh[s], w_ref[4 + s])
+
+    forward(0)
+    forward(1)
+    middle(0)
+    forward(2)
+    middle(1)
+    back(0)
+    forward(3)
+    middle(2)
+    back(1)
+    middle(3)
+    back(2)
+    back(3)
+    done = []
+    for x in range(n):
+        acc = [prior[x, :, cls(s)] if last else None for s in range(4)]
+        for g in range(pairs):
+            q = slice((g * n + x) * 8, (g * n + x + 1) * 8)
             for s, v in enumerate(butterfly([ps[s, q, :] for s in range(4)])):
-                v = v * pf[r, quarter * s : quarter * (s + 1)]
+                v = v * p8[g, x, :, cls(s)]
                 acc[s] = v if acc[s] is None else acc[s] + v
-        if last:
-            folded = {(s, h): acc[s][:, LANES * h : LANES * (h + 1)] for s in range(4) for h in (0, 1)}
-            peers = o_ref.shape[0]
-            each = n // peers
-            for t, v in enumerate(unfold(folded, n)):
-                for d in range(peers):
-                    o_ref[d, i * each : (i + 1) * each, LANES * t : LANES * (t + 1)] = v[
-                        d * each : (d + 1) * each
-                    ]
-        else:
+        if not last:
             for s in range(4):
-                o_ref[i, :, quarter * s : quarter * (s + 1)] = acc[s]
-
-
-def solve(targets, partners, consts, prior=None, peers=16):
+                o_ref[x, :, cls(s)] = acc[s]
+            continue
+        done.append(acc)
+        if len(done) == 2:
+            folded = {}
+            for s in range(4):
+                for h in range(quarter // LANES):
+                    a, b = (v[s][:, at(h)] for v in done)
+                    folded[s, h] = jnp.where(upper, a, pltpu.roll(b, tb, 0)) + jnp.where(upper, pltpu.roll(a, tb, 0), b)
+            for k, v in enumerate(unfold(folded, 8)):
+                o_ref[x // 2, :, at(k)] = v
+            done = []
+
+
+def solve(targets, partners, consts, prior=None):
     last = prior is not None
-    n = targets.shape[1]
-    nj = partners.shape[0] // n
-    tb = prior.shape[0] if last else targets.shape[0] // 2
-    rows, quarter = nj * n, n * n // 4
+    tiles, rows, _ = partners.shape
+    n, tb = 32, 4
+    pairs = rows // n // 2
     vmem = pl.BlockSpec(memory_space=pltpu.VMEM)
-    part = jax.ShapeDtypeStruct((tb, n, n * n), jnp.float32)
+    part = jax.ShapeDtypeStruct((n, 2 * tb, n * n), jnp.float32)
     if last:
         operands = (targets, prior, partners, *consts)
-        out_shape = jax.ShapeDtypeStruct((peers, tb * n // peers, n * n), jnp.float32)
+        out_shape = jax.ShapeDtypeStruct((n // 2, 2 * tb, n * n), jnp.float32)
     else:
         operands = (targets, partners, *consts)
         out_shape = (part, part)
+    long = pairs * n * 2 * tb
+    scratch = [
+        pltpu.VMEM((pairs, n, 2 * tb, n * n), jnp.float32),
+        pltpu.VMEM((4, long, n * n // 4), jnp.bfloat16),
+        pltpu.VMEM((4, long, n * n // 4), jnp.bfloat16),
+        pltpu.VMEM((4, long, n * n // 4), jnp.float32),
+    ]
+    if not last:
+        scratch.append(pltpu.VMEM((tiles, tb * n, LANES), jnp.float32))
     return pl.pallas_call(
-        functools.partial(solve_body, last, tb, nj, n),
+        functools.partial(solve_body, last, tb, n),
         out_shape=out_shape,
         in_specs=[vmem] * len(operands),
         out_specs=vmem if last else (vmem, vmem),
-        scratch_shapes=[
-            pltpu.VMEM((4, tb * rows, quarter), jnp.bfloat16),
-            pltpu.VMEM((4, tb * rows, quarter), jnp.bfloat16),
-            pltpu.VMEM((tb, 2 * rows, quarter), jnp.bfloat16),
-            pltpu.VMEM((4, tb * rows, quarter), jnp.float32),
-        ],
+        scratch_shapes=scratch,
         compiler_params=SOLVE_PARAMS,
         cost_estimate=pl.CostEstimate(
-            flops=2 * 5 * tb * 4 * rows * quarter * quarter, bytes_accessed=8 << 20, transcendentals=0
+            flops=2 * 6 * long * (n * n // 2) ** 2, bytes_accessed=8 << 20, transcendentals=0
         ),
     )(*operands)
 
@@ -250,7 +321,7 @@
         for k in range(core + 2, peers, 2):
             total = total + in_ref[k]
         halves.append(total)
-    order = [v[2 * i + q : 2 * i + q + 1] for q in (0, 1) for v in halves for i in range(rows // 2)]
+    order = [v[q * rows // 2 : (q + 1) * rows // 2] for q in (0, 1) for v in halves]
     slab = jnp.concatenate(order, axis=0)
     for k in range(o_ref.shape[0]):
         o_ref[k] = slab
@@ -368,13 +439,13 @@
 
 def shards(targets, partners, occupied, retained):
     owned, n, plane = targets.shape
-    consts = [jnp.asarray(c) for c in tables(n, partners.shape[2] // n)]
-    peers, groups = lax.axis_size(PTR), lax.axis_size(TGT)
+    consts = [jnp.asarray(c) for c in tables(n)]
+    groups = lax.axis_size(TGT)
     swap = [(0, 1), (1, 0)]
     own_partners, keep = folded_partners(partners, occupied, retained)
     other_partners = lax.ppermute(own_partners, "core", swap)
     partial_actions, folded = solve(targets, own_partners, consts)
-    cut = solve(folded, other_partners, consts, partial_actions, peers)
+    cut = solve(folded, other_partners, consts, partial_actions)
     copies = spread(lax.all_to_all(cut, PTR, 0, 0, tiled=True), groups)
     slab = lax.all_to_all(copies, TGT, 0, 0, tiled=True)
     summands = overlap(targets, slab, lax.axis_size(TGT + PTR), 1.0 / n**3)

time: 69.3 us -> 66.9 us (0.965)
  Pallas kernels: 16.1 us -> 13.2 us
    pallas_call x2, Pallas kernels: 10.5 us -> 8.7 us  [solve(): pl.pallas_call(functools.partial(solve_body, last, tb, n), out_shape=out_...]
    pallas_call x1, Pallas kernels: 1.96 us -> 0.84 us  [folded_partners(): pl.pallas_call(functools.partial(fold_body, nj, n), out_shape=(jax.ShapeD...]
  transfers between devices with their start and end apart: 1 -> 1, of which waited for: 0 -> 0; matrix products, arithmetic and copies ran while one was open for 0% -> 0% of each run, Pallas kernels for 7% -> 6%
where the time goes in v6:
time: 66.9 us; the launch traced here: 66.6 us
  blocking collectives  49.5 us (74%)
  Pallas kernels  13.2 us (20%)
  starting transfers between devices  1.5 us (2%)
  between operations  1.36 us (2%)
  local copies, waits for them, and re-layouts  1.05 us (2%)
    all_to_all x1, blocking collectives, shards(): summands = lax.all_to_all(summands, TGT + PTR, 0, 0, tiled=True)  17.9 us
    all_to_all x1, blocking collectives, shards(): slab = lax.all_to_all(copies, TGT, 0, 0, tiled=True)  16.2 us
    all_to_all x1, blocking collectives, shards(): copies = spread(lax.all_to_all(cut, PTR, 0, 0, tiled=True), groups)  15.4 us
    pallas_call x2, Pallas kernels, solve(): pl.pallas_call(functools.partial(solve_body, last, tb, n), out_shape=out_...  8.7 us
    pallas_call x1, Pallas kernels, compress(): pl.pallas_call(functools.partial(compress_body, owned), out_shape=jax.Sha...  2.97 us
    ppermute x1, starting transfers between devices, shards(): other_partners = lax.ppermute(own_partners, 'core', swap)  1.5 us
  transfers between devices with their start and end apart: 1, of which 0 were waited for; matrix products, arithmetic and copies ran while one was open for 0% of the time, Pallas kernels for 6%

profile of v6, /device:TPU:1, one launch (start us, length us, event | category | flops | bytes accessed | tf_op | source)
XLA Modules:
  0.0 66.6 jit_solution(14143075664968182308)
XLA Ops:
  1.3 0.0 copy-start.1
  1.3 1.0 %copy-done.1 = f32[32,32,128]{2,1,0:T(8,128)S(1)} copy-done((f32[32,32,128]{2,1,0:T(8,128)S(1)}, f32[32,32,128]{2,1,0:T(8,128)}, u32[]{:S(2)}) %copy-start.1) | copy-done | bytes 524312
  2.3 0.0 copy-start
  2.3 0.0 copy-start.2
  2.3 0.0 copy-start.3
  2.3 0.8 %shard_map.64 = (f32[8,128,128]{2,1,0:T(8,128)S(1)}, s32[8,128]{1,0:T(8,128)S(1)}) custom-call(f32[1024,128]{1,0:T(8,128)S(1)} %bitcast.1, s32[1]{0:T(128)S(6)} %copy.7.occ_ref, s32[1]{0:T(128)S(6)} %copy.8.rank_ref), custom_call_target="tpu_custom_call" | custom-call | flops 2147483648 | bytes 8388608 | tf_op jit(solution)/shard_map/pallas_call | solution.py:177
  3.2 1.5 %collective-permute-start = (f32[8,128,128]{2,1,0:T(8,128)S(1)}, f32[8,128,128]{2,1,0:T(8,128)S(1)}, u32[]{:S(2)}, u32[]{:S(2)}) collective-permute-start(f32[8,128,128]{2,1,0:T(8,128)S(1)} %get-tuple-element.9.refs_1_), channel_id=1, source_target_pairs={{0,1},{1,0},{2,3},{3,2},{4,5},{5,4},{6,7},{7,6},{8,9},{9,8},{10,11... | collective-permute-start | bytes 1572872 | tf_op jit(solution)/shard_map/ppermute | solution.py:446
  4.7 0.0 copy-done
  4.7 0.0 copy-done.2
  4.7 0.0 copy-done.3
  4.7 4.2 %shard_map.65 = (f32[32,8,1024]{2,1,0:T(8,128)S(1)}, f32[32,8,1024]{2,1,0:T(8,128)S(1)}) custom-call(f32[8,32,1024]{2,1,0:T(8,128)S(1)} %copy-done, f32[8,128,128]{2,1,0:T(8,128)S(1)} %get-tuple-element.9.refs_1_, bf16[8,256,256]{2,1,0:T(8,128)(2,1)S(1)} %copy-done.2, f32[8,32,128]{2,1,0:T(8,128)S(1)} %copy-done.3), custom_call_target="tpu_custom_call" | custom-call | flops 1610612736 | bytes 8388608 | tf_op jit(solution)/shard_map/pallas_call | solution.py:303
  8.9 0.0 collective-permute-done.refs_2_
  8.9 4.5 %shard_map.66 = f32[16,8,1024]{2,1,0:T(8,128)S(1)} custom-call(f32[32,8,1024]{2,1,0:T(8,128)S(1)} %get-tuple-element.10.refs_0_, f32[32,8,1024]{2,1,0:T(8,128)S(1)} %get-tuple-element.11.refs_1_, f32[8,128,128]{2,1,0:T(8,128)S(1)} %collective-permute-done.refs_2_, bf16[8,256,256]{2,1,0:T(8,128)(2,1)S(1)} %copy-done.2, f32[8,32,128]{2,1,0:T(8,128)S(1)} %copy-done.3), custom_call_target="tpu_custom_call" | custom-call | flops 1610612736 | bytes 8388608 | tf_op jit(solution)/shard_map/pallas_call | solution.py:303
  13.4 15.4 %all_to_all.15.in_ref = f32[16,8,1024]{2,1,0:T(8,128)S(1)} all-to-all(f32[16,8,1024]{2,1,0:T(8,128)S(1)} %shard_map.66), channel_id=1, replica_groups=mesh['tgt_0'=2,'tgt_1'=4,'ptr_0'=4,'ptr_1'=2,'core'=2] {'ptr_0','ptr_1',..., dimensions={0} | all-to-all | bytes 1048576 | tf_op jit(solution)/shard_map/all_to_all | solution.py:449
  28.9 0.1 shard_map.67
  28.9 16.2 %all_to_all.16.a_ref = f32[8,16,1024]{2,1,0:T(8,128)S(1)} all-to-all(f32[8,16,1024]{2,1,0:T(8,128)S(1)} %shard_map.67), channel_id=1, replica_groups=mesh['tgt_0'=2,'tgt_1'=4,'ptr_0'=4,'ptr_1'=2,'core'=2] {'tgt_0','tgt_1'}, dimensions={0} | all-to-all | bytes 1048576 | tf_op jit(solution)/shard_map/all_to_all | solution.py:450
  45.1 0.7 shard_map.68
  45.8 17.9 %all_to_all.17.s_ref = f32[128,4,128]{2,1,0:T(4,128)S(1)} all-to-all(f32[128,4,128]{2,1,0:T(4,128)S(1)} %shard_map.68), channel_id=1, replica_groups=mesh['tgt_0'=2,'tgt_1'=4,'ptr_0'=4,'ptr_1'=2,'core'=2] {'tgt_0','tgt_1',..., dimensions={0} | all-to-all | bytes 524288 | tf_op jit(solution)/shard_map/all_to_all | solution.py:452
  63.7 3.0 %shard_map.69 = f32[8,2,1024]{2,1,0:T(2,128)} custom-call(f32[128,4,128]{2,1,0:T(4,128)S(1)} %all_to_all.17.s_ref, f32[8,16,1024]{2,1,0:T(8,128)S(1)} %all_to_all.16.a_ref, s32[8,128]{1,0:T(8,128)S(1)} %get-tuple-element.12.keep_ref), custom_call_target="tpu_custom_call" | custom-call | tf_op jit(solution)/shard_map/pallas_call | solution.py:430
Async XLA Ops:
  1.3 1.0 %copy-start.1 = (f32[32,32,128]{2,1,0:T(8,128)S(1)}, f32[32,32,128]{2,1,0:T(8,128)}, u32[]{:S(2)}) copy-start(f32[32,32,128]{2,1,0:T(8,128)} %param.7) | copy-start | bytes 1572868
  2.3 2.4 %copy-start = (f32[8,32,1024]{2,1,0:T(8,128)S(1)}, f32[8,32,1024]{2,1,0:T(8,128)}, u32[]{:S(2)}) copy-start(f32[8,32,1024]{2,1,0:T(8,128)} %t_ref.1) | copy-start | bytes 3145732
  2.3 2.4 %copy-start.2 = (bf16[8,256,256]{2,1,0:T(8,128)(2,1)S(1)}, bf16[8,256,256]{2,1,0:T(8,128)(2,1)}, u32[]{:S(2)}) copy-start(bf16[8,256,256]{2,1,0:T(8,128)(2,1)} %constant.4.clone.refs_2_.refs_3_) | copy-start | bytes 3145732
  2.3 2.4 %copy-start.3 = (f32[8,32,128]{2,1,0:T(8,128)S(1)}, f32[8,32,128]{2,1,0:T(8,128)}, u32[]{:S(2)}) copy-start(f32[8,32,128]{2,1,0:T(8,128)} %constant.5.clone.refs_3_.refs_4_) | copy-start | bytes 393220
  3.2 5.7 %collective-permute-start = (f32[8,128,128]{2,1,0:T(8,128)S(1)}, f32[8,128,128]{2,1,0:T(8,128)S(1)}, u32[]{:S(2)}, u32[]{:S(2)}) collective-permute-start(f32[8,128,128]{2,1,0:T(8,128)S(1)} %get-tuple-element.9.refs_1_), channel_id=1, source_target_pairs={{0,1},{1,0},{2,3},{3,2},{4,5},{5,4},{6,7},{7,6},{8,9},{9,8},{10,11... | collective-permute-start | bytes 1572872 | tf_op jit(solution)/shard_map/ppermute | solution.py:446

commit v7 on v6

--- a/solution.py
+++ b/solution.py
@@ -273,8 +273,8 @@
                 for h in range(quarter // LANES):
                     a, b = (v[s][:, at(h)] for v in done)
                     folded[s, h] = jnp.where(upper, a, pltpu.roll(b, tb, 0)) + jnp.where(upper, pltpu.roll(a, tb, 0), b)
-            for k, v in enumerate(unfold(folded, 8)):
-                o_ref[x // 2, :, at(k)] = v
+            for (c, h), v in folded.items():
+                o_ref[x // 2, :, slice(quarter * c + LANES * h, quarter * c + LANES * (h + 1))] = v
             done = []
 
 
@@ -323,6 +323,8 @@
         halves.append(total)
     order = [v[q * rows // 2 : (q + 1) * rows // 2] for q in (0, 1) for v in halves]
     slab = jnp.concatenate(order, axis=0)
+    folded = {(k // 2, k % 2): slab[:, LANES * k : LANES * (k + 1)] for k in range(8)}
+    slab = jnp.concatenate(unfold(folded, slab.shape[0]), axis=1)
     for k in range(o_ref.shape[0]):
         o_ref[k] = slab
 
@@ -397,19 +399,28 @@
             for k in range(8)
         }
         root = jnp.ones((8, LANES), jnp.float32)
-        for k in range(8):
-            pivot = down(cols[p, k], k)
-            over = 1.0 / pivot
-            root = jnp.where(sub == k, lax.rsqrt(pivot), root)
-            line = down(tiles[p], k)
-            cross = [down(cols[p, m], k) for m in range(k + 1, 8)]
+        for k in range(0, 8, 2):
+            first, second = cols[p, k], cols[p, k + 1]
+            a, b, d = down(first, k), down(second, k), down(second, k + 1)
+            over = 1.0 / a
+            pivot = d - b * (b * over)
+            under = a * (1.0 / (a * d - b * b))
+            ratio = b * over
+            root = jnp.where(sub == k, lax.rsqrt(a), jnp.where(sub == k + 1, lax.rsqrt(pivot), root))
+            line, next_line = down(tiles[p], k), down(tiles[p], k + 1)
+            next_line = next_line - ratio * line
+            cross = [(down(cols[p, m], k), down(cols[p, m], k + 1)) for m in range(k + 2, 8)]
+            cross = [(u, v - ratio * u) for u, v in cross]
             for t in later:
                 f = cols[t, k] * over
+                g = (cols[t, k + 1] - cols[t, k] * ratio) * under
                 if t == p:
                     f = jnp.where(sub > k, f, 0.0)
-                tiles[t] = tiles[t] - f * line
-                for m in range(k + 1, 8):
-                    cols[t, m] = cols[t, m] - f * cross[m - k - 1]
+                    g = jnp.where(sub > k + 1, g, 0.0)
+                tiles[t] = tiles[t] - f * line - g * next_line
+                for m in range(k + 2, 8):
+                    u, v = cross[m - k - 2]
+                    cols[t, m] = cols[t, m] - f * u - g * v
         inv_ref[8 * p : 8 * p + 8, :] = tiles[p] * root
     first = lax.axis_index(TGT) * owned
     mine = inv_ref[pl.ds(pl.multiple_of(first, 8), owned), :][:, count:]

time: 66.9 us -> 66.4 us (level)
  no operation moved by 1% of the time
where the time goes in v7:
time: 66.4 us; the launch traced here: 66.1 us
  blocking collectives  49.5 us (75%)
  Pallas kernels  12.6 us (19%)
  starting transfers between devices  1.5 us (2%)
  between operations  1.36 us (2%)
  local copies, waits for them, and re-layouts  1.05 us (2%)
    all_to_all x1, blocking collectives, shards(): summands = lax.all_to_all(summands, TGT + PTR, 0, 0, tiled=True)  17.9 us
    all_to_all x1, blocking collectives, shards(): slab = lax.all_to_all(copies, TGT, 0, 0, tiled=True)  16.2 us
    all_to_all x1, blocking collectives, shards(): copies = spread(lax.all_to_all(cut, PTR, 0, 0, tiled=True), groups)  15.4 us
    pallas_call x2, Pallas kernels, solve(): pl.pallas_call(functools.partial(solve_body, last, tb, n), out_shape=out_...  8.12 us
    pallas_call x1, Pallas kernels, compress(): pl.pallas_call(functools.partial(compress_body, owned), out_shape=jax.Sha...  2.89 us
    ppermute x1, starting transfers between devices, shards(): other_partners = lax.ppermute(own_partners, 'core', swap)  1.5 us
  transfers between devices with their start and end apart: 1, of which 0 were waited for; matrix products, arithmetic and copies ran while one was open for 0% of the time, Pallas kernels for 6%

profile of v7, /device:TPU:1, one launch (start us, length us, event | category | flops | bytes accessed | tf_op | source)
XLA Modules:
  0.0 66.1 jit_solution(9367007181688286821)
XLA Ops:
  1.3 0.0 copy-start.1
  1.3 1.0 %copy-done.1 = f32[32,32,128]{2,1,0:T(8,128)S(1)} copy-done((f32[32,32,128]{2,1,0:T(8,128)S(1)}, f32[32,32,128]{2,1,0:T(8,128)}, u32[]{:S(2)}) %copy-start.1) | copy-done | bytes 524312
  2.3 0.0 copy-start
  2.3 0.0 copy-start.2
  2.3 0.0 copy-start.3
  2.3 0.8 %shard_map.64 = (f32[8,128,128]{2,1,0:T(8,128)S(1)}, s32[8,128]{1,0:T(8,128)S(1)}) custom-call(f32[1024,128]{1,0:T(8,128)S(1)} %bitcast.1, s32[1]{0:T(128)S(6)} %copy.7.occ_ref, s32[1]{0:T(128)S(6)} %copy.8.rank_ref), custom_call_target="tpu_custom_call" | custom-call | flops 2147483648 | bytes 8388608 | tf_op jit(solution)/shard_map/pallas_call | solution.py:177
  3.2 1.5 %collective-permute-start = (f32[8,128,128]{2,1,0:T(8,128)S(1)}, f32[8,128,128]{2,1,0:T(8,128)S(1)}, u32[]{:S(2)}, u32[]{:S(2)}) collective-permute-start(f32[8,128,128]{2,1,0:T(8,128)S(1)} %get-tuple-element.9.refs_1_), channel_id=1, source_target_pairs={{0,1},{1,0},{2,3},{3,2},{4,5},{5,4},{6,7},{7,6},{8,9},{9,8},{10,11... | collective-permute-start | bytes 1572872 | tf_op jit(solution)/shard_map/ppermute | solution.py:457
  4.7 0.0 copy-done
  4.7 0.0 copy-done.2
  4.7 0.0 copy-done.3
  4.7 4.2 %shard_map.65 = (f32[32,8,1024]{2,1,0:T(8,128)S(1)}, f32[32,8,1024]{2,1,0:T(8,128)S(1)}) custom-call(f32[8,32,1024]{2,1,0:T(8,128)S(1)} %copy-done, f32[8,128,128]{2,1,0:T(8,128)S(1)} %get-tuple-element.9.refs_1_, bf16[8,256,256]{2,1,0:T(8,128)(2,1)S(1)} %copy-done.2, f32[8,32,128]{2,1,0:T(8,128)S(1)} %copy-done.3), custom_call_target="tpu_custom_call" | custom-call | flops 1610612736 | bytes 8388608 | tf_op jit(solution)/shard_map/pallas_call | solution.py:303
  8.9 0.0 collective-permute-done.refs_2_
  8.9 3.9 %shard_map.66 = f32[16,8,1024]{2,1,0:T(8,128)S(1)} custom-call(f32[32,8,1024]{2,1,0:T(8,128)S(1)} %get-tuple-element.10.refs_0_, f32[32,8,1024]{2,1,0:T(8,128)S(1)} %get-tuple-element.11.refs_1_, f32[8,128,128]{2,1,0:T(8,128)S(1)} %collective-permute-done.refs_2_, bf16[8,256,256]{2,1,0:T(8,128)(2,1)S(1)} %copy-done.2, f32[8,32,128]{2,1,0:T(8,128)S(1)} %copy-done.3), custom_call_target="tpu_custom_call" | custom-call | flops 1610612736 | bytes 8388608 | tf_op jit(solution)/shard_map/pallas_call | solution.py:303
  12.8 15.4 %all_to_all.15.in_ref = f32[16,8,1024]{2,1,0:T(8,128)S(1)} all-to-all(f32[16,8,1024]{2,1,0:T(8,128)S(1)} %shard_map.66), channel_id=1, replica_groups=mesh['tgt_0'=2,'tgt_1'=4,'ptr_0'=4,'ptr_1'=2,'core'=2] {'ptr_0','ptr_1',..., dimensions={0} | all-to-all | bytes 1048576 | tf_op jit(solution)/shard_map/all_to_all | solution.py:460
  28.3 0.1 shard_map.67
  28.4 16.2 %all_to_all.16.a_ref = f32[8,16,1024]{2,1,0:T(8,128)S(1)} all-to-all(f32[8,16,1024]{2,1,0:T(8,128)S(1)} %shard_map.67), channel_id=1, replica_groups=mesh['tgt_0'=2,'tgt_1'=4,'ptr_0'=4,'ptr_1'=2,'core'=2] {'tgt_0','tgt_1'}, dimensions={0} | all-to-all | bytes 1048576 | tf_op jit(solution)/shard_map/all_to_all | solution.py:461
  44.6 0.7 shard_map.68
  45.3 17.9 %all_to_all.17.s_ref = f32[128,4,128]{2,1,0:T(4,128)S(1)} all-to-all(f32[128,4,128]{2,1,0:T(4,128)S(1)} %shard_map.68), channel_id=1, replica_groups=mesh['tgt_0'=2,'tgt_1'=4,'ptr_0'=4,'ptr_1'=2,'core'=2] {'tgt_0','tgt_1',..., dimensions={0} | all-to-all | bytes 524288 | tf_op jit(solution)/shard_map/all_to_all | solution.py:463
  63.2 2.9 %shard_map.69 = f32[8,2,1024]{2,1,0:T(2,128)} custom-call(f32[128,4,128]{2,1,0:T(4,128)S(1)} %all_to_all.17.s_ref, f32[8,16,1024]{2,1,0:T(8,128)S(1)} %all_to_all.16.a_ref, s32[8,128]{1,0:T(8,128)S(1)} %get-tuple-element.12.keep_ref), custom_call_target="tpu_custom_call" | custom-call | tf_op jit(solution)/shard_map/pallas_call | solution.py:441
Async XLA Ops:
  1.3 1.0 %copy-start.1 = (f32[32,32,128]{2,1,0:T(8,128)S(1)}, f32[32,32,128]{2,1,0:T(8,128)}, u32[]{:S(2)}) copy-start(f32[32,32,128]{2,1,0:T(8,128)} %param.7) | copy-start | bytes 1572868
  2.3 2.4 %copy-start = (f32[8,32,1024]{2,1,0:T(8,128)S(1)}, f32[8,32,1024]{2,1,0:T(8,128)}, u32[]{:S(2)}) copy-start(f32[8,32,1024]{2,1,0:T(8,128)} %t_ref.1) | copy-start | bytes 3145732
  2.3 2.4 %copy-start.2 = (bf16[8,256,256]{2,1,0:T(8,128)(2,1)S(1)}, bf16[8,256,256]{2,1,0:T(8,128)(2,1)}, u32[]{:S(2)}) copy-start(bf16[8,256,256]{2,1,0:T(8,128)(2,1)} %constant.4.clone.refs_2_.refs_3_) | copy-start | bytes 3145732
  2.3 2.4 %copy-start.3 = (f32[8,32,128]{2,1,0:T(8,128)S(1)}, f32[8,32,128]{2,1,0:T(8,128)}, u32[]{:S(2)}) copy-start(f32[8,32,128]{2,1,0:T(8,128)} %constant.5.clone.refs_3_.refs_4_) | copy-start | bytes 393220
  3.2 5.7 %collective-permute-start = (f32[8,128,128]{2,1,0:T(8,128)S(1)}, f32[8,128,128]{2,1,0:T(8,128)S(1)}, u32[]{:S(2)}, u32[]{:S(2)}) collective-permute-start(f32[8,128,128]{2,1,0:T(8,128)S(1)} %get-tuple-element.9.refs_1_), channel_id=1, source_target_pairs={{0,1},{1,0},{2,3},{3,2},{4,5},{5,4},{6,7},{7,6},{8,9},{9,8},{10,11... | collective-permute-start | bytes 1572872 | tf_op jit(solution)/shard_map/ppermute | solution.py:457

commit v8 on v7

--- a/solution.py
+++ b/solution.py
@@ -242,18 +242,11 @@
     def back(s):
         ps[s] = dot_t(gh[s], w_ref[s]) + dot_t(gl[s], w_ref[s]) + dot_t(gh[s], w_ref[4 + s])
 
-    forward(0)
-    forward(1)
-    middle(0)
-    forward(2)
-    middle(1)
-    back(0)
-    forward(3)
-    middle(2)
-    back(1)
-    middle(3)
-    back(2)
-    back(3)
+    steps = "ffffmmmmbbbb" if last else "ffmfmbfmbmbb"
+    seen = dict.fromkeys("fmb", 0)
+    for step in steps:
+        {"f": forward, "m": middle, "b": back}[step](seen[step])
+        seen[step] += 1
     done = []
     for x in range(n):
         acc = [prior[x, :, cls(s)] if last else None for s in range(4)]
@@ -391,37 +384,41 @@
     tiles = [wide[8 * t : 8 * t + 8] for t in range(count // 8)]
     sub = lax.broadcasted_iota(jnp.int32, (8, LANES), 0)
     down = lambda v, k: jnp.broadcast_to(v[k : k + 1], (8, LANES))
-    for p in range(count // 8):
-        later = range(p, count // 8)
+    wide_panel = 16
+    tops = count // 8
+    roots = [jnp.ones((8, LANES), jnp.float32)] * tops
+    for p in range(0, count, wide_panel):
         cols = {
-            (t, k): jnp.broadcast_to(tiles[t][:, 8 * p + k : 8 * p + k + 1], (8, LANES))
-            for t in later
-            for k in range(8)
+            (t, k): jnp.broadcast_to(tiles[t][:, k : k + 1], (8, LANES))
+            for t in range(p // 8, tops)
+            for k in range(p, p + wide_panel)
         }
-        root = jnp.ones((8, LANES), jnp.float32)
-        for k in range(0, 8, 2):
-            first, second = cols[p, k], cols[p, k + 1]
-            a, b, d = down(first, k), down(second, k), down(second, k + 1)
+        for k in range(p, p + wide_panel, 2):
+            top, r = k // 8, k % 8
+            one, two = cols[top, k], cols[top, k + 1]
+            a, b, d = down(one, r), down(two, r), down(two, r + 1)
             over = 1.0 / a
-            pivot = d - b * (b * over)
             under = a * (1.0 / (a * d - b * b))
             ratio = b * over
-            root = jnp.where(sub == k, lax.rsqrt(a), jnp.where(sub == k + 1, lax.rsqrt(pivot), root))
-            line, next_line = down(tiles[p], k), down(tiles[p], k + 1)
-            next_line = next_line - ratio * line
-            cross = [(down(cols[p, m], k), down(cols[p, m], k + 1)) for m in range(k + 2, 8)]
-            cross = [(u, v - ratio * u) for u, v in cross]
-            for t in later:
+            pivot = d - b * ratio
+            roots[top] = jnp.where(sub == r, lax.rsqrt(a), jnp.where(sub == r + 1, lax.rsqrt(pivot), roots[top]))
+            line = down(tiles[top], r)
+            next_line = down(tiles[top], r + 1) - ratio * line
+            rest = range(k + 2, p + wide_panel)
+            cross = {m: (down(cols[top, m], r), down(cols[top, m], r + 1)) for m in rest}
+            cross = {m: (u, v - ratio * u) for m, (u, v) in cross.items()}
+            for t in range(top, tops):
                 f = cols[t, k] * over
                 g = (cols[t, k + 1] - cols[t, k] * ratio) * under
-                if t == p:
-                    f = jnp.where(sub > k, f, 0.0)
-                    g = jnp.where(sub > k + 1, g, 0.0)
+                if t == top:
+                    f = jnp.where(sub > r, f, 0.0)
+                    g = jnp.where(sub > r + 1, g, 0.0)
                 tiles[t] = tiles[t] - f * line - g * next_line
-                for m in range(k + 2, 8):
-                    u, v = cross[m - k - 2]
+                for m in rest:
+                    u, v = cross[m]
                     cols[t, m] = cols[t, m] - f * u - g * v
-        inv_ref[8 * p : 8 * p + 8, :] = tiles[p] * root
+    for t in range(tops):
+        inv_ref[8 * t : 8 * t + 8, :] = tiles[t] * roots[t]
     first = lax.axis_index(TGT) * owned
     mine = inv_ref[pl.ds(pl.multiple_of(first, 8), owned), :][:, count:]
     kept = first + lax.broadcasted_iota(jnp.int32, (owned, count), 0) < keep_ref[:owned, :count]

time: 66.4 us -> 66 us (level)
  no operation moved by 1% of the time
where the time goes in v8:
time: 66 us; the launch traced here: 65.8 us
  blocking collectives  49.5 us (75%)
  Pallas kernels  12.3 us (19%)
  starting transfers between devices  1.5 us (2%)
  between operations  1.36 us (2%)
  local copies, waits for them, and re-layouts  1.05 us (2%)
    all_to_all x1, blocking collectives, shards(): summands = lax.all_to_all(summands, TGT + PTR, 0, 0, tiled=True)  17.9 us
    all_to_all x1, blocking collectives, shards(): slab = lax.all_to_all(copies, TGT, 0, 0, tiled=True)  16.2 us
    all_to_all x1, blocking collectives, shards(): copies = spread(lax.all_to_all(cut, PTR, 0, 0, tiled=True), groups)  15.4 us
    pallas_call x2, Pallas kernels, solve(): pl.pallas_call(functools.partial(solve_body, last, tb, n), out_shape=out_...  8.01 us
    pallas_call x1, Pallas kernels, compress(): pl.pallas_call(functools.partial(compress_body, owned), out_shape=jax.Sha...  2.68 us
    ppermute x1, starting transfers between devices, shards(): other_partners = lax.ppermute(own_partners, 'core', swap)  1.5 us
  transfers between devices with their start and end apart: 1, of which 0 were waited for; matrix products, arithmetic and copies ran while one was open for 0% of the time, Pallas kernels for 6%

profile of v8, /device:TPU:1, one launch (start us, length us, event | category | flops | bytes accessed | tf_op | source)
XLA Modules:
  0.0 65.8 jit_solution(16105330836254092863)
XLA Ops:
  1.3 0.0 copy-start.1
  1.3 1.0 %copy-done.1 = f32[32,32,128]{2,1,0:T(8,128)S(1)} copy-done((f32[32,32,128]{2,1,0:T(8,128)S(1)}, f32[32,32,128]{2,1,0:T(8,128)}, u32[]{:S(2)}) %copy-start.1) | copy-done | bytes 524312
  2.3 0.0 copy-start
  2.3 0.0 copy-start.2
  2.3 0.0 copy-start.3
  2.3 0.8 %shard_map.64 = (f32[8,128,128]{2,1,0:T(8,128)S(1)}, s32[8,128]{1,0:T(8,128)S(1)}) custom-call(f32[1024,128]{1,0:T(8,128)S(1)} %bitcast.1, s32[1]{0:T(128)S(6)} %copy.7.occ_ref, s32[1]{0:T(128)S(6)} %copy.8.rank_ref), custom_call_target="tpu_custom_call" | custom-call | flops 2147483648 | bytes 8388608 | tf_op jit(solution)/shard_map/pallas_call | solution.py:177
  3.2 1.5 %collective-permute-start = (f32[8,128,128]{2,1,0:T(8,128)S(1)}, f32[8,128,128]{2,1,0:T(8,128)S(1)}, u32[]{:S(2)}, u32[]{:S(2)}) collective-permute-start(f32[8,128,128]{2,1,0:T(8,128)S(1)} %get-tuple-element.9.refs_1_), channel_id=1, source_target_pairs={{0,1},{1,0},{2,3},{3,2},{4,5},{5,4},{6,7},{7,6},{8,9},{9,8},{10,11... | collective-permute-start | bytes 1572872 | tf_op jit(solution)/shard_map/ppermute | solution.py:454
  4.7 0.0 copy-done
  4.7 0.0 copy-done.2
  4.7 0.0 copy-done.3
  4.7 4.2 %shard_map.65 = (f32[32,8,1024]{2,1,0:T(8,128)S(1)}, f32[32,8,1024]{2,1,0:T(8,128)S(1)}) custom-call(f32[8,32,1024]{2,1,0:T(8,128)S(1)} %copy-done, f32[8,128,128]{2,1,0:T(8,128)S(1)} %get-tuple-element.9.refs_1_, bf16[8,256,256]{2,1,0:T(8,128)(2,1)S(1)} %copy-done.2, f32[8,32,128]{2,1,0:T(8,128)S(1)} %copy-done.3), custom_call_target="tpu_custom_call" | custom-call | flops 1610612736 | bytes 8388608 | tf_op jit(solution)/shard_map/pallas_call | solution.py:296
  8.9 0.0 collective-permute-done.refs_2_
  8.9 3.8 %shard_map.66 = f32[16,8,1024]{2,1,0:T(8,128)S(1)} custom-call(f32[32,8,1024]{2,1,0:T(8,128)S(1)} %get-tuple-element.10.refs_0_, f32[32,8,1024]{2,1,0:T(8,128)S(1)} %get-tuple-element.11.refs_1_, f32[8,128,128]{2,1,0:T(8,128)S(1)} %collective-permute-done.refs_2_, bf16[8,256,256]{2,1,0:T(8,128)(2,1)S(1)} %copy-done.2, f32[8,32,128]{2,1,0:T(8,128)S(1)} %copy-done.3), custom_call_target="tpu_custom_call" | custom-call | flops 1610612736 | bytes 8388608 | tf_op jit(solution)/shard_map/pallas_call | solution.py:296
  12.7 15.4 %all_to_all.15.in_ref = f32[16,8,1024]{2,1,0:T(8,128)S(1)} all-to-all(f32[16,8,1024]{2,1,0:T(8,128)S(1)} %shard_map.66), channel_id=1, replica_groups=mesh['tgt_0'=2,'tgt_1'=4,'ptr_0'=4,'ptr_1'=2,'core'=2] {'ptr_0','ptr_1',..., dimensions={0} | all-to-all | bytes 1048576 | tf_op jit(solution)/shard_map/all_to_all | solution.py:457
  28.2 0.1 shard_map.67
  28.3 16.2 %all_to_all.16.a_ref = f32[8,16,1024]{2,1,0:T(8,128)S(1)} all-to-all(f32[8,16,1024]{2,1,0:T(8,128)S(1)} %shard_map.67), channel_id=1, replica_groups=mesh['tgt_0'=2,'tgt_1'=4,'ptr_0'=4,'ptr_1'=2,'core'=2] {'tgt_0','tgt_1'}, dimensions={0} | all-to-all | bytes 1048576 | tf_op jit(solution)/shard_map/all_to_all | solution.py:458
  44.5 0.7 shard_map.68
  45.2 17.9 %all_to_all.17.s_ref = f32[128,4,128]{2,1,0:T(4,128)S(1)} all-to-all(f32[128,4,128]{2,1,0:T(4,128)S(1)} %shard_map.68), channel_id=1, replica_groups=mesh['tgt_0'=2,'tgt_1'=4,'ptr_0'=4,'ptr_1'=2,'core'=2] {'tgt_0','tgt_1',..., dimensions={0} | all-to-all | bytes 524288 | tf_op jit(solution)/shard_map/all_to_all | solution.py:460
  63.1 2.7 %shard_map.69 = f32[8,2,1024]{2,1,0:T(2,128)} custom-call(f32[128,4,128]{2,1,0:T(4,128)S(1)} %all_to_all.17.s_ref, f32[8,16,1024]{2,1,0:T(8,128)S(1)} %all_to_all.16.a_ref, s32[8,128]{1,0:T(8,128)S(1)} %get-tuple-element.12.keep_ref), custom_call_target="tpu_custom_call" | custom-call | tf_op jit(solution)/shard_map/pallas_call | solution.py:438
Async XLA Ops:
  1.3 1.0 %copy-start.1 = (f32[32,32,128]{2,1,0:T(8,128)S(1)}, f32[32,32,128]{2,1,0:T(8,128)}, u32[]{:S(2)}) copy-start(f32[32,32,128]{2,1,0:T(8,128)} %param.7) | copy-start | bytes 1572868
  2.3 2.4 %copy-start = (f32[8,32,1024]{2,1,0:T(8,128)S(1)}, f32[8,32,1024]{2,1,0:T(8,128)}, u32[]{:S(2)}) copy-start(f32[8,32,1024]{2,1,0:T(8,128)} %t_ref.1) | copy-start | bytes 3145732
  2.3 2.4 %copy-start.2 = (bf16[8,256,256]{2,1,0:T(8,128)(2,1)S(1)}, bf16[8,256,256]{2,1,0:T(8,128)(2,1)}, u32[]{:S(2)}) copy-start(bf16[8,256,256]{2,1,0:T(8,128)(2,1)} %constant.4.clone.refs_2_.refs_3_) | copy-start | bytes 3145732
  2.3 2.4 %copy-start.3 = (f32[8,32,128]{2,1,0:T(8,128)S(1)}, f32[8,32,128]{2,1,0:T(8,128)}, u32[]{:S(2)}) copy-start(f32[8,32,128]{2,1,0:T(8,128)} %constant.5.clone.refs_3_.refs_4_) | copy-start | bytes 393220
  3.2 5.7 %collective-permute-start = (f32[8,128,128]{2,1,0:T(8,128)S(1)}, f32[8,128,128]{2,1,0:T(8,128)S(1)}, u32[]{:S(2)}, u32[]{:S(2)}) collective-permute-start(f32[8,128,128]{2,1,0:T(8,128)S(1)} %get-tuple-element.9.refs_1_), channel_id=1, source_target_pairs={{0,1},{1,0},{2,3},{3,2},{4,5},{5,4},{6,7},{7,6},{8,9},{9,8},{10,11... | collective-permute-start | bytes 1572872 | tf_op jit(solution)/shard_map/ppermute | solution.py:454

commit v9 on v8

--- a/solution.py
+++ b/solution.py
@@ -339,18 +339,16 @@
 def overlap_body(scale, t_ref, a_ref, o_ref):
     owned = t_ref.shape[0]
     first = 2 * lax.axis_index(PTR)
-    total = None
-    for q in (0, 1):
-        t = [t_ref[i, pl.ds(first + q, 1), :] for i in range(owned)]
-        s = lax.dot_general(
-            jnp.concatenate(t, axis=0),
-            plane_of(a_ref, q),
-            (((1,), (1,)), ((), ())),
-            precision=lax.Precision.HIGHEST,
-            preferred_element_type=jnp.float32,
-        )
-        total = s if total is None else total + s
-    total = total * scale
+    t = [
+        jnp.concatenate([t_ref[i, pl.ds(first + q, 1), :] for i in range(owned)], axis=0) for q in (0, 1)
+    ]
+    total = scale * lax.dot_general(
+        jnp.concatenate(t, axis=1),
+        jnp.concatenate([plane_of(a_ref, q) for q in (0, 1)], axis=1),
+        (((1,), (1,)), ((), ())),
+        precision=lax.Precision.HIGHEST,
+        preferred_element_type=jnp.float32,
+    )
     packed = jnp.concatenate([total[: owned // 2], total[owned // 2 :]], axis=1)
     for k in range(o_ref.shape[0]):
         o_ref[k] = packed
@@ -372,9 +370,10 @@
     count = groups * owned
     rows = []
     for t in range(groups):
-        total = s_ref[t * slabs]
-        for k in range(1, slabs):
-            total = total + s_ref[t * slabs + k]
+        terms = [s_ref[t * slabs + k] for k in range(slabs)]
+        while len(terms) > 1:
+            terms = [a + b for a, b in zip(terms[0::2], terms[1::2])]
+        total = terms[0]
         rows += [total[:, :count], total[:, count:]]
     square = jnp.concatenate(rows, axis=0)
     square = 0.5 * (square + square.T)
@@ -423,13 +422,14 @@
     mine = inv_ref[pl.ds(pl.multiple_of(first, 8), owned), :][:, count:]
     kept = first + lax.broadcasted_iota(jnp.int32, (owned, count), 0) < keep_ref[:owned, :count]
     mine = jnp.where(kept, mine, 0.0)
+    both = jnp.dot(
+        mine,
+        jnp.concatenate([plane_of(a_ref, q) for q in (0, 1)], axis=1),
+        precision=lax.Precision.HIGHEST,
+        preferred_element_type=jnp.float32,
+    )
     for q in (0, 1):
-        o_ref[:, q, :] = jnp.dot(
-            mine,
-            plane_of(a_ref, q),
-            precision=lax.Precision.HIGHEST,
-            preferred_element_type=jnp.float32,
-        )
+        o_ref[:, q, :] = both[:, q * a_ref.shape[2] : (q + 1) * a_ref.shape[2]]
 
 
 def compress(summands, slab, keep, owned):

time: 66 us -> 66.1 us (level)
  no operation moved by 1% of the time
where the time goes in v9:
time: 66.1 us; the launch traced here: 65.8 us
  blocking collectives  49.5 us (75%)
  Pallas kernels  12.3 us (19%)
  starting transfers between devices  1.5 us (2%)
  between operations  1.36 us (2%)
  local copies, waits for them, and re-layouts  1.05 us (2%)
    all_to_all x1, blocking collectives, shards(): summands = lax.all_to_all(summands, TGT + PTR, 0, 0, tiled=True)  17.9 us
    all_to_all x1, blocking collectives, shards(): slab = lax.all_to_all(copies, TGT, 0, 0, tiled=True)  16.2 us
    all_to_all x1, blocking collectives, shards(): copies = spread(lax.all_to_all(cut, PTR, 0, 0, tiled=True), groups)  15.4 us
    pallas_call x2, Pallas kernels, solve(): pl.pallas_call(functools.partial(solve_body, last, tb, n), out_shape=out_...  8.01 us
    pallas_call x1, Pallas kernels, compress(): pl.pallas_call(functools.partial(compress_body, owned), out_shape=jax.Sha...  2.71 us
    ppermute x1, starting transfers between devices, shards(): other_partners = lax.ppermute(own_partners, 'core', swap)  1.5 us
  transfers between devices with their start and end apart: 1, of which 0 were waited for; matrix products, arithmetic and copies ran while one was open for 0% of the time, Pallas kernels for 6%

profile of v9, /device:TPU:1, one launch (start us, length us, event | category | flops | bytes accessed | tf_op | source)
XLA Modules:
  0.0 65.8 jit_solution(6202826793881173927)
XLA Ops:
  1.3 0.0 copy-start.1
  1.3 1.0 %copy-done.1 = f32[32,32,128]{2,1,0:T(8,128)S(1)} copy-done((f32[32,32,128]{2,1,0:T(8,128)S(1)}, f32[32,32,128]{2,1,0:T(8,128)}, u32[]{:S(2)}) %copy-start.1) | copy-done | bytes 524312
  2.3 0.0 copy-start
  2.3 0.0 copy-start.2
  2.3 0.0 copy-start.3
  2.3 0.8 %shard_map.64 = (f32[8,128,128]{2,1,0:T(8,128)S(1)}, s32[8,128]{1,0:T(8,128)S(1)}) custom-call(f32[1024,128]{1,0:T(8,128)S(1)} %bitcast.1, s32[1]{0:T(128)S(6)} %copy.7.occ_ref, s32[1]{0:T(128)S(6)} %copy.8.rank_ref), custom_call_target="tpu_custom_call" | custom-call | flops 2147483648 | bytes 8388608 | tf_op jit(solution)/shard_map/pallas_call | solution.py:177
  3.2 1.5 %collective-permute-start = (f32[8,128,128]{2,1,0:T(8,128)S(1)}, f32[8,128,128]{2,1,0:T(8,128)S(1)}, u32[]{:S(2)}, u32[]{:S(2)}) collective-permute-start(f32[8,128,128]{2,1,0:T(8,128)S(1)} %get-tuple-element.9.refs_1_), channel_id=1, source_target_pairs={{0,1},{1,0},{2,3},{3,2},{4,5},{5,4},{6,7},{7,6},{8,9},{9,8},{10,11... | collective-permute-start | bytes 1572872 | tf_op jit(solution)/shard_map/ppermute | solution.py:454
  4.7 0.0 copy-done
  4.7 0.0 copy-done.2
  4.7 0.0 copy-done.3
  4.7 4.2 %shard_map.65 = (f32[32,8,1024]{2,1,0:T(8,128)S(1)}, f32[32,8,1024]{2,1,0:T(8,128)S(1)}) custom-call(f32[8,32,1024]{2,1,0:T(8,128)S(1)} %copy-done, f32[8,128,128]{2,1,0:T(8,128)S(1)} %get-tuple-element.9.refs_1_, bf16[8,256,256]{2,1,0:T(8,128)(2,1)S(1)} %copy-done.2, f32[8,32,128]{2,1,0:T(8,128)S(1)} %copy-done.3), custom_call_target="tpu_custom_call" | custom-call | flops 1610612736 | bytes 8388608 | tf_op jit(solution)/shard_map/pallas_call | solution.py:296
  8.9 0.0 collective-permute-done.refs_2_
  8.9 3.8 %shard_map.66 = f32[16,8,1024]{2,1,0:T(8,128)S(1)} custom-call(f32[32,8,1024]{2,1,0:T(8,128)S(1)} %get-tuple-element.10.refs_0_, f32[32,8,1024]{2,1,0:T(8,128)S(1)} %get-tuple-element.11.refs_1_, f32[8,128,128]{2,1,0:T(8,128)S(1)} %collective-permute-done.refs_2_, bf16[8,256,256]{2,1,0:T(8,128)(2,1)S(1)} %copy-done.2, f32[8,32,128]{2,1,0:T(8,128)S(1)} %copy-done.3), custom_call_target="tpu_custom_call" | custom-call | flops 1610612736 | bytes 8388608 | tf_op jit(solution)/shard_map/pallas_call | solution.py:296
  12.7 15.4 %all_to_all.15.in_ref = f32[16,8,1024]{2,1,0:T(8,128)S(1)} all-to-all(f32[16,8,1024]{2,1,0:T(8,128)S(1)} %shard_map.66), channel_id=1, replica_groups=mesh['tgt_0'=2,'tgt_1'=4,'ptr_0'=4,'ptr_1'=2,'core'=2] {'ptr_0','ptr_1',..., dimensions={0} | all-to-all | bytes 1048576 | tf_op jit(solution)/shard_map/all_to_all | solution.py:457
  28.2 0.1 shard_map.67
  28.3 16.2 %all_to_all.16.a_ref = f32[8,16,1024]{2,1,0:T(8,128)S(1)} all-to-all(f32[8,16,1024]{2,1,0:T(8,128)S(1)} %shard_map.67), channel_id=1, replica_groups=mesh['tgt_0'=2,'tgt_1'=4,'ptr_0'=4,'ptr_1'=2,'core'=2] {'tgt_0','tgt_1'}, dimensions={0} | all-to-all | bytes 1048576 | tf_op jit(solution)/shard_map/all_to_all | solution.py:458
  44.5 0.7 shard_map.68
  45.2 17.9 %all_to_all.17.s_ref = f32[128,4,128]{2,1,0:T(4,128)S(1)} all-to-all(f32[128,4,128]{2,1,0:T(4,128)S(1)} %shard_map.68), channel_id=1, replica_groups=mesh['tgt_0'=2,'tgt_1'=4,'ptr_0'=4,'ptr_1'=2,'core'=2] {'tgt_0','tgt_1',..., dimensions={0} | all-to-all | bytes 524288 | tf_op jit(solution)/shard_map/all_to_all | solution.py:460
  63.1 2.7 %shard_map.69 = f32[8,2,1024]{2,1,0:T(2,128)} custom-call(f32[128,4,128]{2,1,0:T(4,128)S(1)} %all_to_all.17.s_ref, f32[8,16,1024]{2,1,0:T(8,128)S(1)} %all_to_all.16.a_ref, s32[8,128]{1,0:T(8,128)S(1)} %get-tuple-element.12.keep_ref), custom_call_target="tpu_custom_call" | custom-call | tf_op jit(solution)/shard_map/pallas_call | solution.py:438
Async XLA Ops:
  1.3 1.0 %copy-start.1 = (f32[32,32,128]{2,1,0:T(8,128)S(1)}, f32[32,32,128]{2,1,0:T(8,128)}, u32[]{:S(2)}) copy-start(f32[32,32,128]{2,1,0:T(8,128)} %param.7) | copy-start | bytes 1572868
  2.3 2.4 %copy-start = (f32[8,32,1024]{2,1,0:T(8,128)S(1)}, f32[8,32,1024]{2,1,0:T(8,128)}, u32[]{:S(2)}) copy-start(f32[8,32,1024]{2,1,0:T(8,128)} %t_ref.1) | copy-start | bytes 3145732
  2.3 2.4 %copy-start.2 = (bf16[8,256,256]{2,1,0:T(8,128)(2,1)S(1)}, bf16[8,256,256]{2,1,0:T(8,128)(2,1)}, u32[]{:S(2)}) copy-start(bf16[8,256,256]{2,1,0:T(8,128)(2,1)} %constant.4.clone.refs_2_.refs_3_) | copy-start | bytes 3145732
  2.3 2.4 %copy-start.3 = (f32[8,32,128]{2,1,0:T(8,128)S(1)}, f32[8,32,128]{2,1,0:T(8,128)}, u32[]{:S(2)}) copy-start(f32[8,32,128]{2,1,0:T(8,128)} %constant.5.clone.refs_3_.refs_4_) | copy-start | bytes 393220
  3.2 5.7 %collective-permute-start = (f32[8,128,128]{2,1,0:T(8,128)S(1)}, f32[8,128,128]{2,1,0:T(8,128)S(1)}, u32[]{:S(2)}, u32[]{:S(2)}) collective-permute-start(f32[8,128,128]{2,1,0:T(8,128)S(1)} %get-tuple-element.9.refs_1_), channel_id=1, source_target_pairs={{0,1},{1,0},{2,3},{3,2},{4,5},{5,4},{6,7},{7,6},{8,9},{9,8},{10,11... | collective-permute-start | bytes 1572872 | tf_op jit(solution)/shard_map/ppermute | solution.py:454
